TPU v7x, 256 devices: a whole 4x4x8 slice. The times are simulated.
256 devices in a mesh: row: 8 (over z_hi, x), col: 32 (over y, z_lo, core).
Axes of the slice: x: 4, y: 4, z: 8 (z_hi: 2, z_lo: 4; z = z_hi * 4 + z_lo), core: 2. Of those that a mesh axis runs over, the one named last changes fastest.
Arguments:
- inv_anc: float32 [8, 32, 48, 12288], P(None, 'col', None, 'row'), may hold values from -6 to 6
- factor_cols: float32 [4, 12288, 256], P(None, ('row', 'col')), may hold values from -0.0546875 to 0.0546875
- couple: float32 [6, 256, 256], replicated, may hold values from -0.1875 to 0.1875
- diag_inv: float32 [4, 256, 256], replicated, may hold values from -6 to 6, as said below
- pattern: int32 [4, 48], replicated, may hold values 0 or 1
- parent: int32 [4], replicated, may hold values from 0 to 4, as said below
Outputs:
- inv_cols: float32 [4, 12288, 256], P(None, ('row', 'col'))
- win_cols: float32 [6, 256, 256], replicated
- win_diag: float32 [4, 256, 256], replicated
Inputs may be any that keep to these rules, and one draw needn't show every extreme that they name: parent[0] is 4, meaning a parent in the ancestor set; for j of 1 or more parent[j] is an earlier supernode or 4. Each diag_inv[j] is symmetric.
All inputs are finite; a program needn't handle non-finite values.
Results may differ from a plain program's by a relative error of at most 0.0001.
Values sent between devices are 32-bit elements; how exact they have to be, the bound alone decides.
No kernel may reach another device: no remote copies, remote signals or barrier semaphores. Data moves between devices by JAX's collectives and lax.ppermute only.
A program may use at most 64 MiB of HBM per device.

v0:
```python
import functools

import jax
import jax.numpy as jnp
from jax import lax
from jax.experimental import pallas as pl
from jax.experimental.pallas import tpu as pltpu
from jax.sharding import PartitionSpec as P


W = 256
NSUP = 4
RW = 48
HALF = W // 2
SIZES = {"zh": 2, "x": 4, "y": 4, "zl": 4, "c": 2}
BOTH = ("row", "col")
CHUNKS = ((0, 1, 2, 3),)
F32, BF16 = jnp.float32, jnp.bfloat16
PAIRS = [(m, j) for j in range(NSUP) for m in range(j)]
ALL_BLOCKS = PAIRS + [(j, j) for j in range(NSUP)]
VMEM = pl.BlockSpec(memory_space=pltpu.VMEM)
SMEM = pl.BlockSpec(memory_space=pltpu.SMEM)


def place():
    row, col = lax.axis_index("row"), lax.axis_index("col")
    return {"zh": row >> 2, "x": row & 3, "y": col >> 3, "zl": (col >> 1) & 3, "c": col & 1}


def moved(value, axis, step):
    return sent(value, axis, lambda a: (a + step) % SIZES[axis])


def sent(value, axis, rule):
    names = list(SIZES)
    perm = []
    for device in range(256):
        rest, at = device, {}
        for name in reversed(names):
            at[name] = rest % SIZES[name]
            rest //= SIZES[name]
        at[axis] = rule(at[axis])
        target = 0
        for name in names:
            target = target * SIZES[name] + at[name]
        perm.append((device, target))
    return lax.ppermute(value, BOTH, perm)


def tie(*values):
    return lax.optimization_barrier(values)


def halves(value):
    top = value.astype(BF16)
    return top, (value - top.astype(F32)).astype(BF16)


def mul(left, right, over=(1, 0)):
    dims = (((over[0],), (over[1],)), ((), ()))
    dot = lambda u, v: lax.dot_general(u, v, dims, preferred_element_type=F32)
    return dot(left[0], right[0]) + (dot(left[1], right[0]) + dot(left[0], right[1]))


def couplings(couple, parent):
    linked = {}
    blocks = {}
    for j in range(NSUP):
        for m in range(j):
            now = parent[j] == m
            for p in range(m + 1, j):
                now = now | ((parent[j] == p) & linked[p, m])
            linked[j, m] = now
            blocks[j, m] = couple[j * (j - 1) // 2 + m] * jnp.where(now, 1.0, 0.0).astype(F32)
    return blocks


def pre_kernel(parent, pattern, factor, couple, out):
    first = (lax.axis_index("row") * 32 + lax.axis_index("col")) * RW
    block = first >> 8
    after = jnp.minimum(block + 1, pattern.shape[1] - 1)
    edge = (block + 1) * W - first
    low = lax.broadcasted_iota(jnp.int32, (RW, W), 0) < edge
    blocks = couplings(couple, parent)
    values = []
    for j in range(NSUP):
        here, there = pattern[j, block].astype(F32), pattern[j, after].astype(F32)
        values.append(factor[j] * jnp.where(low, here, there))
    for m in range(NSUP):
        out[:, m * W : (m + 1) * W] = values[m]
        left = halves(values[m])
        for j in range(m + 1, NSUP):
            values[j] = values[j] - mul(left, halves(blocks[j, m]))


def base_kernel(order, parent, couple, diag_inv, out, *held):
    chigh, clow, ihigh, ilow, shigh, slow = held
    at = lambda q, j: order.index((q, j))

    def keep(high, low, i, value):
        high[i], low[i] = halves(value)

    def kept(high, low, i):
        return high[i], low[i]

    for (j, m), value in couplings(couple, parent).items():
        keep(chigh, clow, at(m, j), value)
        keep(ihigh, ilow, at(m, j), -value)
    for gap in range(2, NSUP):
        for m in range(NSUP - gap):
            j = m + gap
            value = -(chigh[at(m, j)].astype(F32) + clow[at(m, j)].astype(F32))
            for q in range(m + 1, j):
                value = value - mul(kept(ihigh, ilow, at(m, q)), kept(chigh, clow, at(q, j)))
            keep(ihigh, ilow, at(m, j), value)
    for q in range(NSUP):
        out[at(q, q) * W : (at(q, q) + 1) * W, :] = diag_inv[q]
        keep(shigh, slow, at(q, q), diag_inv[q])
        for j in range(q + 1, NSUP):
            i = at(q, j)
            value = mul(kept(shigh, slow, at(q, q)), kept(ihigh, ilow, i))
            out[i * W : (i + 1) * W, :] = value
            keep(shigh, slow, i, value)
    for i, (m, j) in enumerate(order):
        rows = slice(i * W, (i + 1) * W)
        for q in range(m):
            out[rows, :] = out[rows, :] + mul(kept(ihigh, ilow, at(q, m)), kept(shigh, slow, at(q, j)), (0, 0))


def put(piece, top, bot, row_of):
    def step(i, carry):
        r = lax.div(i, 3)
        src = pl.multiple_of(i * 16, 16)
        dst = pl.multiple_of(row_of(r) + (i - 3 * r) * 16, 16)
        hi, lo = halves(piece[pl.ds(src, 16), :])
        top[pl.ds(dst, 16), :] = hi
        bot[pl.ds(dst, 16), :] = lo
        return carry

    lax.fori_loop(0, piece.shape[0] // 16, step, 0)


def put_columns(local, top, bot, blocks):
    span = local.shape[1] // 4
    for i, k in enumerate(blocks):
        src = pl.multiple_of(((place()["y"] - k) & 3) * span, 128)

        def step(t, carry, src=src, i=i):
            rows = pl.ds(pl.multiple_of(t * 16, 16), 16)
            hi, lo = halves(local[rows, pl.ds(src, span)])
            top[rows, i * span : (i + 1) * span] = hi
            bot[rows, i * span : (i + 1) * span] = lo
            return carry

        lax.fori_loop(0, local.shape[0] // 16, step, 0)


def early_kernel(local, *refs):
    pieces, out = refs[:6], refs[6]
    top, bot, ltop, lbot = refs[7:]
    at = place()
    put_columns(local, ltop, lbot, (0, 1, 3))
    for i, piece in enumerate(pieces):
        core = at["c"] ^ (i // 3)
        start = (i % 3) * 8
        put(piece, top, bot, lambda r: (start + ((at["zl"] - r) & 3) * 2 + core) * RW)
    out[...] = mul((ltop[...], lbot[...]), (top[...], bot[...]))


def main_kernel(chunk, order, skip, *refs):
    local, base, early = refs[:3]
    pieces, quads = refs[3:7], refs[7:11]
    outs = refs[11:15]
    kept, given = refs[15], refs[16]
    top, bot, ltop, lbot, rtop, rbot, result, ptop, pbot = refs[17:]
    at = place()
    put_columns(local, ltop, lbot, (2,))
    for i, piece in enumerate(pieces):
        core = at["c"] ^ (i // 2)
        start = 2 * (i % 2)
        put(piece, top, bot, lambda r: (((at["zl"] - r - start) & 3) * 2 + core) * RW)
    for k, piece in enumerate(quads):
        xa = (at["x"] - k) & 3
        for r in range(2):
            put(piece.at[r], rtop, rbot, lambda _: ((at["zh"] ^ r) * 4 + xa) * RW)
    result[...] = early[...] + mul((ltop[...], lbot[...]), (top[...], bot[...]))
    for k, out in enumerate(outs):
        xa = (at["x"] + k) & 3

        def step(t, carry, out=out, xa=xa):
            for r in range(2):
                src = pl.multiple_of((r * 4 + xa) * RW + t * 8, 8)
                out[r, pl.ds(pl.multiple_of(t * 8, 8), 8), :] = result[pl.ds(src, 8), :]
            return carry

        lax.fori_loop(0, RW // 8, step, 0)
    lead = (lax.axis_index("row") == 0) & (lax.axis_index("col") == 0)

    def part(t, carry):
        rows = pl.ds(pl.multiple_of(t * 16, 16), 16)
        hi, lo = halves(result[rows, :])
        ptop[rows, :] = hi
        pbot[rows, :] = lo
        return carry

    lax.fori_loop(0, result.shape[0] // 16, part, 0)
    cols = lambda s: (ptop[:, s * W : (s + 1) * W], pbot[:, s * W : (s + 1) * W])
    beside = lambda s: (rtop[:, s * W : (s + 1) * W], rbot[:, s * W : (s + 1) * W])
    even = at["c"] == 0
    for i, (m, j) in enumerate(order):
        if j in chunk:
            block = mul(beside(m), cols(chunk.index(j)), (0, 0))
        else:
            block = mul(cols(chunk.index(m)), beside(j), (0, 0))
        rows = slice(i * W, (i + 1) * W)
        block = block + jnp.where(lead, base[(skip + i) * W : (skip + i + 1) * W, :], 0.0)
        first, second = block[:, :HALF], block[:, HALF:]
        kept[rows, :] = jnp.where(even, first, second)
        given[rows, :] = jnp.where(even, second, first)


def join_kernel(axis, *refs):
    pieces, out = refs[:-1], refs[-1]
    at = place()[axis]
    rows = pieces[0].shape[0]
    for k, piece in enumerate(pieces):
        dst = pl.multiple_of(((at - k) & (SIZES[axis] - 1)) * rows, 8)
        out[pl.ds(dst, rows), :] = piece[...]


def add_split_kernel(axis, count, *refs):
    values, outs = refs[:count], refs[count:-1]
    whole = refs[-1]
    at = place()[axis]
    total = values[0][...]
    for value in values[1:]:
        total = total + value[...]
    whole[...] = total
    rows = outs[0].shape[0]
    for k, out in enumerate(outs):
        src = pl.multiple_of(((at + k) & (SIZES[axis] - 1)) * rows, 8)
        out[...] = whole[pl.ds(src, rows), :]


def final_kernel(orders, *refs):
    count = 8 * len(orders)
    pieces, pair_out, diag_out, wholes = refs[:count], refs[count], refs[count + 1], refs[count + 2 :]
    at = place()
    for i, order in enumerate(orders):
        whole = wholes[i]
        for par in range(2):
            for k in range(4):
                piece = pieces[i * 8 + par * 4 + k]
                rows = piece.shape[0]
                dst = pl.multiple_of(((at["y"] - k) & 3) * rows, 8)
                lane = pl.multiple_of((at["c"] ^ par) * HALF, HALF)
                whole[pl.ds(dst, rows), pl.ds(lane, HALF)] = piece[...]
        for b, (m, j) in enumerate(order):
            rows = slice(b * W, (b + 1) * W)
            if m == j:
                diag_out[j] = whole[rows, :]
            else:
                pair_out[PAIRS.index((m, j))] = whole[rows, :]


def kernel(body, args, out_shapes, scratch=(), smem=0, flops=0):
    single = not isinstance(out_shapes, list)
    return pl.pallas_call(
        body,
        out_shape=jax.ShapeDtypeStruct(out_shapes, F32)
        if single
        else [jax.ShapeDtypeStruct(s, F32) for s in out_shapes],
        in_specs=[SMEM] * smem + [VMEM] * (len(args) - smem),
        out_specs=VMEM if single else [VMEM] * len(out_shapes),
        scratch_shapes=[pltpu.VMEM(s, t) for s, t in scratch],
        compiler_params=pltpu.CompilerParams(vmem_limit_bytes=56 << 20),
        cost_estimate=pl.CostEstimate(
            flops=flops, transcendentals=0, bytes_accessed=sum(4 * a.size for a in args)
        ),
    )(*args)


def split_sum(values, axis):
    rows, width = values[0].shape
    n = SIZES[axis]
    return kernel(
        functools.partial(add_split_kernel, axis, len(values)),
        list(values),
        [(rows // n, width)] * n,
        [((rows, width), F32)],
    )


def scattered(pieces, axis):
    return [pieces[0]] + [moved(pieces[k], axis, k) for k in range(1, len(pieces))]


def gathered(value, axis):
    return [value] + [moved(value, axis, k) for k in range(1, SIZES[axis])]


def total_of(values):
    total = values[0]
    for value in values[1:]:
        total = total + value
    return total


def shards(inv_anc, factor_cols, couple, diag_inv, pattern, parent):
    at = place()
    local = inv_anc.reshape(-1, inv_anc.shape[3])
    height = local.shape[0]

    orders = []
    done = set()
    for chunk in CHUNKS:
        order = [b for b in ALL_BLOCKS if (b[0] in chunk or b[1] in chunk) and b not in done]
        done |= set(order)
        orders.append(order)

    own = kernel(
        pre_kernel, [parent, pattern, factor_cols, couple], (RW, NSUP * W), smem=2, flops=1 << 20
    )

    near = jnp.concatenate(gathered(own, "zl"), axis=0)
    near, later = tie(near, own)
    left, right = moved(near, "y", 1), moved(near, "y", 3)

    pair = jnp.stack([later, moved(later, "zh", 1)])
    pair, couple_later = tie(pair, couple)
    quads = gathered(pair, "x")

    (chunk,), (order,) = CHUNKS, orders
    base = kernel(
        functools.partial(base_kernel, order),
        [parent, couple_later, diag_inv],
        (len(order) * W, W),
        [((len(order), W, W), BF16)] * 6,
        smem=1,
        flops=1 << 31,
    )
    left, right, base = tie(left, right, base)
    half = near.shape[0] // 2
    far_a, far_b = moved(left[:half], "y", 1), moved(right[half:], "y", 3)
    mine = [near, left, right]
    pieces = mine + [moved(v, "c", 1) for v in mine]
    width = len(chunk) * W
    tall = len(order) * W
    span = local.shape[1] // 4
    early = kernel(
        early_kernel,
        [local] + pieces,
        (height, width),
        [((3 * span, width), BF16)] * 2 + [((height, 3 * span), BF16)] * 2,
        flops=1 << 32,
    )
    far_a, far_b, early = tie(far_a, far_b, early)
    columns = []
    finals = []
    skip = 0
    *parts, kept, given = kernel(
        functools.partial(main_kernel, chunk, order, skip),
        [local, base, early, far_a, far_b, moved(far_a, "c", 1), moved(far_b, "c", 1)] + quads,
        [(2, RW, width)] * 4 + [(tall, HALF)] * 2,
        [((span, width), BF16)] * 2
        + [((height, span), BF16)] * 2
        + [((height, NSUP * W), BF16)] * 2
        + [((height, width), F32)]
        + [((height, width), BF16)] * 2,
        flops=1 << 32,
    )
    got = moved(given, "c", 1)
    across = scattered(split_sum([kept, got], "y"), "y")
    cols = scattered(parts, "x")
    *across, first = tie(*across, total_of(cols))
    total = total_of(scattered(split_sum(across, "x"), "x"))
    total = total + sent(total, "zl", lambda a: a ^ 1)
    total = total + sent(total, "zl", lambda a: a ^ 2)
    total = total + moved(total, "zh", 1)
    total, first = tie(total, first)
    keep = lax.dynamic_index_in_dim(first, at["zh"], 0, keepdims=False)
    give = lax.dynamic_index_in_dim(first, 1 - at["zh"], 0, keepdims=False)
    columns.append(-(keep + moved(give, "zh", 1)))
    parts = gathered(total, "x")
    total = kernel(functools.partial(join_kernel, "x"), parts, (4 * parts[0].shape[0], HALF))
    lanes = gathered(total, "y")
    finals += lanes + [moved(v, "c", 1) for v in lanes]

    pair_blocks, diagonal = kernel(
        functools.partial(final_kernel, orders),
        finals,
        [(len(PAIRS), W, W), (NSUP, W, W)],
        [((len(order) * W, W), F32) for order in orders],
    )
    wide = jnp.concatenate(columns, axis=1)
    columns = jnp.stack([wide[:, j * W : (j + 1) * W] for j in range(NSUP)])
    return (columns, pair_blocks, diagonal)


def solution(mesh):
    in_specs = (P(None, "col", None, "row"), P(None, BOTH, None), P(), P(), P(), P())
    out_specs = (P(None, BOTH, None), P(), P())

    return jax.shard_map(shards, mesh=mesh, in_specs=in_specs, out_specs=out_specs, check_vma=False)
```

profile of v0, /device:TPU:1, one launch (start us, length us, event | category | flops | bytes accessed | tf_op | source)
XLA Modules:
  0.0 180.2 jit_solution(14767244250355208511)
XLA Ops:
  0.6 2.9 %shard_map.85 = f32[48,1024]{1,0:T(8,128)} custom-call(s32[4]{0:T(128)} %parent.3, s32[4,48]{1,0:T(4,128)} %pattern.1, f32[4,48,256]{2,1,0:T(8,128)} %factor.1, f32[6,256,256]{2,1,0:T(8,128)} %couple.2), custom_call_target="tpu_custom_call" | custom-call | flops 1048576 | bytes 1770256 | tf_op jit(solution)/shard_map/pallas_call | solution.py:268
  5.9 3.0 %collective-permute-start.1 = (f32[48,1024]{1,0:T(8,128)}, f32[48,1024]{1,0:T(8,128)S(1)}, u32[]{:S(2)}, u32[]{:S(2)}) collective-permute-start(f32[48,1024]{1,0:T(8,128)} %shard_map.85), channel_id=1, source_target_pairs={{0,4},{1,5},{2,6},{3,7},{4,0},{5,1},{6,2},{7,3},{8,12},{9,13},{10,... | collective-permute-start | bytes 589832 | tf_op jit(solution)/shard_map/ppermute | solution.py:47
  9.7 3.1 %collective-permute-done = f32[48,1024]{1,0:T(8,128)S(1)} collective-permute-done((f32[48,1024]{1,0:T(8,128)}, f32[48,1024]{1,0:T(8,128)S(1)}, u32[]{:S(2)}, u32[]{:S(2)}) %collective-permute-start) | collective-permute-done | bytes 196640 | tf_op jit(solution)/shard_map/ppermute | solution.py:47
  12.7 10.0 %collective-permute-done.1 = f32[48,1024]{1,0:T(8,128)S(1)} collective-permute-done((f32[48,1024]{1,0:T(8,128)}, f32[48,1024]{1,0:T(8,128)S(1)}, u32[]{:S(2)}, u32[]{:S(2)}) %collective-permute-start.1) | collective-permute-done | bytes 196640 | tf_op jit(solution)/shard_map/ppermute | solution.py:47
  26.6 5.4 %collective-permute-start.5 = (f32[48,1024]{1,0:T(8,128)S(1)}, f32[48,1024]{1,0:T(8,128)S(1)}, u32[]{:S(2)}, u32[]{:S(2)}) collective-permute-start(f32[48,1024]{1,0:T(8,128)S(1)} %copy-done), channel_id=1, source_target_pairs={{0,128},{1,129},{2,130},{3,131},{4,132},{5,133},{6,134},{7,135},{8... | collective-permute-start | bytes 589832 | tf_op jit(solution)/shard_map/ppermute | solution.py:47
  36.1 5.9 %shard_map.86.refs_1_ = f32[2560,256]{1,0:T(8,128)} custom-call(s32[4]{0:T(128)} %parent.3, f32[6,256,256]{2,1,0:T(8,128)} %couple.2, f32[4,256,256]{2,1,0:T(8,128)} %diag_inv.1), custom_call_target="tpu_custom_call" | custom-call | flops 2147483648 | bytes 2621456 | tf_op jit(solution)/shard_map/pallas_call | solution.py:268
  43.7 3.8 %collective-permute-start.10 = (f32[192,1024]{1,0:T(8,128)S(1)}, f32[192,1024]{1,0:T(8,128)S(1)}, u32[]{:S(2)}, u32[]{:S(2)}) collective-permute-start(f32[192,1024]{1,0:T(8,128)S(1)} %collective-permute-done.4.refs_2_), channel_id=1, source_target_pairs={{0,1},{1,0},{2,3},{3,2},{4,5},{5,4},{6,7},{7,6},{8,9},{9,8},{10,11... | collective-permute-start | bytes 2359304 | tf_op jit(solution)/shard_map/ppermute | solution.py:47
  52.6 2.7 %collective-permute-start.7 = (f32[96,1024]{1,0:T(8,128)S(1)}, f32[96,1024]{1,0:T(8,128)S(1)}, u32[]{:S(2)}, u32[]{:S(2)}) collective-permute-start(f32[96,1024]{1,0:T(8,128)S(1)} %slice.19), channel_id=1, source_target_pairs={{0,24},{1,25},{2,26},{3,27},{4,28},{5,29},{6,30},{7,31},{8,0},{9,1... | collective-permute-start | bytes 1179656 | tf_op jit(solution)/shard_map/ppermute | solution.py:47
  55.3 9.1 %shard_map.87.refs_2_ = f32[384,1024]{1,0:T(8,128)} custom-call(f32[384,1536]{1,0:T(8,128)} %bitcast.19, f32[192,1024]{1,0:T(8,128)} %copy-done.2, f32[192,1024]{1,0:T(8,128)} %copy-done.16, f32[192,1024]{1,0:T(8,128)} %copy-done.17, f32[192,1024]{1,0:T(8,128)} %copy-done.21, f32[192,1024]{1,0:T(8,128)} %copy-done.23, f32[192,1024]{1,0:T(8,128)} %copy-done.22), custom_call_target="tpu_custom_call" | custom-call | flops 4294967296 | bytes 7077888 | tf_op jit(solution)/shard_map/pallas_call | solution.py:268
  70.4 10.3 %shard_map.88 = (f32[2,48,1024]{2,1,0:T(8,128)}, f32[2,48,1024]{2,1,0:T(8,128)}, f32[2,48,1024]{2,1,0:T(8,128)}, f32[2,48,1024]{2,1,0:T(8,128)}, f32[2560,128]{1,0:T(8,128)}, /*index=5*/f32[2560,128]{1,0:T(8,128)}) custom-call(f32[384,1536]{1,0:T(8,128)} %bitcast.20, f32[2560,256]{1,0:T(8,128)} %shard_map.86.refs_1_, f32[384,1024]{1,0:T(8,128)} %shard_map.87.refs_2_, ...), custom_call_target="tpu_custom_call" | custom-call | flops 4294967296 | bytes 9699328 | tf_op jit(solution)/shard_map/pallas_call | solution.py:268
  87.4 2.9 %shard_map.89 = (f32[640,128]{1,0:T(8,128)}, f32[640,128]{1,0:T(8,128)}, f32[640,128]{1,0:T(8,128)}, f32[640,128]{1,0:T(8,128)}) custom-call(f32[2560,128]{1,0:T(8,128)} %get-tuple-element.46.refs_0_, f32[2560,128]{1,0:T(8,128)} %copy-done.1), custom_call_target="tpu_custom_call" | custom-call | bytes 2621440 | tf_op jit(solution)/shard_map/pallas_call | solution.py:268
  90.3 2.6 %collective-permute-start.18 = (f32[640,128]{1,0:T(8,128)}, f32[640,128]{1,0:T(8,128)S(1)}, u32[]{:S(2)}, u32[]{:S(2)}) collective-permute-start(f32[640,128]{1,0:T(8,128)} %get-tuple-element.50), channel_id=1, source_target_pairs={{0,16},{1,17},{2,18},{3,19},{4,20},{5,21},{6,22},{7,23},{8,24},{9,... | collective-permute-start | bytes 983048 | tf_op jit(solution)/shard_map/ppermute | solution.py:47
  95.3 7.4 %collective-permute-done.21 = f32[2,48,1024]{2,1,0:T(8,128)S(1)} collective-permute-done((f32[2,48,1024]{2,1,0:T(8,128)}, f32[2,48,1024]{2,1,0:T(8,128)S(1)}, u32[]{:S(2)}, u32[]{:S(2)}) %collective-permute-start.21) | collective-permute-done | bytes 393248 | tf_op jit(solution)/shard_map/ppermute | solution.py:47
  102.9 4.1 %collective-permute-done.18.refs_2_ = f32[640,128]{1,0:T(8,128)S(1)} collective-permute-done((f32[640,128]{1,0:T(8,128)}, f32[640,128]{1,0:T(8,128)S(1)}, u32[]{:S(2)}, u32[]{:S(2)}) %collective-permute-start.18) | collective-permute-done | bytes 327712 | tf_op jit(solution)/shard_map/ppermute | solution.py:47
  118.2 4.8 %collective-permute-start.26 = (f32[160,128]{1,0:T(8,128)S(1)}, f32[160,128]{1,0:T(8,128)S(1)}, u32[]{:S(2)}, u32[]{:S(2)}) collective-permute-start(f32[160,128]{1,0:T(8,128)S(1)} %add_add_fusion.1), channel_id=1, source_target_pairs={{0,2},{1,3},{2,0},{3,1},{4,6},{5,7},{6,4},{7,5},{8,10},{9,11},{10,... | collective-permute-start | bytes 245768 | tf_op jit(solution)/shard_map/ppermute | solution.py:47
  125.0 4.2 %collective-permute-done.27 = f32[160,128]{1,0:T(8,128)S(1)} collective-permute-done((f32[160,128]{1,0:T(8,128)S(1)}, f32[160,128]{1,0:T(8,128)S(1)}, u32[]{:S(2)}, u32[]{:S(2)}) %collective-permute-start.27) | collective-permute-done | bytes 81952 | tf_op jit(solution)/shard_map/ppermute | solution.py:47
  129.2 5.2 %collective-permute-start.28 = (f32[160,128]{1,0:T(8,128)S(1)}, f32[160,128]{1,0:T(8,128)S(1)}, u32[]{:S(2)}, u32[]{:S(2)}) collective-permute-start(f32[160,128]{1,0:T(8,128)S(1)} %add.45), channel_id=1, source_target_pairs={{0,128},{1,129},{2,130},{3,131},{4,132},{5,133},{6,134},{7,135},{8... | collective-permute-start | bytes 245768 | tf_op jit(solution)/shard_map/ppermute | solution.py:47
  136.8 5.0 %collective-permute-start.29 = (f32[48,1024]{1,0:T(8,128)S(1)}, f32[48,1024]{1,0:T(8,128)S(1)}, u32[]{:S(2)}, u32[]{:S(2)}) collective-permute-start(f32[48,1024]{1,0:T(8,128)S(1)} %dynamic-slice_bitcast_fusion), channel_id=1, source_target_pairs={{0,128},{1,129},{2,130},{3,131},{4,132},{5,133},{6,134},{7,135},{8... | collective-permute-start | bytes 589832 | tf_op jit(solution)/shard_map/ppermute | solution.py:47
  142.0 2.9 %collective-permute-start.31 = (f32[160,128]{1,0:T(8,128)S(1)}, f32[160,128]{1,0:T(8,128)S(1)}, u32[]{:S(2)}, u32[]{:S(2)}) collective-permute-start(f32[160,128]{1,0:T(8,128)S(1)} %add.46.refs_0_), channel_id=1, source_target_pairs={{0,64},{1,65},{2,66},{3,67},{4,68},{5,69},{6,70},{7,71},{8,72},{9,... | collective-permute-start | bytes 245768 | tf_op jit(solution)/shard_map/ppermute | solution.py:47
  150.6 3.8 %collective-permute-start.33 = (f32[640,128]{1,0:T(8,128)}, f32[640,128]{1,0:T(8,128)S(1)}, u32[]{:S(2)}, u32[]{:S(2)}) collective-permute-start(f32[640,128]{1,0:T(8,128)} %shard_map.91.refs_0_), channel_id=1, source_target_pairs={{0,8},{1,9},{2,10},{3,11},{4,12},{5,13},{6,14},{7,15},{8,16},{9,17... | collective-permute-start | bytes 983048 | tf_op jit(solution)/shard_map/ppermute | solution.py:47
  154.4 2.6 %collective-permute-start.34 = (f32[640,128]{1,0:T(8,128)}, f32[640,128]{1,0:T(8,128)S(1)}, u32[]{:S(2)}, u32[]{:S(2)}) collective-permute-start(f32[640,128]{1,0:T(8,128)} %shard_map.91.refs_0_), channel_id=1, source_target_pairs={{0,16},{1,17},{2,18},{3,19},{4,20},{5,21},{6,22},{7,23},{8,24},{9,... | collective-permute-start | bytes 983048 | tf_op jit(solution)/shard_map/ppermute | solution.py:47
  157.0 8.7 %collective-permute-start.36 = (f32[640,128]{1,0:T(8,128)}, f32[640,128]{1,0:T(8,128)S(1)}, u32[]{:S(2)}, u32[]{:S(2)}) collective-permute-start(f32[640,128]{1,0:T(8,128)} %shard_map.91.refs_0_), channel_id=1, source_target_pairs={{0,1},{1,0},{2,3},{3,2},{4,5},{5,4},{6,7},{7,6},{8,9},{9,8},{10,11... | collective-permute-start | bytes 983048 | tf_op jit(solution)/shard_map/ppermute | solution.py:47
  165.8 7.8 %collective-permute-start.37 = (f32[640,128]{1,0:T(8,128)S(1)}, f32[640,128]{1,0:T(8,128)S(1)}, u32[]{:S(2)}, u32[]{:S(2)}) collective-permute-start(f32[640,128]{1,0:T(8,128)S(1)} %collective-permute-done.33.refs_1_), channel_id=1, source_target_pairs={{0,1},{1,0},{2,3},{3,2},{4,5},{5,4},{6,7},{7,6},{8,9},{9,8},{10,11... | collective-permute-start | bytes 983048 | tf_op jit(solution)/shard_map/ppermute | solution.py:47
  176.7 3.5 %shard_map.92 = (f32[6,256,256]{2,1,0:T(8,128)}, f32[4,256,256]{2,1,0:T(8,128)}) custom-call(f32[640,128]{1,0:T(8,128)} %shard_map.91.refs_0_, f32[640,128]{1,0:T(8,128)} %copy-done.5, f32[640,128]{1,0:T(8,128)} %copy-done.6, f32[640,128]{1,0:T(8,128)} %copy-done.7, f32[640,128]{1,0:T(8,128)} %copy-done.8, f32[640,128]{1,0:T(8,128)} %copy-done.9, ...), custom_call_target="tpu_custom_call" | custom-call | bytes 2621440 | tf_op jit(solution)/shard_map/pallas_call | solution.py:268
  (139 shorter events, 57.7 us)
Async XLA Ops:
  3.5 9.3 %collective-permute-start = (f32[48,1024]{1,0:T(8,128)}, f32[48,1024]{1,0:T(8,128)S(1)}, u32[]{:S(2)}, u32[]{:S(2)}) collective-permute-start(f32[48,1024]{1,0:T(8,128)} %shard_map.85), channel_id=1, source_target_pairs={{0,2},{1,3},{2,4},{3,5},{4,6},{5,7},{6,0},{7,1},{8,10},{9,11},{10,... | collective-permute-start | bytes 589832 | tf_op jit(solution)/shard_map/ppermute | solution.py:47
  5.9 16.8 %collective-permute-start.1 = (f32[48,1024]{1,0:T(8,128)}, f32[48,1024]{1,0:T(8,128)S(1)}, u32[]{:S(2)}, u32[]{:S(2)}) collective-permute-start(f32[48,1024]{1,0:T(8,128)} %shard_map.85), channel_id=1, source_target_pairs={{0,4},{1,5},{2,6},{3,7},{4,0},{5,1},{6,2},{7,3},{8,12},{9,13},{10,... | collective-permute-start | bytes 589832 | tf_op jit(solution)/shard_map/ppermute | solution.py:47
  8.9 13.8 %collective-permute-start.2 = (f32[48,1024]{1,0:T(8,128)}, f32[48,1024]{1,0:T(8,128)S(1)}, u32[]{:S(2)}, u32[]{:S(2)}) collective-permute-start(f32[48,1024]{1,0:T(8,128)} %shard_map.85), channel_id=1, source_target_pairs={{0,6},{1,7},{2,0},{3,1},{4,2},{5,3},{6,4},{7,5},{8,14},{9,15},{10,... | collective-permute-start | bytes 589832 | tf_op jit(solution)/shard_map/ppermute | solution.py:47
  23.7 20.0 %collective-permute-start.3 = (f32[192,1024]{1,0:T(8,128)S(1)}, f32[192,1024]{1,0:T(8,128)S(1)}, u32[]{:S(2)}, u32[]{:S(2)}) collective-permute-start(f32[192,1024]{1,0:T(8,128)S(1)} %pad_maximum_fusion.refs_0_), channel_id=1, source_target_pairs={{0,8},{1,9},{2,10},{3,11},{4,12},{5,13},{6,14},{7,15},{8,16},{9,17... | collective-permute-start | bytes 2359304 | tf_op jit(solution)/shard_map/ppermute | solution.py:47
  25.1 18.6 %collective-permute-start.4 = (f32[192,1024]{1,0:T(8,128)S(1)}, f32[192,1024]{1,0:T(8,128)S(1)}, u32[]{:S(2)}, u32[]{:S(2)}) collective-permute-start(f32[192,1024]{1,0:T(8,128)S(1)} %pad_maximum_fusion.refs_0_), channel_id=1, source_target_pairs={{0,24},{1,25},{2,26},{3,27},{4,28},{5,29},{6,30},{7,31},{8,0},{9,1... | collective-permute-start | bytes 2359304 | tf_op jit(solution)/shard_map/ppermute | solution.py:47
  26.6 9.4 %collective-permute-start.5 = (f32[48,1024]{1,0:T(8,128)S(1)}, f32[48,1024]{1,0:T(8,128)S(1)}, u32[]{:S(2)}, u32[]{:S(2)}) collective-permute-start(f32[48,1024]{1,0:T(8,128)S(1)} %copy-done), channel_id=1, source_target_pairs={{0,128},{1,129},{2,130},{3,131},{4,132},{5,133},{6,134},{7,135},{8... | collective-permute-start | bytes 589832 | tf_op jit(solution)/shard_map/ppermute | solution.py:47
  32.1 19.2 %collective-permute-start.8 = (f32[192,1024]{1,0:T(8,128)S(1)}, f32[192,1024]{1,0:T(8,128)S(1)}, u32[]{:S(2)}, u32[]{:S(2)}) collective-permute-start(f32[192,1024]{1,0:T(8,128)S(1)} %pad_maximum_fusion.refs_0_), channel_id=1, source_target_pairs={{0,1},{1,0},{2,3},{3,2},{4,5},{5,4},{6,7},{7,6},{8,9},{9,8},{10,11... | collective-permute-start | bytes 2359304 | tf_op jit(solution)/shard_map/ppermute | solution.py:47
  47.6 18.9 %collective-permute-start.13 = (f32[2,48,1024]{2,1,0:T(8,128)S(1)}, f32[2,48,1024]{2,1,0:T(8,128)S(1)}, u32[]{:S(2)}, u32[]{:S(2)}) collective-permute-start(f32[2,48,1024]{2,1,0:T(8,128)S(1)} %pad_maximum_fusion.1.refs_7_), channel_id=1, source_target_pairs={{0,32},{1,33},{2,34},{3,35},{4,36},{5,37},{6,38},{7,39},{8,40},{9,... | collective-permute-start | bytes 1179656 | tf_op jit(solution)/shard_map/ppermute | solution.py:47
  48.8 19.7 %collective-permute-start.14 = (f32[2,48,1024]{2,1,0:T(8,128)S(1)}, f32[2,48,1024]{2,1,0:T(8,128)S(1)}, u32[]{:S(2)}, u32[]{:S(2)}) collective-permute-start(f32[2,48,1024]{2,1,0:T(8,128)S(1)} %pad_maximum_fusion.1.refs_7_), channel_id=1, source_target_pairs={{0,64},{1,65},{2,66},{3,67},{4,68},{5,69},{6,70},{7,71},{8,72},{9,... | collective-permute-start | bytes 1179656 | tf_op jit(solution)/shard_map/ppermute | solution.py:47
  51.4 17.1 %collective-permute-start.15 = (f32[2,48,1024]{2,1,0:T(8,128)S(1)}, f32[2,48,1024]{2,1,0:T(8,128)S(1)}, u32[]{:S(2)}, u32[]{:S(2)}) collective-permute-start(f32[2,48,1024]{2,1,0:T(8,128)S(1)} %pad_maximum_fusion.1.refs_7_), channel_id=1, source_target_pairs={{0,96},{1,97},{2,98},{3,99},{4,100},{5,101},{6,102},{7,103},{8,104... | collective-permute-start | bytes 1179656 | tf_op jit(solution)/shard_map/ppermute | solution.py:47
  52.6 11.8 %collective-permute-start.6 = (f32[96,1024]{1,0:T(8,128)S(1)}, f32[96,1024]{1,0:T(8,128)S(1)}, u32[]{:S(2)}, u32[]{:S(2)}) collective-permute-start(f32[96,1024]{1,0:T(8,128)S(1)} %slice.18), channel_id=1, source_target_pairs={{0,8},{1,9},{2,10},{3,11},{4,12},{5,13},{6,14},{7,15},{8,16},{9,17... | collective-permute-start | bytes 1179656 | tf_op jit(solution)/shard_map/ppermute | solution.py:47
  52.6 11.8 %collective-permute-start.7 = (f32[96,1024]{1,0:T(8,128)S(1)}, f32[96,1024]{1,0:T(8,128)S(1)}, u32[]{:S(2)}, u32[]{:S(2)}) collective-permute-start(f32[96,1024]{1,0:T(8,128)S(1)} %slice.19), channel_id=1, source_target_pairs={{0,24},{1,25},{2,26},{3,27},{4,28},{5,29},{6,30},{7,31},{8,0},{9,1... | collective-permute-start | bytes 1179656 | tf_op jit(solution)/shard_map/ppermute | solution.py:47
  82.0 12.0 %collective-permute-start.20 = (f32[2,48,1024]{2,1,0:T(8,128)}, f32[2,48,1024]{2,1,0:T(8,128)S(1)}, u32[]{:S(2)}, u32[]{:S(2)}) collective-permute-start(f32[2,48,1024]{2,1,0:T(8,128)} %get-tuple-element.53), channel_id=1, source_target_pairs={{0,32},{1,33},{2,34},{3,35},{4,36},{5,37},{6,38},{7,39},{8,40},{9,... | collective-permute-start | bytes 1179656 | tf_op jit(solution)/shard_map/ppermute | solution.py:47
  83.1 19.7 %collective-permute-start.21 = (f32[2,48,1024]{2,1,0:T(8,128)}, f32[2,48,1024]{2,1,0:T(8,128)S(1)}, u32[]{:S(2)}, u32[]{:S(2)}) collective-permute-start(f32[2,48,1024]{2,1,0:T(8,128)} %get-tuple-element.54), channel_id=1, source_target_pairs={{0,64},{1,65},{2,66},{3,67},{4,68},{5,69},{6,70},{7,71},{8,72},{9,... | collective-permute-start | bytes 1179656 | tf_op jit(solution)/shard_map/ppermute | solution.py:47
  85.0 17.8 %collective-permute-start.22 = (f32[2,48,1024]{2,1,0:T(8,128)}, f32[2,48,1024]{2,1,0:T(8,128)S(1)}, u32[]{:S(2)}, u32[]{:S(2)}) collective-permute-start(f32[2,48,1024]{2,1,0:T(8,128)} %get-tuple-element.55), channel_id=1, source_target_pairs={{0,96},{1,97},{2,98},{3,99},{4,100},{5,101},{6,102},{7,103},{8,104... | collective-permute-start | bytes 1179656 | tf_op jit(solution)/shard_map/ppermute | solution.py:47
  90.3 12.6 %collective-permute-start.17 = (f32[640,128]{1,0:T(8,128)}, f32[640,128]{1,0:T(8,128)S(1)}, u32[]{:S(2)}, u32[]{:S(2)}) collective-permute-start(f32[640,128]{1,0:T(8,128)} %get-tuple-element.49), channel_id=1, source_target_pairs={{0,8},{1,9},{2,10},{3,11},{4,12},{5,13},{6,14},{7,15},{8,16},{9,17... | collective-permute-start | bytes 983048 | tf_op jit(solution)/shard_map/ppermute | solution.py:47
  90.3 16.7 %collective-permute-start.18 = (f32[640,128]{1,0:T(8,128)}, f32[640,128]{1,0:T(8,128)S(1)}, u32[]{:S(2)}, u32[]{:S(2)}) collective-permute-start(f32[640,128]{1,0:T(8,128)} %get-tuple-element.50), channel_id=1, source_target_pairs={{0,16},{1,17},{2,18},{3,19},{4,20},{5,21},{6,22},{7,23},{8,24},{9,... | collective-permute-start | bytes 983048 | tf_op jit(solution)/shard_map/ppermute | solution.py:47
  94.0 14.1 %collective-permute-start.19 = (f32[640,128]{1,0:T(8,128)}, f32[640,128]{1,0:T(8,128)S(1)}, u32[]{:S(2)}, u32[]{:S(2)}) collective-permute-start(f32[640,128]{1,0:T(8,128)} %get-tuple-element.51), channel_id=1, source_target_pairs={{0,24},{1,25},{2,26},{3,27},{4,28},{5,29},{6,30},{7,31},{8,0},{9,1... | collective-permute-start | bytes 983048 | tf_op jit(solution)/shard_map/ppermute | solution.py:47
  136.8 29.0 %collective-permute-start.29 = (f32[48,1024]{1,0:T(8,128)S(1)}, f32[48,1024]{1,0:T(8,128)S(1)}, u32[]{:S(2)}, u32[]{:S(2)}) collective-permute-start(f32[48,1024]{1,0:T(8,128)S(1)} %dynamic-slice_bitcast_fusion), channel_id=1, source_target_pairs={{0,128},{1,129},{2,130},{3,131},{4,132},{5,133},{6,134},{7,135},{8... | collective-permute-start | bytes 589832 | tf_op jit(solution)/shard_map/ppermute | solution.py:47
  150.6 15.1 %collective-permute-start.33 = (f32[640,128]{1,0:T(8,128)}, f32[640,128]{1,0:T(8,128)S(1)}, u32[]{:S(2)}, u32[]{:S(2)}) collective-permute-start(f32[640,128]{1,0:T(8,128)} %shard_map.91.refs_0_), channel_id=1, source_target_pairs={{0,8},{1,9},{2,10},{3,11},{4,12},{5,13},{6,14},{7,15},{8,16},{9,17... | collective-permute-start | bytes 983048 | tf_op jit(solution)/shard_map/ppermute | solution.py:47
  154.4 19.2 %collective-permute-start.34 = (f32[640,128]{1,0:T(8,128)}, f32[640,128]{1,0:T(8,128)S(1)}, u32[]{:S(2)}, u32[]{:S(2)}) collective-permute-start(f32[640,128]{1,0:T(8,128)} %shard_map.91.refs_0_), channel_id=1, source_target_pairs={{0,16},{1,17},{2,18},{3,19},{4,20},{5,21},{6,22},{7,23},{8,24},{9,... | collective-permute-start | bytes 983048 | tf_op jit(solution)/shard_map/ppermute | solution.py:47
  157.0 16.6 %collective-permute-start.35 = (f32[640,128]{1,0:T(8,128)}, f32[640,128]{1,0:T(8,128)S(1)}, u32[]{:S(2)}, u32[]{:S(2)}) collective-permute-start(f32[640,128]{1,0:T(8,128)} %shard_map.91.refs_0_), channel_id=1, source_target_pairs={{0,24},{1,25},{2,26},{3,27},{4,28},{5,29},{6,30},{7,31},{8,0},{9,1... | collective-permute-start | bytes 983048 | tf_op jit(solution)/shard_map/ppermute | solution.py:47
  157.0 17.9 %collective-permute-start.36 = (f32[640,128]{1,0:T(8,128)}, f32[640,128]{1,0:T(8,128)S(1)}, u32[]{:S(2)}, u32[]{:S(2)}) collective-permute-start(f32[640,128]{1,0:T(8,128)} %shard_map.91.refs_0_), channel_id=1, source_target_pairs={{0,1},{1,0},{2,3},{3,2},{4,5},{5,4},{6,7},{7,6},{8,9},{9,8},{10,11... | collective-permute-start | bytes 983048 | tf_op jit(solution)/shard_map/ppermute | solution.py:47
  165.8 9.1 %collective-permute-start.37 = (f32[640,128]{1,0:T(8,128)S(1)}, f32[640,128]{1,0:T(8,128)S(1)}, u32[]{:S(2)}, u32[]{:S(2)}) collective-permute-start(f32[640,128]{1,0:T(8,128)S(1)} %collective-permute-done.33.refs_1_), channel_id=1, source_target_pairs={{0,1},{1,0},{2,3},{3,2},{4,5},{5,4},{6,7},{7,6},{8,9},{9,8},{10,11... | collective-permute-start | bytes 983048 | tf_op jit(solution)/shard_map/ppermute | solution.py:47
  (47 other events, 242.4 us)
where the time goes:
time: 181 us; the launch traced here: 180 us
  starting transfers between devices  83.7 us (46%)
  waiting for transfers between devices  48.9 us (27%)
  Pallas kernels  38.5 us (21%)
  local copies, waits for them, and re-layouts  5.41 us (3%)
  other arithmetic  2.76 us (2%)
    ppermute x40, starting transfers between devices, sent(): return lax.ppermute(value, BOTH, perm)  83.7 us
    ppermute x40, waiting for transfers between devices, sent(): return lax.ppermute(value, BOTH, perm)  48.9 us
    pallas_call x8, Pallas kernels, kernel(): pl.pallas_call(body, out_shape=jax.ShapeDtypeStruct(out_shapes, F32) if s...  38.5 us
    unnamed x62, local copies, waits for them, and re-layouts  5.32 us
  transfers between devices with their start and end apart: 40, of which 20 were waited for; matrix products, arithmetic and copies ran while one was open for 1% of the time, Pallas kernels for 11%

commit v1 on v0

--- a/solution.py
+++ b/solution.py
@@ -14,7 +14,6 @@
 HALF = W // 2
 SIZES = {"zh": 2, "x": 4, "y": 4, "zl": 4, "c": 2}
 BOTH = ("row", "col")
-CHUNKS = ((0, 1, 2, 3),)
 F32, BF16 = jnp.float32, jnp.bfloat16
 PAIRS = [(m, j) for j in range(NSUP) for m in range(j)]
 ALL_BLOCKS = PAIRS + [(j, j) for j in range(NSUP)]
@@ -128,95 +127,100 @@
 
 
 def put(piece, top, bot, row_of):
-    def step(i, carry):
-        r = lax.div(i, 3)
-        src = pl.multiple_of(i * 16, 16)
-        dst = pl.multiple_of(row_of(r) + (i - 3 * r) * 16, 16)
-        hi, lo = halves(piece[pl.ds(src, 16), :])
-        top[pl.ds(dst, 16), :] = hi
-        bot[pl.ds(dst, 16), :] = lo
+    def step(r, carry):
+        src = pl.multiple_of(r * RW, 16)
+        dst = pl.multiple_of(row_of(r), 16)
+        hi, lo = halves(piece[pl.ds(src, RW), :])
+        top[pl.ds(dst, RW), :] = hi
+        bot[pl.ds(dst, RW), :] = lo
         return carry
 
-    lax.fori_loop(0, piece.shape[0] // 16, step, 0)
-
-
-def put_columns(local, top, bot, blocks):
+    lax.fori_loop(0, piece.shape[0] // RW, step, 0)
+
+
+def near_kernel(local, near, twin, cross, out, ltop, lbot, rtop, rbot, top, bot):
+    at = place()
     span = local.shape[1] // 4
-    for i, k in enumerate(blocks):
-        src = pl.multiple_of(((place()["y"] - k) & 3) * span, 128)
+    for i, k in enumerate((0, 1, 3, 2)):
+        src = pl.multiple_of(((at["y"] - k) & 3) * span, 128)
 
         def step(t, carry, src=src, i=i):
-            rows = pl.ds(pl.multiple_of(t * 16, 16), 16)
+            rows = pl.ds(pl.multiple_of(t * RW, 16), RW)
             hi, lo = halves(local[rows, pl.ds(src, span)])
-            top[rows, i * span : (i + 1) * span] = hi
-            bot[rows, i * span : (i + 1) * span] = lo
+            ltop[rows, i * span : (i + 1) * span] = hi
+            lbot[rows, i * span : (i + 1) * span] = lo
             return carry
 
-        lax.fori_loop(0, local.shape[0] // 16, step, 0)
-
-
-def early_kernel(local, *refs):
-    pieces, out = refs[:6], refs[6]
-    top, bot, ltop, lbot = refs[7:]
+        lax.fori_loop(0, local.shape[0] // RW, step, 0)
+    put(cross, rtop, rbot, lambda r: ((at["x"] - r) & 3) * RW)
+    for par, piece in enumerate((near, twin)):
+        core = at["c"] ^ par
+        put(piece, top, bot, lambda r: (((at["zl"] - r) & 3) * 2 + core) * RW)
+    out[...] = mul((ltop[:, :span], lbot[:, :span]), (top[...], bot[...]))
+
+
+def early_kernel(start, ltop, lbot, left, right, ltwin, rtwin, out, top, bot):
     at = place()
-    put_columns(local, ltop, lbot, (0, 1, 3))
-    for i, piece in enumerate(pieces):
-        core = at["c"] ^ (i // 3)
-        start = (i % 3) * 8
-        put(piece, top, bot, lambda r: (start + ((at["zl"] - r) & 3) * 2 + core) * RW)
-    out[...] = mul((ltop[...], lbot[...]), (top[...], bot[...]))
-
-
-def main_kernel(chunk, order, skip, *refs):
-    local, base, early = refs[:3]
-    pieces, quads = refs[3:7], refs[7:11]
-    outs = refs[11:15]
+    span = ltop.shape[1] // 4
+    for i, piece in enumerate((left, right, ltwin, rtwin)):
+        core = at["c"] ^ (i // 2)
+        put(piece, top, bot, lambda r: ((i % 2) * 8 + ((at["zl"] - r) & 3) * 2 + core) * RW)
+    cols = slice(span, 3 * span)
+    out[...] = start[...] + mul((ltop[:, cols], lbot[:, cols]), (top[...], bot[...]))
+
+
+def main_kernel(order, *refs):
+    early, base, ltop, lbot, ra, rb, distant = refs[:7]
+    pieces, outs = refs[7:11], refs[11:15]
     kept, given = refs[15], refs[16]
-    top, bot, ltop, lbot, rtop, rbot, result, ptop, pbot = refs[17:]
+    top, bot, rtop, rbot, result, ptop, pbot = refs[17:]
     at = place()
-    put_columns(local, ltop, lbot, (2,))
+    span = ltop.shape[1] // 4
+    quad = ra.shape[0]
     for i, piece in enumerate(pieces):
         core = at["c"] ^ (i // 2)
         start = 2 * (i % 2)
         put(piece, top, bot, lambda r: (((at["zl"] - r - start) & 3) * 2 + core) * RW)
-    for k, piece in enumerate(quads):
-        xa = (at["x"] - k) & 3
-        for r in range(2):
-            put(piece.at[r], rtop, rbot, lambda _: ((at["zh"] ^ r) * 4 + xa) * RW)
-    result[...] = early[...] + mul((ltop[...], lbot[...]), (top[...], bot[...]))
+    here = pl.ds(pl.multiple_of(at["zh"] * quad, 16), quad)
+    rtop[here, :] = ra[...]
+    rbot[here, :] = rb[...]
+    put(distant, rtop, rbot, lambda r: (1 - at["zh"]) * quad + ((at["x"] - r) & 3) * RW)
+    cols = slice(3 * span, 4 * span)
+    value = early[...] + mul((ltop[:, cols], lbot[:, cols]), (top[...], bot[...]))
+    result[...] = value
+    hi, lo = halves(value)
+    ptop[...] = hi
+    pbot[...] = lo
     for k, out in enumerate(outs):
         xa = (at["x"] + k) & 3
-
-        def step(t, carry, out=out, xa=xa):
-            for r in range(2):
-                src = pl.multiple_of((r * 4 + xa) * RW + t * 8, 8)
-                out[r, pl.ds(pl.multiple_of(t * 8, 8), 8), :] = result[pl.ds(src, 8), :]
-            return carry
-
-        lax.fori_loop(0, RW // 8, step, 0)
+        for r in range(2):
+            out[r] = result[pl.ds(pl.multiple_of((r * 4 + xa) * RW, 16), RW), :]
     lead = (lax.axis_index("row") == 0) & (lax.axis_index("col") == 0)
-
-    def part(t, carry):
-        rows = pl.ds(pl.multiple_of(t * 16, 16), 16)
-        hi, lo = halves(result[rows, :])
-        ptop[rows, :] = hi
-        pbot[rows, :] = lo
-        return carry
-
-    lax.fori_loop(0, result.shape[0] // 16, part, 0)
-    cols = lambda s: (ptop[:, s * W : (s + 1) * W], pbot[:, s * W : (s + 1) * W])
-    beside = lambda s: (rtop[:, s * W : (s + 1) * W], rbot[:, s * W : (s + 1) * W])
     even = at["c"] == 0
     for i, (m, j) in enumerate(order):
-        if j in chunk:
-            block = mul(beside(m), cols(chunk.index(j)), (0, 0))
-        else:
-            block = mul(cols(chunk.index(m)), beside(j), (0, 0))
+        one, two = slice(m * W, (m + 1) * W), slice(j * W, (j + 1) * W)
+        block = mul((rtop[:, one], rbot[:, one]), (ptop[:, two], pbot[:, two]), (0, 0))
         rows = slice(i * W, (i + 1) * W)
-        block = block + jnp.where(lead, base[(skip + i) * W : (skip + i + 1) * W, :], 0.0)
+        block = block + jnp.where(lead, base[rows, :], 0.0)
         first, second = block[:, :HALF], block[:, HALF:]
         kept[rows, :] = jnp.where(even, first, second)
         given[rows, :] = jnp.where(even, second, first)
+
+
+def pick_kernel(*refs):
+    pieces, keep, give = refs[:4], refs[4], refs[5]
+    zh = place()["zh"]
+    for out, side in ((keep, zh), (give, 1 - zh)):
+        total = pieces[0][side]
+        for piece in pieces[1:]:
+            total = total + piece[side]
+        out[...] = total
+
+
+def columns_kernel(keep, got, out):
+    for j in range(NSUP):
+        cols = slice(j * W, (j + 1) * W)
+        out[j] = -(keep[:, cols] + got[:, cols])
 
 
 def join_kernel(axis, *refs):
@@ -229,17 +233,15 @@
 
 
 def add_split_kernel(axis, count, *refs):
-    values, outs = refs[:count], refs[count:-1]
-    whole = refs[-1]
+    values, outs = refs[:count], refs[count:]
     at = place()[axis]
-    total = values[0][...]
-    for value in values[1:]:
-        total = total + value[...]
-    whole[...] = total
     rows = outs[0].shape[0]
     for k, out in enumerate(outs):
-        src = pl.multiple_of(((at + k) & (SIZES[axis] - 1)) * rows, 8)
-        out[...] = whole[pl.ds(src, rows), :]
+        src = pl.ds(pl.multiple_of(((at + k) & (SIZES[axis] - 1)) * rows, 8), rows)
+        total = values[0][src, :]
+        for value in values[1:]:
+            total = total + value[src, :]
+        out[...] = total
 
 
 def final_kernel(orders, *refs):
@@ -269,7 +271,7 @@
         body,
         out_shape=jax.ShapeDtypeStruct(out_shapes, F32)
         if single
-        else [jax.ShapeDtypeStruct(s, F32) for s in out_shapes],
+        else [jax.ShapeDtypeStruct(s, F32) if isinstance(s[-1], int) else jax.ShapeDtypeStruct(*s) for s in out_shapes],
         in_specs=[SMEM] * smem + [VMEM] * (len(args) - smem),
         out_specs=VMEM if single else [VMEM] * len(out_shapes),
         scratch_shapes=[pltpu.VMEM(s, t) for s, t in scratch],
@@ -287,7 +289,6 @@
         functools.partial(add_split_kernel, axis, len(values)),
         list(values),
         [(rows // n, width)] * n,
-        [((rows, width), F32)],
     )
 
 
@@ -307,93 +308,85 @@
 
 
 def shards(inv_anc, factor_cols, couple, diag_inv, pattern, parent):
-    at = place()
     local = inv_anc.reshape(-1, inv_anc.shape[3])
     height = local.shape[0]
 
-    orders = []
-    done = set()
-    for chunk in CHUNKS:
-        order = [b for b in ALL_BLOCKS if (b[0] in chunk or b[1] in chunk) and b not in done]
-        done |= set(order)
-        orders.append(order)
-
     own = kernel(
         pre_kernel, [parent, pattern, factor_cols, couple], (RW, NSUP * W), smem=2, flops=1 << 20
     )
-
-    near = jnp.concatenate(gathered(own, "zl"), axis=0)
-    near, later = tie(near, own)
-    left, right = moved(near, "y", 1), moved(near, "y", 3)
-
-    pair = jnp.stack([later, moved(later, "zh", 1)])
-    pair, couple_later = tie(pair, couple)
-    quads = gathered(pair, "x")
-
-    (chunk,), (order,) = CHUNKS, orders
+    width = NSUP * W
+    tall = len(ALL_BLOCKS) * W
+    span = local.shape[1] // 4
+
+    near = gathered(own, "zl")
+    cross = gathered(own, "x")
+    _, couple_later = tie(own, couple)
     base = kernel(
-        functools.partial(base_kernel, order),
+        functools.partial(base_kernel, ALL_BLOCKS),
         [parent, couple_later, diag_inv],
-        (len(order) * W, W),
-        [((len(order), W, W), BF16)] * 6,
+        (tall, W),
+        [((len(ALL_BLOCKS), W, W), BF16)] * 6,
         smem=1,
         flops=1 << 31,
     )
-    left, right, base = tie(left, right, base)
+    near = jnp.concatenate(near, axis=0)
+    near, base, *cross = tie(near, base, *cross)
+    cross = jnp.concatenate(cross, axis=0)
+
+    left, right = moved(near, "y", 1), moved(near, "y", 3)
+    distant = moved(cross, "zh", 1)
+    start, ltop, lbot, ra, rb = kernel(
+        near_kernel,
+        [local, near, moved(near, "c", 1), cross],
+        [(height, width)] + [((height, 4 * span), BF16)] * 2 + [(cross.shape, BF16)] * 2,
+        [((span, width), BF16)] * 2,
+        flops=1 << 31,
+    )
+    left, right, start = tie(left, right, start)
     half = near.shape[0] // 2
     far_a, far_b = moved(left[:half], "y", 1), moved(right[half:], "y", 3)
-    mine = [near, left, right]
-    pieces = mine + [moved(v, "c", 1) for v in mine]
-    width = len(chunk) * W
-    tall = len(order) * W
-    span = local.shape[1] // 4
     early = kernel(
         early_kernel,
-        [local] + pieces,
+        [start, ltop, lbot, left, right, moved(left, "c", 1), moved(right, "c", 1)],
         (height, width),
-        [((3 * span, width), BF16)] * 2 + [((height, 3 * span), BF16)] * 2,
-        flops=1 << 32,
+        [((2 * span, width), BF16)] * 2,
+        flops=1 << 31,
     )
     far_a, far_b, early = tie(far_a, far_b, early)
-    columns = []
-    finals = []
-    skip = 0
     *parts, kept, given = kernel(
-        functools.partial(main_kernel, chunk, order, skip),
-        [local, base, early, far_a, far_b, moved(far_a, "c", 1), moved(far_b, "c", 1)] + quads,
+        functools.partial(main_kernel, ALL_BLOCKS),
+        [early, base, ltop, lbot, ra, rb, distant]
+        + [far_a, far_b, moved(far_a, "c", 1), moved(far_b, "c", 1)],
         [(2, RW, width)] * 4 + [(tall, HALF)] * 2,
         [((span, width), BF16)] * 2
-        + [((height, span), BF16)] * 2
-        + [((height, NSUP * W), BF16)] * 2
+        + [((height, width), BF16)] * 2
         + [((height, width), F32)]
         + [((height, width), BF16)] * 2,
         flops=1 << 32,
     )
+
     got = moved(given, "c", 1)
-    across = scattered(split_sum([kept, got], "y"), "y")
+    cut = split_sum([kept, got], "y")
     cols = scattered(parts, "x")
-    *across, first = tie(*across, total_of(cols))
-    total = total_of(scattered(split_sum(across, "x"), "x"))
+    across = scattered(cut, "y")
+    keep, give = kernel(pick_kernel, cols, [(RW, width)] * 2)
+    summed = moved(give, "zh", 1)
+    cut = split_sum(across, "x")
+    total = total_of(scattered(cut, "x"))
+    total, summed = tie(total, summed)
     total = total + sent(total, "zl", lambda a: a ^ 1)
     total = total + sent(total, "zl", lambda a: a ^ 2)
     total = total + moved(total, "zh", 1)
-    total, first = tie(total, first)
-    keep = lax.dynamic_index_in_dim(first, at["zh"], 0, keepdims=False)
-    give = lax.dynamic_index_in_dim(first, 1 - at["zh"], 0, keepdims=False)
-    columns.append(-(keep + moved(give, "zh", 1)))
-    parts = gathered(total, "x")
-    total = kernel(functools.partial(join_kernel, "x"), parts, (4 * parts[0].shape[0], HALF))
+    lines = gathered(total, "x")
+    total = kernel(functools.partial(join_kernel, "x"), lines, (4 * total.shape[0], HALF))
     lanes = gathered(total, "y")
-    finals += lanes + [moved(v, "c", 1) for v in lanes]
-
     pair_blocks, diagonal = kernel(
-        functools.partial(final_kernel, orders),
-        finals,
+        functools.partial(final_kernel, [ALL_BLOCKS]),
+        lanes + [moved(v, "c", 1) for v in lanes],
         [(len(PAIRS), W, W), (NSUP, W, W)],
-        [((len(order) * W, W), F32) for order in orders],
-    )
-    wide = jnp.concatenate(columns, axis=1)
-    columns = jnp.stack([wide[:, j * W : (j + 1) * W] for j in range(NSUP)])
+        [((tall, W), F32)],
+    )
+    columns = kernel(columns_kernel, [keep, summed], (NSUP, RW, W))
     return (columns, pair_blocks, diagonal)
 
 

time: 181 us -> 209 us (1.15)
  the two profiles are of different devices: /device:TPU:1 before, /device:TPU:97 now
where the time goes in v1:
time: 209 us; the launch traced here: 206 us
  starting transfers between devices  88.8 us (42%)
  waiting for transfers between devices  63.3 us (30%)
  Pallas kernels  44.8 us (21%)
  local copies, waits for them, and re-layouts  8.48 us (4%)
    ppermute x40, starting transfers between devices, sent(): return lax.ppermute(value, BOTH, perm)  88.8 us
    ppermute x40, waiting for transfers between devices, sent(): return lax.ppermute(value, BOTH, perm)  63.3 us
    pallas_call x11, Pallas kernels, kernel(): pl.pallas_call(body, out_shape=jax.ShapeDtypeStruct(out_shapes, F32) if s...  44.8 us
    unnamed x77, local copies, waits for them, and re-layouts  8.41 us
  transfers between devices with their start and end apart: 40, of which 17 were waited for; matrix products, arithmetic and copies ran while one was open for 0% of the time, Pallas kernels for 12%

profile of v1, /device:TPU:97, one launch (start us, length us, event | category | flops | bytes accessed | tf_op | source)
XLA Modules:
  0.0 206.5 jit_solution(5682919338835575607)
XLA Ops:
  7.1 4.2 %collective-permute-done.2 = f32[48,1024]{1,0:T(8,128)S(1)} collective-permute-done((f32[48,1024]{1,0:T(8,128)}, f32[48,1024]{1,0:T(8,128)S(1)}, u32[]{:S(2)}, u32[]{:S(2)}) %collective-permute-start.2) | collective-permute-done | bytes 196640 | tf_op jit(solution)/shard_map/ppermute | solution.py:46
  11.3 5.7 %shard_map.86.refs_1_ = f32[2560,256]{1,0:T(8,128)} custom-call(s32[4]{0:T(128)} %parent.3, f32[6,256,256]{2,1,0:T(8,128)} %couple.2, f32[4,256,256]{2,1,0:T(8,128)} %diag_inv.1), custom_call_target="tpu_custom_call" | custom-call | flops 2147483648 | bytes 2621456 | tf_op jit(solution)/shard_map/pallas_call | solution.py:270
  17.0 3.8 %collective-permute-done.1 = f32[48,1024]{1,0:T(8,128)S(1)} collective-permute-done((f32[48,1024]{1,0:T(8,128)}, f32[48,1024]{1,0:T(8,128)S(1)}, u32[]{:S(2)}, u32[]{:S(2)}) %collective-permute-start.1) | collective-permute-done | bytes 196640 | tf_op jit(solution)/shard_map/ppermute | solution.py:46
  27.1 5.8 %shard_map.87 = (f32[384,1024]{1,0:T(8,128)}, bf16[384,1536]{1,0:T(8,128)(2,1)}, bf16[384,1536]{1,0:T(8,128)(2,1)}, bf16[192,1024]{1,0:T(8,128)(2,1)}, bf16[192,1024]{1,0:T(8,128)(2,1)}) custom-call(f32[384,1536]{1,0:T(8,128)} %bitcast.1, f32[192,1024]{1,0:T(8,128)} %copy-done.6, f32[192,1024]{1,0:T(8,128)} %copy-done.29, f32[192,1024]{1,0:T(8,128)} %copy-done.26), custom_call_target="tpu_custom_call" | custom-call | flops 2147483648 | bytes 4718592 | tf_op jit(solution)/shard_map/pallas_call | solution.py:270
  32.9 9.7 %collective-permute-done.7.right = f32[192,1024]{1,0:T(8,128)S(1)} collective-permute-done((f32[192,1024]{1,0:T(8,128)S(1)}, f32[192,1024]{1,0:T(8,128)S(1)}, u32[]{:S(2)}, u32[]{:S(2)}) %collective-permute-start.7) | collective-permute-done | bytes 786464 | tf_op jit(solution)/shard_map/ppermute | solution.py:46
  48.6 4.2 %collective-permute-start.13 = (f32[192,1024]{1,0:T(8,128)S(1)}, f32[192,1024]{1,0:T(8,128)S(1)}, u32[]{:S(2)}, u32[]{:S(2)}) collective-permute-start(f32[192,1024]{1,0:T(8,128)S(1)} %copy-done.27), channel_id=1, source_target_pairs={{0,128},{1,129},{2,130},{3,131},{4,132},{5,133},{6,134},{7,135},{8... | collective-permute-start | bytes 2359304 | tf_op jit(solution)/shard_map/ppermute | solution.py:46
  54.0 6.7 %shard_map.88.refs_0_ = f32[384,1024]{1,0:T(8,128)} custom-call(f32[384,1024]{1,0:T(8,128)} %get-tuple-element.50.start, bf16[384,1536]{1,0:T(8,128)(2,1)} %get-tuple-element.51.ltop.refs_2_, bf16[384,1536]{1,0:T(8,128)(2,1)} %get-tuple-element.52.lbot.refs_3_, f32[192,1024]{1,0:T(8,128)} %copy-done.1, f32[192,1024]{1,0:T(8,128)} %copy-done, ...), custom_call_target="tpu_custom_call" | custom-call | flops 2147483648 | bytes 9437184 | tf_op jit(solution)/shard_map/pallas_call | solution.py:270
  62.2 9.4 %collective-permute-done.13.refs_6_ = f32[192,1024]{1,0:T(8,128)S(1)} collective-permute-done((f32[192,1024]{1,0:T(8,128)S(1)}, f32[192,1024]{1,0:T(8,128)S(1)}, u32[]{:S(2)}, u32[]{:S(2)}) %collective-permute-start.13) | collective-permute-done | bytes 786464 | tf_op jit(solution)/shard_map/ppermute | solution.py:46
  72.8 9.6 %shard_map.89 = (f32[2,48,1024]{2,1,0:T(8,128)}, f32[2,48,1024]{2,1,0:T(8,128)}, f32[2,48,1024]{2,1,0:T(8,128)}, f32[2,48,1024]{2,1,0:T(8,128)}, f32[2560,128]{1,0:T(8,128)}, /*index=5*/f32[2560,128]{1,0:T(8,128)}) custom-call(f32[384,1024]{1,0:T(8,128)} %shard_map.88.refs_0_, f32[2560,256]{1,0:T(8,128)} %shard_map.86.refs_1_, ...), custom_call_target="tpu_custom_call" | custom-call | flops 4294967296 | bytes 12845056 | tf_op jit(solution)/shard_map/pallas_call | solution.py:270
  95.3 3.9 %collective-permute-start.17 = (f32[2,48,1024]{2,1,0:T(8,128)S(1)}, f32[2,48,1024]{2,1,0:T(8,128)S(1)}, u32[]{:S(2)}, u32[]{:S(2)}) collective-permute-start(f32[2,48,1024]{2,1,0:T(8,128)S(1)} %copy-done.31), channel_id=1, source_target_pairs={{0,64},{1,65},{2,66},{3,67},{4,68},{5,69},{6,70},{7,71},{8,72},{9,... | collective-permute-start | bytes 1179656 | tf_op jit(solution)/shard_map/ppermute | solution.py:46
  101.6 3.6 %collective-permute-start.18 = (f32[2,48,1024]{2,1,0:T(8,128)S(1)}, f32[2,48,1024]{2,1,0:T(8,128)S(1)}, u32[]{:S(2)}, u32[]{:S(2)}) collective-permute-start(f32[2,48,1024]{2,1,0:T(8,128)S(1)} %copy-done.30), channel_id=1, source_target_pairs={{0,96},{1,97},{2,98},{3,99},{4,100},{5,101},{6,102},{7,103},{8,104... | collective-permute-start | bytes 1179656 | tf_op jit(solution)/shard_map/ppermute | solution.py:46
  105.2 3.4 %collective-permute-done.21.refs_2_ = f32[640,128]{1,0:T(8,128)S(1)} collective-permute-done((f32[640,128]{1,0:T(8,128)}, f32[640,128]{1,0:T(8,128)S(1)}, u32[]{:S(2)}, u32[]{:S(2)}) %collective-permute-start.21) | collective-permute-done | bytes 327712 | tf_op jit(solution)/shard_map/ppermute | solution.py:46
  112.9 3.5 %collective-permute-start.23 = (f32[160,128]{1,0:T(8,128)}, f32[160,128]{1,0:T(8,128)S(1)}, u32[]{:S(2)}, u32[]{:S(2)}) collective-permute-start(f32[160,128]{1,0:T(8,128)} %get-tuple-element.71), channel_id=1, source_target_pairs={{0,32},{1,33},{2,34},{3,35},{4,36},{5,37},{6,38},{7,39},{8,40},{9,... | collective-permute-start | bytes 245768 | tf_op jit(solution)/shard_map/ppermute | solution.py:46
  122.2 4.2 %collective-permute-start.26 = (f32[48,1024]{1,0:T(8,128)}, f32[48,1024]{1,0:T(8,128)S(1)}, u32[]{:S(2)}, u32[]{:S(2)}) collective-permute-start(f32[48,1024]{1,0:T(8,128)} %get-tuple-element.74), channel_id=1, source_target_pairs={{0,128},{1,129},{2,130},{3,131},{4,132},{5,133},{6,134},{7,135},{8... | collective-permute-start | bytes 589832 | tf_op jit(solution)/shard_map/ppermute | solution.py:46
  126.4 4.4 %collective-permute-done.26.got = f32[48,1024]{1,0:T(8,128)S(1)} collective-permute-done((f32[48,1024]{1,0:T(8,128)}, f32[48,1024]{1,0:T(8,128)S(1)}, u32[]{:S(2)}, u32[]{:S(2)}) %collective-permute-start.26) | collective-permute-done | bytes 196640 | tf_op jit(solution)/shard_map/ppermute | solution.py:46
  130.8 21.5 %collective-permute-start.27 = (f32[160,128]{1,0:T(8,128)S(1)}, f32[160,128]{1,0:T(8,128)S(1)}, u32[]{:S(2)}, u32[]{:S(2)}) collective-permute-start(f32[160,128]{1,0:T(8,128)S(1)} %add_add_fusion), channel_id=1, source_target_pairs={{0,2},{1,3},{2,0},{3,1},{4,6},{5,7},{6,4},{7,5},{8,10},{9,11},{10,... | collective-permute-start | bytes 245768 | tf_op jit(solution)/shard_map/ppermute | solution.py:46
  154.2 4.2 %collective-permute-done.28 = f32[160,128]{1,0:T(8,128)S(1)} collective-permute-done((f32[160,128]{1,0:T(8,128)S(1)}, f32[160,128]{1,0:T(8,128)S(1)}, u32[]{:S(2)}, u32[]{:S(2)}) %collective-permute-start.28) | collective-permute-done | bytes 81952 | tf_op jit(solution)/shard_map/ppermute | solution.py:46
  158.4 4.7 %collective-permute-start.29 = (f32[160,128]{1,0:T(8,128)S(1)}, f32[160,128]{1,0:T(8,128)S(1)}, u32[]{:S(2)}, u32[]{:S(2)}) collective-permute-start(f32[160,128]{1,0:T(8,128)S(1)} %add.22), channel_id=1, source_target_pairs={{0,128},{1,129},{2,130},{3,131},{4,132},{5,133},{6,134},{7,135},{8... | collective-permute-start | bytes 245768 | tf_op jit(solution)/shard_map/ppermute | solution.py:46
  167.7 3.2 %collective-permute-start.31 = (f32[160,128]{1,0:T(8,128)S(1)}, f32[160,128]{1,0:T(8,128)S(1)}, u32[]{:S(2)}, u32[]{:S(2)}) collective-permute-start(f32[160,128]{1,0:T(8,128)S(1)} %add.23.refs_0_), channel_id=1, source_target_pairs={{0,64},{1,65},{2,66},{3,67},{4,68},{5,69},{6,70},{7,71},{8,72},{9,... | collective-permute-start | bytes 245768 | tf_op jit(solution)/shard_map/ppermute | solution.py:46
  177.8 3.2 %collective-permute-start.35 = (f32[640,128]{1,0:T(8,128)}, f32[640,128]{1,0:T(8,128)S(1)}, u32[]{:S(2)}, u32[]{:S(2)}) collective-permute-start(f32[640,128]{1,0:T(8,128)} %shard_map.94.refs_0_), channel_id=1, source_target_pairs={{0,24},{1,25},{2,26},{3,27},{4,28},{5,29},{6,30},{7,31},{8,0},{9,1... | collective-permute-start | bytes 983048 | tf_op jit(solution)/shard_map/ppermute | solution.py:46
  181.6 4.2 %collective-permute-start.36 = (f32[640,128]{1,0:T(8,128)}, f32[640,128]{1,0:T(8,128)S(1)}, u32[]{:S(2)}, u32[]{:S(2)}) collective-permute-start(f32[640,128]{1,0:T(8,128)} %shard_map.94.refs_0_), channel_id=1, source_target_pairs={{0,1},{1,0},{2,3},{3,2},{4,5},{5,4},{6,7},{7,6},{8,9},{9,8},{10,11... | collective-permute-start | bytes 983048 | tf_op jit(solution)/shard_map/ppermute | solution.py:46
  185.8 3.7 %collective-permute-done.35.refs_3_ = f32[640,128]{1,0:T(8,128)S(1)} collective-permute-done((f32[640,128]{1,0:T(8,128)}, f32[640,128]{1,0:T(8,128)S(1)}, u32[]{:S(2)}, u32[]{:S(2)}) %collective-permute-start.35) | collective-permute-done | bytes 327712 | tf_op jit(solution)/shard_map/ppermute | solution.py:46
  189.6 6.7 %collective-permute-start.39 = (f32[640,128]{1,0:T(8,128)S(1)}, f32[640,128]{1,0:T(8,128)S(1)}, u32[]{:S(2)}, u32[]{:S(2)}) collective-permute-start(f32[640,128]{1,0:T(8,128)S(1)} %collective-permute-done.35.refs_3_), channel_id=1, source_target_pairs={{0,1},{1,0},{2,3},{3,2},{4,5},{5,4},{6,7},{7,6},{8,9},{9,8},{10,11... | collective-permute-start | bytes 983048 | tf_op jit(solution)/shard_map/ppermute | solution.py:46
  203.0 3.5 %shard_map.95 = (f32[6,256,256]{2,1,0:T(8,128)}, f32[4,256,256]{2,1,0:T(8,128)}) custom-call(f32[640,128]{1,0:T(8,128)} %shard_map.94.refs_0_, f32[640,128]{1,0:T(8,128)} %copy-done.12, f32[640,128]{1,0:T(8,128)} %copy-done.11, f32[640,128]{1,0:T(8,128)} %copy-done.10, f32[640,128]{1,0:T(8,128)} %copy-done.13, f32[640,128]{1,0:T(8,128)} %copy-done.19, ...), custom_call_target="tpu_custom_call" | custom-call | bytes 2621440 | tf_op jit(solution)/shard_map/pallas_call | solution.py:270
  (152 shorter events, 68.5 us)
Async XLA Ops:
  3.5 17.4 %collective-permute-start.5 = (f32[48,1024]{1,0:T(8,128)}, f32[48,1024]{1,0:T(8,128)S(1)}, u32[]{:S(2)}, u32[]{:S(2)}) collective-permute-start(f32[48,1024]{1,0:T(8,128)} %shard_map.85), channel_id=1, source_target_pairs={{0,96},{1,97},{2,98},{3,99},{4,100},{5,101},{6,102},{7,103},{8,104... | collective-permute-start | bytes 589832 | tf_op jit(solution)/shard_map/ppermute | solution.py:46
  6.0 14.9 %collective-permute-start.4 = (f32[48,1024]{1,0:T(8,128)}, f32[48,1024]{1,0:T(8,128)S(1)}, u32[]{:S(2)}, u32[]{:S(2)}) collective-permute-start(f32[48,1024]{1,0:T(8,128)} %shard_map.85), channel_id=1, source_target_pairs={{0,64},{1,65},{2,66},{3,67},{4,68},{5,69},{6,70},{7,71},{8,72},{9,... | collective-permute-start | bytes 589832 | tf_op jit(solution)/shard_map/ppermute | solution.py:46
  6.5 14.4 %collective-permute-start.3 = (f32[48,1024]{1,0:T(8,128)}, f32[48,1024]{1,0:T(8,128)S(1)}, u32[]{:S(2)}, u32[]{:S(2)}) collective-permute-start(f32[48,1024]{1,0:T(8,128)} %shard_map.85), channel_id=1, source_target_pairs={{0,32},{1,33},{2,34},{3,35},{4,36},{5,37},{6,38},{7,39},{8,40},{9,... | collective-permute-start | bytes 589832 | tf_op jit(solution)/shard_map/ppermute | solution.py:46
  7.1 13.7 %collective-permute-start.1 = (f32[48,1024]{1,0:T(8,128)}, f32[48,1024]{1,0:T(8,128)S(1)}, u32[]{:S(2)}, u32[]{:S(2)}) collective-permute-start(f32[48,1024]{1,0:T(8,128)} %shard_map.85), channel_id=1, source_target_pairs={{0,4},{1,5},{2,6},{3,7},{4,0},{5,1},{6,2},{7,3},{8,12},{9,13},{10,... | collective-permute-start | bytes 589832 | tf_op jit(solution)/shard_map/ppermute | solution.py:46
  23.1 19.5 %collective-permute-start.7 = (f32[192,1024]{1,0:T(8,128)S(1)}, f32[192,1024]{1,0:T(8,128)S(1)}, u32[]{:S(2)}, u32[]{:S(2)}) collective-permute-start(f32[192,1024]{1,0:T(8,128)S(1)} %pad_maximum_fusion.near), channel_id=1, source_target_pairs={{0,24},{1,25},{2,26},{3,27},{4,28},{5,29},{6,30},{7,31},{8,0},{9,1... | collective-permute-start | bytes 2359304 | tf_op jit(solution)/shard_map/ppermute | solution.py:46
  25.9 19.9 %collective-permute-start.6 = (f32[192,1024]{1,0:T(8,128)S(1)}, f32[192,1024]{1,0:T(8,128)S(1)}, u32[]{:S(2)}, u32[]{:S(2)}) collective-permute-start(f32[192,1024]{1,0:T(8,128)S(1)} %pad_maximum_fusion.near), channel_id=1, source_target_pairs={{0,8},{1,9},{2,10},{3,11},{4,12},{5,13},{6,14},{7,15},{8,16},{9,17... | collective-permute-start | bytes 2359304 | tf_op jit(solution)/shard_map/ppermute | solution.py:46
  47.1 13.6 %collective-permute-start.10 = (f32[96,1024]{1,0:T(8,128)S(1)}, f32[96,1024]{1,0:T(8,128)S(1)}, u32[]{:S(2)}, u32[]{:S(2)}) collective-permute-start(f32[96,1024]{1,0:T(8,128)S(1)} %slice.7), channel_id=1, source_target_pairs={{0,24},{1,25},{2,26},{3,27},{4,28},{5,29},{6,30},{7,31},{8,0},{9,1... | collective-permute-start | bytes 1179656 | tf_op jit(solution)/shard_map/ppermute | solution.py:46
  47.4 13.3 %collective-permute-start.9 = (f32[96,1024]{1,0:T(8,128)S(1)}, f32[96,1024]{1,0:T(8,128)S(1)}, u32[]{:S(2)}, u32[]{:S(2)}) collective-permute-start(f32[96,1024]{1,0:T(8,128)S(1)} %slice.6), channel_id=1, source_target_pairs={{0,8},{1,9},{2,10},{3,11},{4,12},{5,13},{6,14},{7,15},{8,16},{9,17... | collective-permute-start | bytes 1179656 | tf_op jit(solution)/shard_map/ppermute | solution.py:46
  48.6 23.0 %collective-permute-start.13 = (f32[192,1024]{1,0:T(8,128)S(1)}, f32[192,1024]{1,0:T(8,128)S(1)}, u32[]{:S(2)}, u32[]{:S(2)}) collective-permute-start(f32[192,1024]{1,0:T(8,128)S(1)} %copy-done.27), channel_id=1, source_target_pairs={{0,128},{1,129},{2,130},{3,131},{4,132},{5,133},{6,134},{7,135},{8... | collective-permute-start | bytes 2359304 | tf_op jit(solution)/shard_map/ppermute | solution.py:46
  60.7 10.9 %collective-permute-start.14 = (f32[96,1024]{1,0:T(8,128)S(1)}, f32[96,1024]{1,0:T(8,128)S(1)}, u32[]{:S(2)}, u32[]{:S(2)}) collective-permute-start(f32[96,1024]{1,0:T(8,128)S(1)} %collective-permute-done.9.refs_7_), channel_id=1, source_target_pairs={{0,1},{1,0},{2,3},{3,2},{4,5},{5,4},{6,7},{7,6},{8,9},{9,8},{10,11... | collective-permute-start | bytes 1179656 | tf_op jit(solution)/shard_map/ppermute | solution.py:46
  91.3 10.3 %collective-permute-start.20 = (f32[640,128]{1,0:T(8,128)}, f32[640,128]{1,0:T(8,128)S(1)}, u32[]{:S(2)}, u32[]{:S(2)}) collective-permute-start(f32[640,128]{1,0:T(8,128)} %get-tuple-element.67), channel_id=1, source_target_pairs={{0,8},{1,9},{2,10},{3,11},{4,12},{5,13},{6,14},{7,15},{8,16},{9,17... | collective-permute-start | bytes 983048 | tf_op jit(solution)/shard_map/ppermute | solution.py:46
  91.3 25.8 %collective-permute-start.16 = (f32[2,48,1024]{2,1,0:T(8,128)S(1)}, f32[2,48,1024]{2,1,0:T(8,128)S(1)}, u32[]{:S(2)}, u32[]{:S(2)}) collective-permute-start(f32[2,48,1024]{2,1,0:T(8,128)S(1)} %copy-done.32), channel_id=1, source_target_pairs={{0,32},{1,33},{2,34},{3,35},{4,36},{5,37},{6,38},{7,39},{8,40},{9,... | collective-permute-start | bytes 1179656 | tf_op jit(solution)/shard_map/ppermute | solution.py:46
  92.7 15.9 %collective-permute-start.21 = (f32[640,128]{1,0:T(8,128)}, f32[640,128]{1,0:T(8,128)S(1)}, u32[]{:S(2)}, u32[]{:S(2)}) collective-permute-start(f32[640,128]{1,0:T(8,128)} %get-tuple-element.68), channel_id=1, source_target_pairs={{0,16},{1,17},{2,18},{3,19},{4,20},{5,21},{6,22},{7,23},{8,24},{9,... | collective-permute-start | bytes 983048 | tf_op jit(solution)/shard_map/ppermute | solution.py:46
  95.3 14.8 %collective-permute-start.22 = (f32[640,128]{1,0:T(8,128)}, f32[640,128]{1,0:T(8,128)S(1)}, u32[]{:S(2)}, u32[]{:S(2)}) collective-permute-start(f32[640,128]{1,0:T(8,128)} %get-tuple-element.69), channel_id=1, source_target_pairs={{0,24},{1,25},{2,26},{3,27},{4,28},{5,29},{6,30},{7,31},{8,0},{9,1... | collective-permute-start | bytes 983048 | tf_op jit(solution)/shard_map/ppermute | solution.py:46
  95.3 23.7 %collective-permute-start.17 = (f32[2,48,1024]{2,1,0:T(8,128)S(1)}, f32[2,48,1024]{2,1,0:T(8,128)S(1)}, u32[]{:S(2)}, u32[]{:S(2)}) collective-permute-start(f32[2,48,1024]{2,1,0:T(8,128)S(1)} %copy-done.31), channel_id=1, source_target_pairs={{0,64},{1,65},{2,66},{3,67},{4,68},{5,69},{6,70},{7,71},{8,72},{9,... | collective-permute-start | bytes 1179656 | tf_op jit(solution)/shard_map/ppermute | solution.py:46
  101.6 17.4 %collective-permute-start.18 = (f32[2,48,1024]{2,1,0:T(8,128)S(1)}, f32[2,48,1024]{2,1,0:T(8,128)S(1)}, u32[]{:S(2)}, u32[]{:S(2)}) collective-permute-start(f32[2,48,1024]{2,1,0:T(8,128)S(1)} %copy-done.30), channel_id=1, source_target_pairs={{0,96},{1,97},{2,98},{3,99},{4,100},{5,101},{6,102},{7,103},{8,104... | collective-permute-start | bytes 1179656 | tf_op jit(solution)/shard_map/ppermute | solution.py:46
  112.9 13.5 %collective-permute-start.23 = (f32[160,128]{1,0:T(8,128)}, f32[160,128]{1,0:T(8,128)S(1)}, u32[]{:S(2)}, u32[]{:S(2)}) collective-permute-start(f32[160,128]{1,0:T(8,128)} %get-tuple-element.71), channel_id=1, source_target_pairs={{0,32},{1,33},{2,34},{3,35},{4,36},{5,37},{6,38},{7,39},{8,40},{9,... | collective-permute-start | bytes 245768 | tf_op jit(solution)/shard_map/ppermute | solution.py:46
  116.4 10.0 %collective-permute-start.24 = (f32[160,128]{1,0:T(8,128)}, f32[160,128]{1,0:T(8,128)S(1)}, u32[]{:S(2)}, u32[]{:S(2)}) collective-permute-start(f32[160,128]{1,0:T(8,128)} %get-tuple-element.72), channel_id=1, source_target_pairs={{0,64},{1,65},{2,66},{3,67},{4,68},{5,69},{6,70},{7,71},{8,72},{9,... | collective-permute-start | bytes 245768 | tf_op jit(solution)/shard_map/ppermute | solution.py:46
  130.8 23.3 %collective-permute-start.27 = (f32[160,128]{1,0:T(8,128)S(1)}, f32[160,128]{1,0:T(8,128)S(1)}, u32[]{:S(2)}, u32[]{:S(2)}) collective-permute-start(f32[160,128]{1,0:T(8,128)S(1)} %add_add_fusion), channel_id=1, source_target_pairs={{0,2},{1,3},{2,0},{3,1},{4,6},{5,7},{6,4},{7,5},{8,10},{9,11},{10,... | collective-permute-start | bytes 245768 | tf_op jit(solution)/shard_map/ppermute | solution.py:46
  177.8 11.8 %collective-permute-start.35 = (f32[640,128]{1,0:T(8,128)}, f32[640,128]{1,0:T(8,128)S(1)}, u32[]{:S(2)}, u32[]{:S(2)}) collective-permute-start(f32[640,128]{1,0:T(8,128)} %shard_map.94.refs_0_), channel_id=1, source_target_pairs={{0,24},{1,25},{2,26},{3,27},{4,28},{5,29},{6,30},{7,31},{8,0},{9,1... | collective-permute-start | bytes 983048 | tf_op jit(solution)/shard_map/ppermute | solution.py:46
  181.0 15.3 %collective-permute-start.34 = (f32[640,128]{1,0:T(8,128)}, f32[640,128]{1,0:T(8,128)S(1)}, u32[]{:S(2)}, u32[]{:S(2)}) collective-permute-start(f32[640,128]{1,0:T(8,128)} %shard_map.94.refs_0_), channel_id=1, source_target_pairs={{0,16},{1,17},{2,18},{3,19},{4,20},{5,21},{6,22},{7,23},{8,24},{9,... | collective-permute-start | bytes 983048 | tf_op jit(solution)/shard_map/ppermute | solution.py:46
  181.0 17.1 %collective-permute-start.33 = (f32[640,128]{1,0:T(8,128)}, f32[640,128]{1,0:T(8,128)S(1)}, u32[]{:S(2)}, u32[]{:S(2)}) collective-permute-start(f32[640,128]{1,0:T(8,128)} %shard_map.94.refs_0_), channel_id=1, source_target_pairs={{0,8},{1,9},{2,10},{3,11},{4,12},{5,13},{6,14},{7,15},{8,16},{9,17... | collective-permute-start | bytes 983048 | tf_op jit(solution)/shard_map/ppermute | solution.py:46
  181.6 19.7 %collective-permute-start.36 = (f32[640,128]{1,0:T(8,128)}, f32[640,128]{1,0:T(8,128)S(1)}, u32[]{:S(2)}, u32[]{:S(2)}) collective-permute-start(f32[640,128]{1,0:T(8,128)} %shard_map.94.refs_0_), channel_id=1, source_target_pairs={{0,1},{1,0},{2,3},{3,2},{4,5},{5,4},{6,7},{7,6},{8,9},{9,8},{10,11... | collective-permute-start | bytes 983048 | tf_op jit(solution)/shard_map/ppermute | solution.py:46
  189.6 11.8 %collective-permute-start.39 = (f32[640,128]{1,0:T(8,128)S(1)}, f32[640,128]{1,0:T(8,128)S(1)}, u32[]{:S(2)}, u32[]{:S(2)}) collective-permute-start(f32[640,128]{1,0:T(8,128)S(1)} %collective-permute-done.35.refs_3_), channel_id=1, source_target_pairs={{0,1},{1,0},{2,3},{3,2},{4,5},{5,4},{6,7},{7,6},{8,9},{9,8},{10,11... | collective-permute-start | bytes 983048 | tf_op jit(solution)/shard_map/ppermute | solution.py:46
  (53 other events, 366.4 us)

commit v2 on v1

--- a/solution.py
+++ b/solution.py
@@ -11,12 +11,13 @@
 W = 256
 NSUP = 4
 RW = 48
-HALF = W // 2
 SIZES = {"zh": 2, "x": 4, "y": 4, "zl": 4, "c": 2}
 BOTH = ("row", "col")
 F32, BF16 = jnp.float32, jnp.bfloat16
 PAIRS = [(m, j) for j in range(NSUP) for m in range(j)]
-ALL_BLOCKS = PAIRS + [(j, j) for j in range(NSUP)]
+BLOCKS = ([(0, 1), (0, 2), (1, 2), (0, 0), (1, 1)], [(0, 3), (1, 3), (2, 3), (2, 2), (3, 3)])
+FACTORS = ([(0, 5), (4, 2), (5, 2), (0, 4), (1, 5)], [(0, 5), (1, 5), (2, 5), (2, 4), (3, 5)])
+ALL_BLOCKS = BLOCKS[0] + BLOCKS[1]
 VMEM = pl.BlockSpec(memory_space=pltpu.VMEM)
 SMEM = pl.BlockSpec(memory_space=pltpu.SMEM)
 
@@ -92,7 +93,15 @@
             values[j] = values[j] - mul(left, halves(blocks[j, m]))
 
 
-def base_kernel(order, parent, couple, diag_inv, out, *held):
+def base_tables(order):
+    at = lambda q, j: order.index((q, j))
+    rows = [(at(q, j), at(q, q), at(q, j)) for q in range(NSUP) for j in range(q + 1, NSUP)]
+    split = len(rows)
+    rows += [(at(m, j), at(q, m), at(q, j)) for j in range(NSUP) for m in range(j + 1) for q in range(m)]
+    return split, rows
+
+
+def base_kernel(order, parent, table, couple, diag_inv, out, *held):
     chigh, clow, ihigh, ilow, shigh, slow = held
     at = lambda q, j: order.index((q, j))
 
@@ -115,15 +124,23 @@
     for q in range(NSUP):
         out[at(q, q) * W : (at(q, q) + 1) * W, :] = diag_inv[q]
         keep(shigh, slow, at(q, q), diag_inv[q])
-        for j in range(q + 1, NSUP):
-            i = at(q, j)
-            value = mul(kept(shigh, slow, at(q, q)), kept(ihigh, ilow, i))
-            out[i * W : (i + 1) * W, :] = value
-            keep(shigh, slow, i, value)
-    for i, (m, j) in enumerate(order):
-        rows = slice(i * W, (i + 1) * W)
-        for q in range(m):
-            out[rows, :] = out[rows, :] + mul(kept(ihigh, ilow, at(q, m)), kept(shigh, slow, at(q, j)), (0, 0))
+    split, rows = base_tables(order)
+
+    def scale(t, carry):
+        i = table[t, 0]
+        value = mul(kept(shigh, slow, table[t, 1]), kept(ihigh, ilow, table[t, 2]))
+        out[pl.ds(pl.multiple_of(i * W, W), W), :] = value
+        keep(shigh, slow, i, value)
+        return carry
+
+    def gain(t, carry):
+        where = pl.ds(pl.multiple_of(table[t, 0] * W, W), W)
+        left, right = kept(ihigh, ilow, table[t, 1]), kept(shigh, slow, table[t, 2])
+        out[where, :] = out[where, :] + mul(left, right, (0, 0))
+        return carry
+
+    lax.fori_loop(0, split, scale, 0)
+    lax.fori_loop(split, len(rows), gain, 0)
 
 
 def put(piece, top, bot, row_of):
@@ -169,42 +186,67 @@
     out[...] = start[...] + mul((ltop[:, cols], lbot[:, cols]), (top[...], bot[...]))
 
 
-def main_kernel(order, *refs):
-    early, base, ltop, lbot, ra, rb, distant = refs[:7]
-    pieces, outs = refs[7:11], refs[11:15]
-    kept, given = refs[15], refs[16]
-    top, bot, rtop, rbot, result, ptop, pbot = refs[17:]
+def late_kernel(*refs):
+    early, ltop, lbot = refs[:3]
+    pieces, outs = refs[3:7], refs[7:11]
+    high, low, give = refs[11:14]
+    top, bot, result = refs[14:]
     at = place()
     span = ltop.shape[1] // 4
-    quad = ra.shape[0]
     for i, piece in enumerate(pieces):
         core = at["c"] ^ (i // 2)
         start = 2 * (i % 2)
         put(piece, top, bot, lambda r: (((at["zl"] - r - start) & 3) * 2 + core) * RW)
-    here = pl.ds(pl.multiple_of(at["zh"] * quad, 16), quad)
-    rtop[here, :] = ra[...]
-    rbot[here, :] = rb[...]
-    put(distant, rtop, rbot, lambda r: (1 - at["zh"]) * quad + ((at["x"] - r) & 3) * RW)
     cols = slice(3 * span, 4 * span)
-    value = early[...] + mul((ltop[:, cols], lbot[:, cols]), (top[...], bot[...]))
-    result[...] = value
-    hi, lo = halves(value)
-    ptop[...] = hi
-    pbot[...] = lo
+    result[...] = early[...] + mul((ltop[:, cols], lbot[:, cols]), (top[...], bot[...]))
+    wide = give.shape[1]
+    high[...], low[...] = halves(result[:, pl.ds(pl.multiple_of(at["c"] * wide, wide), wide)])
+    give[...] = result[:, pl.ds(pl.multiple_of((1 - at["c"]) * wide, wide), wide)]
     for k, out in enumerate(outs):
         xa = (at["x"] + k) & 3
         for r in range(2):
             out[r] = result[pl.ds(pl.multiple_of((r * 4 + xa) * RW, 16), RW), :]
-    lead = (lax.axis_index("row") == 0) & (lax.axis_index("col") == 0)
-    even = at["c"] == 0
-    for i, (m, j) in enumerate(order):
-        one, two = slice(m * W, (m + 1) * W), slice(j * W, (j + 1) * W)
-        block = mul((rtop[:, one], rbot[:, one]), (ptop[:, two], pbot[:, two]), (0, 0))
+
+
+def window_blocks(top, bot, core):
+    for first, second in zip(*FACTORS):
+        left, right = [
+            pl.ds(pl.multiple_of(jnp.where(core == 0, first[side], second[side]) * W, W), W) for side in (0, 1)
+        ]
+        yield mul((top[:, left], bot[:, left]), (top[:, right], bot[:, right]), (0, 0))
+
+
+def own_kernel(high, low, ra, rb, distant, cross2, distant2, out, rtop, rbot, top, bot):
+    at = place()
+    quad = ra.shape[0]
+    wide = NSUP * W
+    here = pl.ds(pl.multiple_of(at["zh"] * quad, 16), quad)
+    top[here, :wide] = ra[...]
+    bot[here, :wide] = rb[...]
+    put(distant, top.at[:, :wide], bot.at[:, :wide], lambda r: (1 - at["zh"]) * quad + ((at["x"] - r) & 3) * RW)
+    top[:, wide:] = high[...]
+    bot[:, wide:] = low[...]
+    for i, block in enumerate(window_blocks(top, bot, at["c"])):
+        out[i * W : (i + 1) * W, :] = block
+    for side, piece in ((at["zh"], cross2), (1 - at["zh"], distant2)):
+        put(piece, rtop, rbot, lambda r: side * quad + ((at["x"] - r) & 3) * RW)
+
+
+def twin_kernel(own, rtop, rbot, got, base, *refs):
+    outs, (top, bot, whole) = refs[:4], refs[4:]
+    at = place()
+    wide = NSUP * W
+    top[:, :wide] = rtop[...]
+    bot[:, :wide] = rbot[...]
+    top[:, wide:], bot[:, wide:] = halves(got[...])
+    lead = (lax.axis_index("row") == 0) & (lax.axis_index("col") < 2)
+    for i, block in enumerate(window_blocks(top, bot, at["c"])):
         rows = slice(i * W, (i + 1) * W)
-        block = block + jnp.where(lead, base[rows, :], 0.0)
-        first, second = block[:, :HALF], block[:, HALF:]
-        kept[rows, :] = jnp.where(even, first, second)
-        given[rows, :] = jnp.where(even, second, first)
+        plus = base[pl.ds(pl.multiple_of(at["c"] * own.shape[0] + i * W, W), W), :]
+        whole[rows, :] = own[rows, :] + block + jnp.where(lead, plus, 0.0)
+    size = outs[0].shape[0]
+    for k, out in enumerate(outs):
+        out[...] = whole[pl.ds(pl.multiple_of(((at["y"] + k) & 3) * size, 8), size), :]
 
 
 def pick_kernel(*refs):
@@ -244,25 +286,19 @@
         out[...] = total
 
 
-def final_kernel(orders, *refs):
-    count = 8 * len(orders)
-    pieces, pair_out, diag_out, wholes = refs[:count], refs[count], refs[count + 1], refs[count + 2 :]
-    at = place()
-    for i, order in enumerate(orders):
-        whole = wholes[i]
-        for par in range(2):
-            for k in range(4):
-                piece = pieces[i * 8 + par * 4 + k]
-                rows = piece.shape[0]
-                dst = pl.multiple_of(((at["y"] - k) & 3) * rows, 8)
-                lane = pl.multiple_of((at["c"] ^ par) * HALF, HALF)
-                whole[pl.ds(dst, rows), pl.ds(lane, HALF)] = piece[...]
-        for b, (m, j) in enumerate(order):
-            rows = slice(b * W, (b + 1) * W)
-            if m == j:
-                diag_out[j] = whole[rows, :]
-            else:
-                pair_out[PAIRS.index((m, j))] = whole[rows, :]
+def final_kernel(*refs):
+    pieces, pair_out, diag_out, whole = refs[:8], refs[8], refs[9], refs[10]
+    at = place()
+    rows = pieces[0].shape[0]
+    for par in range(2):
+        core = at["c"] ^ par
+        for k in range(4):
+            dst = pl.multiple_of(((at["y"] - k) & 3) * rows, 8)
+            whole[pl.ds(dst, rows), :] = pieces[par * 4 + k][...]
+        for i in range(3):
+            pair_out[core * 3 + i] = whole[i * W : (i + 1) * W, :]
+        for i in range(2):
+            diag_out[core * 2 + i] = whole[(3 + i) * W : (4 + i) * W, :]
 
 
 def kernel(body, args, out_shapes, scratch=(), smem=0, flops=0):
@@ -321,12 +357,13 @@
     near = gathered(own, "zl")
     cross = gathered(own, "x")
     _, couple_later = tie(own, couple)
+    table = jnp.array(base_tables(ALL_BLOCKS)[1], jnp.int32)
     base = kernel(
         functools.partial(base_kernel, ALL_BLOCKS),
-        [parent, couple_later, diag_inv],
+        [parent, table, couple_later, diag_inv],
         (tall, W),
         [((len(ALL_BLOCKS), W, W), BF16)] * 6,
-        smem=1,
+        smem=2,
         flops=1 << 31,
     )
     near = jnp.concatenate(near, axis=0)
@@ -335,6 +372,7 @@
 
     left, right = moved(near, "y", 1), moved(near, "y", 3)
     distant = moved(cross, "zh", 1)
+    cross2 = moved(cross, "c", 1)
     start, ltop, lbot, ra, rb = kernel(
         near_kernel,
         [local, near, moved(near, "c", 1), cross],
@@ -353,39 +391,49 @@
         flops=1 << 31,
     )
     far_a, far_b, early = tie(far_a, far_b, early)
-    *parts, kept, given = kernel(
-        functools.partial(main_kernel, ALL_BLOCKS),
-        [early, base, ltop, lbot, ra, rb, distant]
-        + [far_a, far_b, moved(far_a, "c", 1), moved(far_b, "c", 1)],
-        [(2, RW, width)] * 4 + [(tall, HALF)] * 2,
-        [((span, width), BF16)] * 2
-        + [((height, width), BF16)] * 2
-        + [((height, width), F32)]
-        + [((height, width), BF16)] * 2,
-        flops=1 << 32,
-    )
-
-    got = moved(given, "c", 1)
-    cut = split_sum([kept, got], "y")
+    *parts, high, low, give = kernel(
+        late_kernel,
+        [early, ltop, lbot, far_a, far_b, moved(far_a, "c", 1), moved(far_b, "c", 1)],
+        [(2, RW, width)] * 4 + [((height, width // 2), BF16)] * 2 + [(height, width // 2)],
+        [((span, width), BF16)] * 2 + [((height, width), F32)],
+        flops=1 << 31,
+    )
+
+    got = moved(give, "c", 1)
+    sums, rtop, rbot = kernel(
+        own_kernel,
+        [high, low, ra, rb, distant, cross2, moved(distant, "c", 1)],
+        [(tall // 2, W)] + [((height, width), BF16)] * 2,
+        [((height, width + width // 2), BF16)] * 2,
+        flops=1 << 31,
+    )
+    cut = kernel(
+        twin_kernel,
+        [sums, rtop, rbot, got, base],
+        [(tall // 8, W)] * 4,
+        [((height, width + width // 2), BF16)] * 2 + [((tall // 2, W), F32)],
+        flops=1 << 31,
+    )
+    across = scattered(cut, "y")
     cols = scattered(parts, "x")
-    across = scattered(cut, "y")
     keep, give = kernel(pick_kernel, cols, [(RW, width)] * 2)
     summed = moved(give, "zh", 1)
     cut = split_sum(across, "x")
     total = total_of(scattered(cut, "x"))
-    total, summed = tie(total, summed)
     total = total + sent(total, "zl", lambda a: a ^ 1)
     total = total + sent(total, "zl", lambda a: a ^ 2)
     total = total + moved(total, "zh", 1)
     lines = gathered(total, "x")
-    total = kernel(functools.partial(join_kernel, "x"), lines, (4 * total.shape[0], HALF))
+    total = kernel(functools.partial(join_kernel, "x"), lines, (4 * total.shape[0], W))
     lanes = gathered(total, "y")
+    twins = [moved(v, "c", 1) for v in lanes]
     pair_blocks, diagonal = kernel(
-        functools.partial(final_kernel, [ALL_BLOCKS]),
-        lanes + [moved(v, "c", 1) for v in lanes],
+        final_kernel,
+        lanes + twins,
         [(len(PAIRS), W, W), (NSUP, W, W)],
-        [((tall, W), F32)],
-    )
+        [((tall // 2, W), F32)],
+    )
+    keep, pair_blocks, diagonal = tie(keep, pair_blocks, diagonal)
     columns = kernel(columns_kernel, [keep, summed], (NSUP, RW, W))
     return (columns, pair_blocks, diagonal)
 

time: 209 us -> 209 us (level)
  the two profiles are of different devices: /device:TPU:97 before, /device:TPU:35 now
where the time goes in v2:
time: 209 us
  starting transfers between devices  73.7 us (35%)
  waiting for transfers between devices  69.9 us (33%)
  Pallas kernels  52.5 us (25%)
  local copies, waits for them, and re-layouts  10.6 us (5%)
    ppermute x42, starting transfers between devices, sent(): return lax.ppermute(value, BOTH, perm)  73.7 us
    ppermute x42, waiting for transfers between devices, sent(): return lax.ppermute(value, BOTH, perm)  69.9 us
    pallas_call x12, Pallas kernels, kernel(): pl.pallas_call(body, out_shape=jax.ShapeDtypeStruct(out_shapes, F32) if s...  52.5 us
    unnamed x79, local copies, waits for them, and re-layouts  10.5 us
  transfers between devices with their start and end apart: 42, of which 15 were waited for; matrix products, arithmetic and copies ran while one was open for 0% of the time, Pallas kernels for 19%

profile of v2, /device:TPU:35, one launch (start us, length us, event | category | flops | bytes accessed | tf_op | source)
XLA Modules:
  0.0 208.6 jit_solution(14058377345365599004)
XLA Ops:
  0.6 2.8 %shard_map.94 = f32[48,1024]{1,0:T(8,128)} custom-call(s32[4]{0:T(128)} %parent.3, s32[4,48]{1,0:T(4,128)} %pattern.1, f32[4,48,256]{2,1,0:T(8,128)} %factor.1, f32[6,256,256]{2,1,0:T(8,128)} %couple.2), custom_call_target="tpu_custom_call" | custom-call | flops 1048576 | bytes 1770256 | tf_op jit(solution)/shard_map/pallas_call | solution.py:306
  11.9 9.0 %shard_map.95.base = f32[2560,256]{1,0:T(8,128)} custom-call(s32[4]{0:T(128)} %parent.3, s32[16,3]{1,0:T(8,128)} %constant.2.clone.table, f32[6,256,256]{2,1,0:T(8,128)} %couple.2, f32[4,256,256]{2,1,0:T(8,128)} %diag_inv.1), custom_call_target="tpu_custom_call" | custom-call | flops 2147483648 | bytes 2621648 | tf_op jit(solution)/shard_map/pallas_call | solution.py:306
  21.7 3.1 %collective-permute-done.2 = f32[48,1024]{1,0:T(8,128)S(1)} collective-permute-done((f32[48,1024]{1,0:T(8,128)}, f32[48,1024]{1,0:T(8,128)S(1)}, u32[]{:S(2)}, u32[]{:S(2)}) %collective-permute-start.2) | collective-permute-done | bytes 196640 | tf_op jit(solution)/shard_map/ppermute | solution.py:47
  24.9 4.9 %collective-permute-start.8 = (f32[192,1024]{1,0:T(8,128)S(1)}, f32[192,1024]{1,0:T(8,128)S(1)}, u32[]{:S(2)}, u32[]{:S(2)}) collective-permute-start(f32[192,1024]{1,0:T(8,128)S(1)} %pad_maximum_fusion.near), channel_id=1, source_target_pairs={{0,1},{1,0},{2,3},{3,2},{4,5},{5,4},{6,7},{7,6},{8,9},{9,8},{10,11... | collective-permute-start | bytes 2359304 | tf_op jit(solution)/shard_map/ppermute | solution.py:47
  33.8 5.8 %shard_map.96 = (f32[384,1024]{1,0:T(8,128)}, bf16[384,1536]{1,0:T(8,128)(2,1)}, bf16[384,1536]{1,0:T(8,128)(2,1)}, bf16[192,1024]{1,0:T(8,128)(2,1)}, bf16[192,1024]{1,0:T(8,128)(2,1)}) custom-call(f32[384,1536]{1,0:T(8,128)} %bitcast.1, f32[192,1024]{1,0:T(8,128)} %copy-done.5, f32[192,1024]{1,0:T(8,128)} %copy-done.30, f32[192,1024]{1,0:T(8,128)} %copy-done.24), custom_call_target="tpu_custom_call" | custom-call | flops 2147483648 | bytes 4718592 | tf_op jit(solution)/shard_map/pallas_call | solution.py:306
  39.6 10.6 %collective-permute-done.6.left = f32[192,1024]{1,0:T(8,128)S(1)} collective-permute-done((f32[192,1024]{1,0:T(8,128)S(1)}, f32[192,1024]{1,0:T(8,128)S(1)}, u32[]{:S(2)}, u32[]{:S(2)}) %collective-permute-start.6) | collective-permute-done | bytes 786464 | tf_op jit(solution)/shard_map/ppermute | solution.py:47
  53.9 5.0 %collective-permute-start.18 = (f32[192,1024]{1,0:T(8,128)S(1)}, f32[192,1024]{1,0:T(8,128)S(1)}, u32[]{:S(2)}, u32[]{:S(2)}) collective-permute-start(f32[192,1024]{1,0:T(8,128)S(1)} %copy-done.25), channel_id=1, source_target_pairs={{0,128},{1,129},{2,130},{3,131},{4,132},{5,133},{6,134},{7,135},{8... | collective-permute-start | bytes 2359304 | tf_op jit(solution)/shard_map/ppermute | solution.py:47
  60.1 6.7 %shard_map.97.refs_0_ = f32[384,1024]{1,0:T(8,128)} custom-call(f32[384,1024]{1,0:T(8,128)} %get-tuple-element.55.start, bf16[384,1536]{1,0:T(8,128)(2,1)} %get-tuple-element.56.ltop.refs_1_, bf16[384,1536]{1,0:T(8,128)(2,1)} %get-tuple-element.57.lbot.refs_2_, f32[192,1024]{1,0:T(8,128)} %copy-done, f32[192,1024]{1,0:T(8,128)} %copy-done.1, ...), custom_call_target="tpu_custom_call" | custom-call | flops 2147483648 | bytes 9437184 | tf_op jit(solution)/shard_map/pallas_call | solution.py:306
  68.4 22.0 %collective-permute-done.18.distant = f32[192,1024]{1,0:T(8,128)S(1)} collective-permute-done((f32[192,1024]{1,0:T(8,128)S(1)}, f32[192,1024]{1,0:T(8,128)S(1)}, u32[]{:S(2)}, u32[]{:S(2)}) %collective-permute-start.18) | collective-permute-done | bytes 786464 | tf_op jit(solution)/shard_map/ppermute | solution.py:47
  92.5 6.1 %shard_map.98 = (f32[2,48,1024]{2,1,0:T(8,128)}, f32[2,48,1024]{2,1,0:T(8,128)}, f32[2,48,1024]{2,1,0:T(8,128)}, f32[2,48,1024]{2,1,0:T(8,128)}, bf16[384,512]{1...) custom-call(f32[384,1024]{1,0:T(8,128)} %shard_map.97.refs_0_, ...), custom_call_target="tpu_custom_call" | custom-call | flops 2147483648 | bytes 7864320 | tf_op jit(solution)/shard_map/pallas_call | solution.py:306
  99.8 5.4 %shard_map.100 = (f32[1280,256]{1,0:T(8,128)}, bf16[384,1024]{1,0:T(8,128)(2,1)}, bf16[384,1024]{1,0:T(8,128)(2,1)}) custom-call(bf16[384,512]{1,0:T(8,128)(2,1)} %get-tuple-element.66.high, bf16[384,512]{1,0:T(8,128)(2,1)} %get-tuple-element.67.low, bf16[192,1024]{1,0:T(8,128)(2,1)} %get-tuple-element.68.ra, bf16[192,1024]{1,0:T(8,128)(2,1)} %get-tuple-element.69.rb, ...), custom_call_target="tpu_custom_call" | custom-call | flops 2147483648 | bytes 5505024 | tf_op jit(solution)/shard_map/pallas_call | solution.py:306
  106.0 5.6 %shard_map.101 = (f32[320,256]{1,0:T(8,128)}, f32[320,256]{1,0:T(8,128)}, f32[320,256]{1,0:T(8,128)}, f32[320,256]{1,0:T(8,128)}) custom-call(f32[1280,256]{1,0:T(8,128)} %get-tuple-element.70.own, bf16[384,1024]{1,0:T(8,128)(2,1)} %get-tuple-element.71.rtop, bf16[384,1024]{1,0:T(8,128)(2,1)} %get-tuple-element.72.rbot, f32[384,512]{1,0:T(8,128)} %copy-done.29, ...), custom_call_target="tpu_custom_call" | custom-call | flops 2147483648 | bytes 7864320 | tf_op jit(solution)/shard_map/pallas_call | solution.py:306
  111.8 3.7 %collective-permute-start.23 = (f32[320,256]{1,0:T(8,128)}, f32[320,256]{1,0:T(8,128)S(1)}, u32[]{:S(2)}, u32[]{:S(2)}) collective-permute-start(f32[320,256]{1,0:T(8,128)} %get-tuple-element.77), channel_id=1, source_target_pairs={{0,16},{1,17},{2,18},{3,19},{4,20},{5,21},{6,22},{7,23},{8,24},{9,... | collective-permute-start | bytes 983048 | tf_op jit(solution)/shard_map/ppermute | solution.py:47
  115.5 6.4 %collective-permute-done.22.refs_1_ = f32[320,256]{1,0:T(8,128)S(1)} collective-permute-done((f32[320,256]{1,0:T(8,128)}, f32[320,256]{1,0:T(8,128)S(1)}, u32[]{:S(2)}, u32[]{:S(2)}) %collective-permute-start.22) | collective-permute-done | bytes 327712 | tf_op jit(solution)/shard_map/ppermute | solution.py:47
  121.9 8.2 %collective-permute-done.23.refs_2_ = f32[320,256]{1,0:T(8,128)S(1)} collective-permute-done((f32[320,256]{1,0:T(8,128)}, f32[320,256]{1,0:T(8,128)S(1)}, u32[]{:S(2)}, u32[]{:S(2)}) %collective-permute-start.23) | collective-permute-done | bytes 327712 | tf_op jit(solution)/shard_map/ppermute | solution.py:47
  145.8 2.9 %collective-permute-done.29 = f32[80,256]{1,0:T(8,128)S(1)} collective-permute-done((f32[80,256]{1,0:T(8,128)S(1)}, f32[80,256]{1,0:T(8,128)S(1)}, u32[]{:S(2)}, u32[]{:S(2)}) %collective-permute-start.29) | collective-permute-done | bytes 81952 | tf_op jit(solution)/shard_map/ppermute | solution.py:47
  148.6 5.3 %collective-permute-start.30 = (f32[80,256]{1,0:T(8,128)S(1)}, f32[80,256]{1,0:T(8,128)S(1)}, u32[]{:S(2)}, u32[]{:S(2)}) collective-permute-start(f32[80,256]{1,0:T(8,128)S(1)} %add.22), channel_id=1, source_target_pairs={{0,128},{1,129},{2,130},{3,131},{4,132},{5,133},{6,134},{7,135},{8... | collective-permute-start | bytes 245768 | tf_op jit(solution)/shard_map/ppermute | solution.py:47
  166.5 2.8 %collective-permute-start.35 = (f32[320,256]{1,0:T(8,128)}, f32[320,256]{1,0:T(8,128)S(1)}, u32[]{:S(2)}, u32[]{:S(2)}) collective-permute-start(f32[320,256]{1,0:T(8,128)} %shard_map.103.refs_0_), channel_id=1, source_target_pairs={{0,16},{1,17},{2,18},{3,19},{4,20},{5,21},{6,22},{7,23},{8,24},{9,... | collective-permute-start | bytes 983048 | tf_op jit(solution)/shard_map/ppermute | solution.py:47
  173.0 7.4 %collective-permute-start.37 = (f32[320,256]{1,0:T(8,128)}, f32[320,256]{1,0:T(8,128)S(1)}, u32[]{:S(2)}, u32[]{:S(2)}) collective-permute-start(f32[320,256]{1,0:T(8,128)} %shard_map.103.refs_0_), channel_id=1, source_target_pairs={{0,1},{1,0},{2,3},{3,2},{4,5},{5,4},{6,7},{7,6},{8,9},{9,8},{10,11... | collective-permute-start | bytes 983048 | tf_op jit(solution)/shard_map/ppermute | solution.py:47
  180.4 2.8 %collective-permute-start.38 = (f32[320,256]{1,0:T(8,128)S(1)}, f32[320,256]{1,0:T(8,128)S(1)}, u32[]{:S(2)}, u32[]{:S(2)}) collective-permute-start(f32[320,256]{1,0:T(8,128)S(1)} %collective-permute-done.34.refs_1_), channel_id=1, source_target_pairs={{0,1},{1,0},{2,3},{3,2},{4,5},{5,4},{6,7},{7,6},{8,9},{9,8},{10,11... | collective-permute-start | bytes 983048 | tf_op jit(solution)/shard_map/ppermute | solution.py:47
  183.2 5.0 %collective-permute-start.39 = (f32[320,256]{1,0:T(8,128)S(1)}, f32[320,256]{1,0:T(8,128)S(1)}, u32[]{:S(2)}, u32[]{:S(2)}) collective-permute-start(f32[320,256]{1,0:T(8,128)S(1)} %collective-permute-done.35.refs_2_), channel_id=1, source_target_pairs={{0,1},{1,0},{2,3},{3,2},{4,5},{5,4},{6,7},{7,6},{8,9},{9,8},{10,11... | collective-permute-start | bytes 983048 | tf_op jit(solution)/shard_map/ppermute | solution.py:47
  191.3 4.2 %collective-permute-start.41 = (f32[48,1024]{1,0:T(8,128)}, f32[48,1024]{1,0:T(8,128)S(1)}, u32[]{:S(2)}, u32[]{:S(2)}) collective-permute-start(f32[48,1024]{1,0:T(8,128)} %get-tuple-element.86), channel_id=1, source_target_pairs={{0,128},{1,129},{2,130},{3,131},{4,132},{5,133},{6,134},{7,135},{8... | collective-permute-start | bytes 589832 | tf_op jit(solution)/shard_map/ppermute | solution.py:47
  197.1 3.5 %shard_map.104 = (f32[6,256,256]{2,1,0:T(8,128)}, f32[4,256,256]{2,1,0:T(8,128)}) custom-call(f32[320,256]{1,0:T(8,128)} %shard_map.103.refs_0_, f32[320,256]{1,0:T(8,128)} %copy-done.9, f32[320,256]{1,0:T(8,128)} %copy-done.10, f32[320,256]{1,0:T(8,128)} %copy-done.11, f32[320,256]{1,0:T(8,128)} %copy-done.12, f32[320,256]{1,0:T(8,128)} %copy-done.13, ...), custom_call_target="tpu_custom_call" | custom-call | bytes 2621440 | tf_op jit(solution)/shard_map/pallas_call | solution.py:306
  200.6 5.6 %collective-permute-done.41.got = f32[48,1024]{1,0:T(8,128)S(1)} collective-permute-done((f32[48,1024]{1,0:T(8,128)}, f32[48,1024]{1,0:T(8,128)S(1)}, u32[]{:S(2)}, u32[]{:S(2)}) %collective-permute-start.41) | collective-permute-done | bytes 196640 | tf_op jit(solution)/shard_map/ppermute | solution.py:47
  (159 shorter events, 63.0 us)
Async XLA Ops:
  5.1 16.5 %collective-permute-start.1 = (f32[48,1024]{1,0:T(8,128)}, f32[48,1024]{1,0:T(8,128)S(1)}, u32[]{:S(2)}, u32[]{:S(2)}) collective-permute-start(f32[48,1024]{1,0:T(8,128)} %shard_map.94), channel_id=1, source_target_pairs={{0,4},{1,5},{2,6},{3,7},{4,0},{5,1},{6,2},{7,3},{8,12},{9,13},{10,... | collective-permute-start | bytes 589832 | tf_op jit(solution)/shard_map/ppermute | solution.py:47
  6.5 18.3 %collective-permute-start.2 = (f32[48,1024]{1,0:T(8,128)}, f32[48,1024]{1,0:T(8,128)S(1)}, u32[]{:S(2)}, u32[]{:S(2)}) collective-permute-start(f32[48,1024]{1,0:T(8,128)} %shard_map.94), channel_id=1, source_target_pairs={{0,6},{1,7},{2,0},{3,1},{4,2},{5,3},{6,4},{7,5},{8,14},{9,15},{10,... | collective-permute-start | bytes 589832 | tf_op jit(solution)/shard_map/ppermute | solution.py:47
  7.9 16.9 %collective-permute-start.3 = (f32[48,1024]{1,0:T(8,128)}, f32[48,1024]{1,0:T(8,128)S(1)}, u32[]{:S(2)}, u32[]{:S(2)}) collective-permute-start(f32[48,1024]{1,0:T(8,128)} %shard_map.94), channel_id=1, source_target_pairs={{0,32},{1,33},{2,34},{3,35},{4,36},{5,37},{6,38},{7,39},{8,40},{9,... | collective-permute-start | bytes 589832 | tf_op jit(solution)/shard_map/ppermute | solution.py:47
  9.2 15.7 %collective-permute-start.4 = (f32[48,1024]{1,0:T(8,128)}, f32[48,1024]{1,0:T(8,128)S(1)}, u32[]{:S(2)}, u32[]{:S(2)}) collective-permute-start(f32[48,1024]{1,0:T(8,128)} %shard_map.94), channel_id=1, source_target_pairs={{0,64},{1,65},{2,66},{3,67},{4,68},{5,69},{6,70},{7,71},{8,72},{9,... | collective-permute-start | bytes 589832 | tf_op jit(solution)/shard_map/ppermute | solution.py:47
  10.0 14.9 %collective-permute-start.5 = (f32[48,1024]{1,0:T(8,128)}, f32[48,1024]{1,0:T(8,128)S(1)}, u32[]{:S(2)}, u32[]{:S(2)}) collective-permute-start(f32[48,1024]{1,0:T(8,128)} %shard_map.94), channel_id=1, source_target_pairs={{0,96},{1,97},{2,98},{3,99},{4,100},{5,101},{6,102},{7,103},{8,104... | collective-permute-start | bytes 589832 | tf_op jit(solution)/shard_map/ppermute | solution.py:47
  29.8 20.3 %collective-permute-start.6 = (f32[192,1024]{1,0:T(8,128)S(1)}, f32[192,1024]{1,0:T(8,128)S(1)}, u32[]{:S(2)}, u32[]{:S(2)}) collective-permute-start(f32[192,1024]{1,0:T(8,128)S(1)} %pad_maximum_fusion.near), channel_id=1, source_target_pairs={{0,8},{1,9},{2,10},{3,11},{4,12},{5,13},{6,14},{7,15},{8,16},{9,17... | collective-permute-start | bytes 2359304 | tf_op jit(solution)/shard_map/ppermute | solution.py:47
  31.2 19.0 %collective-permute-start.7 = (f32[192,1024]{1,0:T(8,128)S(1)}, f32[192,1024]{1,0:T(8,128)S(1)}, u32[]{:S(2)}, u32[]{:S(2)}) collective-permute-start(f32[192,1024]{1,0:T(8,128)S(1)} %pad_maximum_fusion.near), channel_id=1, source_target_pairs={{0,24},{1,25},{2,26},{3,27},{4,28},{5,29},{6,30},{7,31},{8,0},{9,1... | collective-permute-start | bytes 2359304 | tf_op jit(solution)/shard_map/ppermute | solution.py:47
  51.3 15.4 %collective-permute-start.10 = (f32[96,1024]{1,0:T(8,128)S(1)}, f32[96,1024]{1,0:T(8,128)S(1)}, u32[]{:S(2)}, u32[]{:S(2)}) collective-permute-start(f32[96,1024]{1,0:T(8,128)S(1)} %slice.7), channel_id=1, source_target_pairs={{0,24},{1,25},{2,26},{3,27},{4,28},{5,29},{6,30},{7,31},{8,0},{9,1... | collective-permute-start | bytes 1179656 | tf_op jit(solution)/shard_map/ppermute | solution.py:47
  53.9 12.9 %collective-permute-start.9 = (f32[96,1024]{1,0:T(8,128)S(1)}, f32[96,1024]{1,0:T(8,128)S(1)}, u32[]{:S(2)}, u32[]{:S(2)}) collective-permute-start(f32[96,1024]{1,0:T(8,128)S(1)} %slice.6), channel_id=1, source_target_pairs={{0,8},{1,9},{2,10},{3,11},{4,12},{5,13},{6,14},{7,15},{8,16},{9,17... | collective-permute-start | bytes 1179656 | tf_op jit(solution)/shard_map/ppermute | solution.py:47
  53.9 36.5 %collective-permute-start.18 = (f32[192,1024]{1,0:T(8,128)S(1)}, f32[192,1024]{1,0:T(8,128)S(1)}, u32[]{:S(2)}, u32[]{:S(2)}) collective-permute-start(f32[192,1024]{1,0:T(8,128)S(1)} %copy-done.25), channel_id=1, source_target_pairs={{0,128},{1,129},{2,130},{3,131},{4,132},{5,133},{6,134},{7,135},{8... | collective-permute-start | bytes 2359304 | tf_op jit(solution)/shard_map/ppermute | solution.py:47
  66.8 24.1 %collective-permute-start.13 = (f32[96,1024]{1,0:T(8,128)S(1)}, f32[96,1024]{1,0:T(8,128)S(1)}, u32[]{:S(2)}, u32[]{:S(2)}) collective-permute-start(f32[96,1024]{1,0:T(8,128)S(1)} %collective-permute-done.9.refs_3_), channel_id=1, source_target_pairs={{0,1},{1,0},{2,3},{3,2},{4,5},{5,4},{6,7},{7,6},{8,9},{9,8},{10,11... | collective-permute-start | bytes 1179656 | tf_op jit(solution)/shard_map/ppermute | solution.py:47
  67.9 23.0 %collective-permute-start.14 = (f32[96,1024]{1,0:T(8,128)S(1)}, f32[96,1024]{1,0:T(8,128)S(1)}, u32[]{:S(2)}, u32[]{:S(2)}) collective-permute-start(f32[96,1024]{1,0:T(8,128)S(1)} %collective-permute-done.10.refs_4_), channel_id=1, source_target_pairs={{0,1},{1,0},{2,3},{3,2},{4,5},{5,4},{6,7},{7,6},{8,9},{9,8},{10,11... | collective-permute-start | bytes 1179656 | tf_op jit(solution)/shard_map/ppermute | solution.py:47
  68.0 30.6 %collective-permute-start.19 = (f32[192,1024]{1,0:T(8,128)S(1)}, f32[192,1024]{1,0:T(8,128)S(1)}, u32[]{:S(2)}, u32[]{:S(2)}) collective-permute-start(f32[192,1024]{1,0:T(8,128)S(1)} %copy-done.25), channel_id=1, source_target_pairs={{0,1},{1,0},{2,3},{3,2},{4,5},{5,4},{6,7},{7,6},{8,9},{9,8},{10,11... | collective-permute-start | bytes 2359304 | tf_op jit(solution)/shard_map/ppermute | solution.py:47
  111.8 18.3 %collective-permute-start.23 = (f32[320,256]{1,0:T(8,128)}, f32[320,256]{1,0:T(8,128)S(1)}, u32[]{:S(2)}, u32[]{:S(2)}) collective-permute-start(f32[320,256]{1,0:T(8,128)} %get-tuple-element.77), channel_id=1, source_target_pairs={{0,16},{1,17},{2,18},{3,19},{4,20},{5,21},{6,22},{7,23},{8,24},{9,... | collective-permute-start | bytes 983048 | tf_op jit(solution)/shard_map/ppermute | solution.py:47
  115.5 14.6 %collective-permute-start.24 = (f32[320,256]{1,0:T(8,128)}, f32[320,256]{1,0:T(8,128)S(1)}, u32[]{:S(2)}, u32[]{:S(2)}) collective-permute-start(f32[320,256]{1,0:T(8,128)} %get-tuple-element.78), channel_id=1, source_target_pairs={{0,24},{1,25},{2,26},{3,27},{4,28},{5,29},{6,30},{7,31},{8,0},{9,1... | collective-permute-start | bytes 983048 | tf_op jit(solution)/shard_map/ppermute | solution.py:47
  141.0 28.4 %collective-permute-start.15 = (f32[2,48,1024]{2,1,0:T(8,128)S(1)}, f32[2,48,1024]{2,1,0:T(8,128)S(1)}, u32[]{:S(2)}, u32[]{:S(2)}) collective-permute-start(f32[2,48,1024]{2,1,0:T(8,128)S(1)} %copy-done.33), channel_id=1, source_target_pairs={{0,32},{1,33},{2,34},{3,35},{4,36},{5,37},{6,38},{7,39},{8,40},{9,... | collective-permute-start | bytes 1179656 | tf_op jit(solution)/shard_map/ppermute | solution.py:47
  166.3 14.1 %collective-permute-start.34 = (f32[320,256]{1,0:T(8,128)}, f32[320,256]{1,0:T(8,128)S(1)}, u32[]{:S(2)}, u32[]{:S(2)}) collective-permute-start(f32[320,256]{1,0:T(8,128)} %shard_map.103.refs_0_), channel_id=1, source_target_pairs={{0,8},{1,9},{2,10},{3,11},{4,12},{5,13},{6,14},{7,15},{8,16},{9,17... | collective-permute-start | bytes 983048 | tf_op jit(solution)/shard_map/ppermute | solution.py:47
  166.5 16.7 %collective-permute-start.35 = (f32[320,256]{1,0:T(8,128)}, f32[320,256]{1,0:T(8,128)S(1)}, u32[]{:S(2)}, u32[]{:S(2)}) collective-permute-start(f32[320,256]{1,0:T(8,128)} %shard_map.103.refs_0_), channel_id=1, source_target_pairs={{0,16},{1,17},{2,18},{3,19},{4,20},{5,21},{6,22},{7,23},{8,24},{9,... | collective-permute-start | bytes 983048 | tf_op jit(solution)/shard_map/ppermute | solution.py:47
  169.3 18.9 %collective-permute-start.36 = (f32[320,256]{1,0:T(8,128)}, f32[320,256]{1,0:T(8,128)S(1)}, u32[]{:S(2)}, u32[]{:S(2)}) collective-permute-start(f32[320,256]{1,0:T(8,128)} %shard_map.103.refs_0_), channel_id=1, source_target_pairs={{0,24},{1,25},{2,26},{3,27},{4,28},{5,29},{6,30},{7,31},{8,0},{9,1... | collective-permute-start | bytes 983048 | tf_op jit(solution)/shard_map/ppermute | solution.py:47
  169.4 18.9 %collective-permute-start.17 = (f32[2,48,1024]{2,1,0:T(8,128)S(1)}, f32[2,48,1024]{2,1,0:T(8,128)S(1)}, u32[]{:S(2)}, u32[]{:S(2)}) collective-permute-start(f32[2,48,1024]{2,1,0:T(8,128)S(1)} %copy-done.31), channel_id=1, source_target_pairs={{0,96},{1,97},{2,98},{3,99},{4,100},{5,101},{6,102},{7,103},{8,104... | collective-permute-start | bytes 1179656 | tf_op jit(solution)/shard_map/ppermute | solution.py:47
  173.0 22.4 %collective-permute-start.37 = (f32[320,256]{1,0:T(8,128)}, f32[320,256]{1,0:T(8,128)S(1)}, u32[]{:S(2)}, u32[]{:S(2)}) collective-permute-start(f32[320,256]{1,0:T(8,128)} %shard_map.103.refs_0_), channel_id=1, source_target_pairs={{0,1},{1,0},{2,3},{3,2},{4,5},{5,4},{6,7},{7,6},{8,9},{9,8},{10,11... | collective-permute-start | bytes 983048 | tf_op jit(solution)/shard_map/ppermute | solution.py:47
  180.4 15.0 %collective-permute-start.38 = (f32[320,256]{1,0:T(8,128)S(1)}, f32[320,256]{1,0:T(8,128)S(1)}, u32[]{:S(2)}, u32[]{:S(2)}) collective-permute-start(f32[320,256]{1,0:T(8,128)S(1)} %collective-permute-done.34.refs_1_), channel_id=1, source_target_pairs={{0,1},{1,0},{2,3},{3,2},{4,5},{5,4},{6,7},{7,6},{8,9},{9,8},{10,11... | collective-permute-start | bytes 983048 | tf_op jit(solution)/shard_map/ppermute | solution.py:47
  183.2 12.2 %collective-permute-start.39 = (f32[320,256]{1,0:T(8,128)S(1)}, f32[320,256]{1,0:T(8,128)S(1)}, u32[]{:S(2)}, u32[]{:S(2)}) collective-permute-start(f32[320,256]{1,0:T(8,128)S(1)} %collective-permute-done.35.refs_2_), channel_id=1, source_target_pairs={{0,1},{1,0},{2,3},{3,2},{4,5},{5,4},{6,7},{7,6},{8,9},{9,8},{10,11... | collective-permute-start | bytes 983048 | tf_op jit(solution)/shard_map/ppermute | solution.py:47
  191.3 14.9 %collective-permute-start.41 = (f32[48,1024]{1,0:T(8,128)}, f32[48,1024]{1,0:T(8,128)S(1)}, u32[]{:S(2)}, u32[]{:S(2)}) collective-permute-start(f32[48,1024]{1,0:T(8,128)} %get-tuple-element.86), channel_id=1, source_target_pairs={{0,128},{1,129},{2,130},{3,131},{4,132},{5,133},{6,134},{7,135},{8... | collective-permute-start | bytes 589832 | tf_op jit(solution)/shard_map/ppermute | solution.py:47
  (56 other events, 476.1 us)

commit v3 on v2

--- a/solution.py
+++ b/solution.py
@@ -15,9 +15,9 @@
 BOTH = ("row", "col")
 F32, BF16 = jnp.float32, jnp.bfloat16
 PAIRS = [(m, j) for j in range(NSUP) for m in range(j)]
-BLOCKS = ([(0, 1), (0, 2), (1, 2), (0, 0), (1, 1)], [(0, 3), (1, 3), (2, 3), (2, 2), (3, 3)])
-FACTORS = ([(0, 5), (4, 2), (5, 2), (0, 4), (1, 5)], [(0, 5), (1, 5), (2, 5), (2, 4), (3, 5)])
-ALL_BLOCKS = BLOCKS[0] + BLOCKS[1]
+BLOCKS = ([(0, 1), (2, 0), (2, 1), (0, 0), (1, 1)], [(0, 3), (1, 3), (2, 3), (2, 2), (3, 3)])
+ALL_BLOCKS = [tuple(sorted(b)) for b in BLOCKS[0] + BLOCKS[1]]
+TURNED = (1, 2)
 VMEM = pl.BlockSpec(memory_space=pltpu.VMEM)
 SMEM = pl.BlockSpec(memory_space=pltpu.SMEM)
 
@@ -141,6 +141,9 @@
 
     lax.fori_loop(0, split, scale, 0)
     lax.fori_loop(split, len(rows), gain, 0)
+    for i in TURNED:
+        where = slice(i * W, (i + 1) * W)
+        out[where, :] = out[where, :].T
 
 
 def put(piece, top, bot, row_of):
@@ -208,42 +211,30 @@
             out[r] = result[pl.ds(pl.multiple_of((r * 4 + xa) * RW, 16), RW), :]
 
 
-def window_blocks(top, bot, core):
-    for first, second in zip(*FACTORS):
-        left, right = [
-            pl.ds(pl.multiple_of(jnp.where(core == 0, first[side], second[side]) * W, W), W) for side in (0, 1)
-        ]
-        yield mul((top[:, left], bot[:, left]), (top[:, right], bot[:, right]), (0, 0))
-
-
-def own_kernel(high, low, ra, rb, distant, cross2, distant2, out, rtop, rbot, top, bot):
+def rows_kernel(ra, rb, distant, cross2, distant2, rtop, rbot):
     at = place()
     quad = ra.shape[0]
-    wide = NSUP * W
     here = pl.ds(pl.multiple_of(at["zh"] * quad, 16), quad)
-    top[here, :wide] = ra[...]
-    bot[here, :wide] = rb[...]
-    put(distant, top.at[:, :wide], bot.at[:, :wide], lambda r: (1 - at["zh"]) * quad + ((at["x"] - r) & 3) * RW)
-    top[:, wide:] = high[...]
-    bot[:, wide:] = low[...]
-    for i, block in enumerate(window_blocks(top, bot, at["c"])):
-        out[i * W : (i + 1) * W, :] = block
-    for side, piece in ((at["zh"], cross2), (1 - at["zh"], distant2)):
-        put(piece, rtop, rbot, lambda r: side * quad + ((at["x"] - r) & 3) * RW)
-
-
-def twin_kernel(own, rtop, rbot, got, base, *refs):
+    rtop[here, :] = ra[...]
+    rbot[here, :] = rb[...]
+    for base, side, piece in ((0, 1 - at["zh"], distant), (2, at["zh"], cross2), (2, 1 - at["zh"], distant2)):
+        put(piece, rtop, rbot, lambda r: (base + side) * quad + ((at["x"] - r) & 3) * RW)
+
+
+def window_kernel(high, low, got, rtop, rbot, base, *refs):
     outs, (top, bot, whole) = refs[:4], refs[4:]
     at = place()
-    wide = NSUP * W
-    top[:, :wide] = rtop[...]
-    bot[:, :wide] = rbot[...]
-    top[:, wide:], bot[:, wide:] = halves(got[...])
+    rows = high.shape[0]
+    top[:rows, :] = high[...]
+    bot[:rows, :] = low[...]
+    top[rows:, :], bot[rows:, :] = halves(got[...])
     lead = (lax.axis_index("row") == 0) & (lax.axis_index("col") < 2)
-    for i, block in enumerate(window_blocks(top, bot, at["c"])):
-        rows = slice(i * W, (i + 1) * W)
-        plus = base[pl.ds(pl.multiple_of(at["c"] * own.shape[0] + i * W, W), W), :]
-        whole[rows, :] = own[rows, :] + block + jnp.where(lead, plus, 0.0)
+    for i, (one, two) in enumerate(zip(*BLOCKS)):
+        pick = lambda a, b: pl.ds(pl.multiple_of(jnp.where(at["c"] == 0, a, b) * W, W), W)
+        left, right = pick(one[0], two[0]), pick(one[1], two[1] - 2)
+        block = mul((rtop[:, left], rbot[:, left]), (top[:, right], bot[:, right]), (0, 0))
+        plus = base[pl.ds(pl.multiple_of(at["c"] * (len(BLOCKS[0]) * W) + i * W, W), W), :]
+        whole[i * W : (i + 1) * W, :] = block + jnp.where(lead, plus, 0.0)
     size = outs[0].shape[0]
     for k, out in enumerate(outs):
         out[...] = whole[pl.ds(pl.multiple_of(((at["y"] + k) & 3) * size, 8), size), :]
@@ -295,6 +286,12 @@
         for k in range(4):
             dst = pl.multiple_of(((at["y"] - k) & 3) * rows, 8)
             whole[pl.ds(dst, rows), :] = pieces[par * 4 + k][...]
+
+        @pl.when(core == 0)
+        def _():
+            for i in TURNED:
+                whole[i * W : (i + 1) * W, :] = whole[i * W : (i + 1) * W, :].T
+
         for i in range(3):
             pair_out[core * 3 + i] = whole[i * W : (i + 1) * W, :]
         for i in range(2):
@@ -400,22 +397,21 @@
     )
 
     got = moved(give, "c", 1)
-    sums, rtop, rbot = kernel(
-        own_kernel,
-        [high, low, ra, rb, distant, cross2, moved(distant, "c", 1)],
-        [(tall // 2, W)] + [((height, width), BF16)] * 2,
-        [((height, width + width // 2), BF16)] * 2,
+    cols = scattered(parts, "x")
+    rtop, rbot = kernel(
+        rows_kernel,
+        [ra, rb, distant, cross2, moved(distant, "c", 1)],
+        [((2 * height, width), BF16)] * 2,
+        flops=1 << 28,
+    )
+    cut = kernel(
+        window_kernel,
+        [high, low, got, rtop, rbot, base],
+        [(tall // 8, W)] * 4,
+        [((2 * height, width // 2), BF16)] * 2 + [((tall // 2, W), F32)],
         flops=1 << 31,
     )
-    cut = kernel(
-        twin_kernel,
-        [sums, rtop, rbot, got, base],
-        [(tall // 8, W)] * 4,
-        [((height, width + width // 2), BF16)] * 2 + [((tall // 2, W), F32)],
-        flops=1 << 31,
-    )
     across = scattered(cut, "y")
-    cols = scattered(parts, "x")
     keep, give = kernel(pick_kernel, cols, [(RW, width)] * 2)
     summed = moved(give, "zh", 1)
     cut = split_sum(across, "x")

time: 209 us -> 214 us (1.024)
  the two profiles are of different devices: /device:TPU:35 before, /device:TPU:33 now
where the time goes in v3:
time: 214 us; the launch traced here: 213 us
  starting transfers between devices  81.1 us (38%)
  waiting for transfers between devices  67.3 us (31%)
  Pallas kernels  52.5 us (25%)
  local copies, waits for them, and re-layouts  10.5 us (5%)
    ppermute x42, starting transfers between devices, sent(): return lax.ppermute(value, BOTH, perm)  81.1 us
    ppermute x42, waiting for transfers between devices, sent(): return lax.ppermute(value, BOTH, perm)  67.3 us
    pallas_call x12, Pallas kernels, kernel(): pl.pallas_call(body, out_shape=jax.ShapeDtypeStruct(out_shapes, F32) if s...  52.5 us
    unnamed x79, local copies, waits for them, and re-layouts  10.5 us
  transfers between devices with their start and end apart: 42, of which 15 were waited for; matrix products, arithmetic and copies ran while one was open for 0% of the time, Pallas kernels for 18%

profile of v3, /device:TPU:33, one launch (start us, length us, event | category | flops | bytes accessed | tf_op | source)
XLA Modules:
  0.0 213.5 jit_solution(5067000280245038697)
XLA Ops:
  0.6 2.9 %shard_map.94 = f32[48,1024]{1,0:T(8,128)} custom-call(s32[4]{0:T(128)} %parent.3, s32[4,48]{1,0:T(4,128)} %pattern.1, f32[4,48,256]{2,1,0:T(8,128)} %factor.1, f32[6,256,256]{2,1,0:T(8,128)} %couple.2), custom_call_target="tpu_custom_call" | custom-call | flops 1048576 | bytes 1770256 | tf_op jit(solution)/shard_map/pallas_call | solution.py:303
  3.5 3.0 %collective-permute-start.1 = (f32[48,1024]{1,0:T(8,128)}, f32[48,1024]{1,0:T(8,128)S(1)}, u32[]{:S(2)}, u32[]{:S(2)}) collective-permute-start(f32[48,1024]{1,0:T(8,128)} %shard_map.94), channel_id=1, source_target_pairs={{0,4},{1,5},{2,6},{3,7},{4,0},{5,1},{6,2},{7,3},{8,12},{9,13},{10,... | collective-permute-start | bytes 589832 | tf_op jit(solution)/shard_map/ppermute | solution.py:47
  13.7 9.2 %shard_map.95.base = f32[2560,256]{1,0:T(8,128)} custom-call(s32[4]{0:T(128)} %parent.3, s32[16,3]{1,0:T(8,128)} %constant.2.clone.table, f32[6,256,256]{2,1,0:T(8,128)} %couple.2, f32[4,256,256]{2,1,0:T(8,128)} %diag_inv.1), custom_call_target="tpu_custom_call" | custom-call | flops 2147483648 | bytes 2621648 | tf_op jit(solution)/shard_map/pallas_call | solution.py:303
  29.4 5.8 %shard_map.96 = (f32[384,1024]{1,0:T(8,128)}, bf16[384,1536]{1,0:T(8,128)(2,1)}, bf16[384,1536]{1,0:T(8,128)(2,1)}, bf16[192,1024]{1,0:T(8,128)(2,1)}, bf16[192,1024]{1,0:T(8,128)(2,1)}) custom-call(f32[384,1536]{1,0:T(8,128)} %bitcast.1, f32[192,1024]{1,0:T(8,128)} %copy-done.5, f32[192,1024]{1,0:T(8,128)} %copy-done.30, f32[192,1024]{1,0:T(8,128)} %copy-done.27), custom_call_target="tpu_custom_call" | custom-call | flops 2147483648 | bytes 4718592 | tf_op jit(solution)/shard_map/pallas_call | solution.py:303
  35.2 10.6 %collective-permute-done.6.left = f32[192,1024]{1,0:T(8,128)S(1)} collective-permute-done((f32[192,1024]{1,0:T(8,128)S(1)}, f32[192,1024]{1,0:T(8,128)S(1)}, u32[]{:S(2)}, u32[]{:S(2)}) %collective-permute-start.6) | collective-permute-done | bytes 786464 | tf_op jit(solution)/shard_map/ppermute | solution.py:47
  49.7 13.3 %collective-permute-start.19 = (f32[192,1024]{1,0:T(8,128)S(1)}, f32[192,1024]{1,0:T(8,128)S(1)}, u32[]{:S(2)}, u32[]{:S(2)}) collective-permute-start(f32[192,1024]{1,0:T(8,128)S(1)} %copy-done.28), channel_id=1, source_target_pairs={{0,128},{1,129},{2,130},{3,131},{4,132},{5,133},{6,134},{7,135},{8... | collective-permute-start | bytes 2359304 | tf_op jit(solution)/shard_map/ppermute | solution.py:47
  64.2 6.7 %shard_map.97.refs_0_ = f32[384,1024]{1,0:T(8,128)} custom-call(f32[384,1024]{1,0:T(8,128)} %get-tuple-element.54.start, bf16[384,1536]{1,0:T(8,128)(2,1)} %get-tuple-element.55.ltop.refs_1_, bf16[384,1536]{1,0:T(8,128)(2,1)} %get-tuple-element.56.lbot.refs_2_, f32[192,1024]{1,0:T(8,128)} %copy-done, f32[192,1024]{1,0:T(8,128)} %copy-done.1, ...), custom_call_target="tpu_custom_call" | custom-call | flops 2147483648 | bytes 9437184 | tf_op jit(solution)/shard_map/pallas_call | solution.py:303
  72.7 20.6 %collective-permute-done.19.distant = f32[192,1024]{1,0:T(8,128)S(1)} collective-permute-done((f32[192,1024]{1,0:T(8,128)S(1)}, f32[192,1024]{1,0:T(8,128)S(1)}, u32[]{:S(2)}, u32[]{:S(2)}) %collective-permute-start.19) | collective-permute-done | bytes 786464 | tf_op jit(solution)/shard_map/ppermute | solution.py:47
  95.4 6.1 %shard_map.98 = (f32[2,48,1024]{2,1,0:T(8,128)}, f32[2,48,1024]{2,1,0:T(8,128)}, f32[2,48,1024]{2,1,0:T(8,128)}, f32[2,48,1024]{2,1,0:T(8,128)}, bf16[384,512]{1...) custom-call(f32[384,1024]{1,0:T(8,128)} %shard_map.97.refs_0_, ...), custom_call_target="tpu_custom_call" | custom-call | flops 2147483648 | bytes 7864320 | tf_op jit(solution)/shard_map/pallas_call | solution.py:303
  102.8 4.0 %shard_map.100 = (bf16[768,1024]{1,0:T(8,128)(2,1)}, bf16[768,1024]{1,0:T(8,128)(2,1)}) custom-call(bf16[192,1024]{1,0:T(8,128)(2,1)} %get-tuple-element.68.ra, bf16[192,1024]{1,0:T(8,128)(2,1)} %get-tuple-element.69.rb, f32[192,1024]{1,0:T(8,128)} %copy-done.6, f32[192,1024]{1,0:T(8,128)} %copy-done.7, f32[192,1024]{1,0:T(8,128)} %copy-done.8), custom_call_target="tpu_custom_call" | custom-call | flops 268435456 | bytes 3932160 | tf_op jit(solution)/shard_map/pallas_call | solution.py:303
  107.6 6.4 %shard_map.101 = (f32[320,256]{1,0:T(8,128)}, f32[320,256]{1,0:T(8,128)}, f32[320,256]{1,0:T(8,128)}, f32[320,256]{1,0:T(8,128)}) custom-call(bf16[384,512]{1,0:T(8,128)(2,1)} %get-tuple-element.65.high, bf16[384,512]{1,0:T(8,128)(2,1)} %get-tuple-element.66.low, f32[384,512]{1,0:T(8,128)} %copy-done.29, bf16[768,1024]{1,0:T(8,128)(2,1)} %get-tuple-element.70.rtop, ...), custom_call_target="tpu_custom_call" | custom-call | flops 2147483648 | bytes 11272192 | tf_op jit(solution)/shard_map/pallas_call | solution.py:303
  117.4 7.1 %collective-permute-done.22.refs_1_ = f32[320,256]{1,0:T(8,128)S(1)} collective-permute-done((f32[320,256]{1,0:T(8,128)}, f32[320,256]{1,0:T(8,128)S(1)}, u32[]{:S(2)}, u32[]{:S(2)}) %collective-permute-start.22) | collective-permute-done | bytes 327712 | tf_op jit(solution)/shard_map/ppermute | solution.py:47
  124.6 6.7 %collective-permute-done.23.refs_2_ = f32[320,256]{1,0:T(8,128)S(1)} collective-permute-done((f32[320,256]{1,0:T(8,128)}, f32[320,256]{1,0:T(8,128)S(1)}, u32[]{:S(2)}, u32[]{:S(2)}) %collective-permute-start.23) | collective-permute-done | bytes 327712 | tf_op jit(solution)/shard_map/ppermute | solution.py:47
  142.4 3.1 %collective-permute-done.28 = f32[80,256]{1,0:T(8,128)S(1)} collective-permute-done((f32[80,256]{1,0:T(8,128)S(1)}, f32[80,256]{1,0:T(8,128)S(1)}, u32[]{:S(2)}, u32[]{:S(2)}) %collective-permute-start.28) | collective-permute-done | bytes 81952 | tf_op jit(solution)/shard_map/ppermute | solution.py:47
  145.7 4.5 %collective-permute-done.29 = f32[80,256]{1,0:T(8,128)S(1)} collective-permute-done((f32[80,256]{1,0:T(8,128)S(1)}, f32[80,256]{1,0:T(8,128)S(1)}, u32[]{:S(2)}, u32[]{:S(2)}) %collective-permute-start.29) | collective-permute-done | bytes 81952 | tf_op jit(solution)/shard_map/ppermute | solution.py:47
  150.2 4.5 %collective-permute-start.30 = (f32[80,256]{1,0:T(8,128)S(1)}, f32[80,256]{1,0:T(8,128)S(1)}, u32[]{:S(2)}, u32[]{:S(2)}) collective-permute-start(f32[80,256]{1,0:T(8,128)S(1)} %add.22), channel_id=1, source_target_pairs={{0,128},{1,129},{2,130},{3,131},{4,132},{5,133},{6,134},{7,135},{8... | collective-permute-start | bytes 245768 | tf_op jit(solution)/shard_map/ppermute | solution.py:47
  154.7 4.2 %collective-permute-done.30 = f32[80,256]{1,0:T(8,128)S(1)} collective-permute-done((f32[80,256]{1,0:T(8,128)S(1)}, f32[80,256]{1,0:T(8,128)S(1)}, u32[]{:S(2)}, u32[]{:S(2)}) %collective-permute-start.30) | collective-permute-done | bytes 81952 | tf_op jit(solution)/shard_map/ppermute | solution.py:47
  170.1 2.9 %collective-permute-start.35 = (f32[320,256]{1,0:T(8,128)}, f32[320,256]{1,0:T(8,128)S(1)}, u32[]{:S(2)}, u32[]{:S(2)}) collective-permute-start(f32[320,256]{1,0:T(8,128)} %shard_map.103.refs_0_), channel_id=1, source_target_pairs={{0,16},{1,17},{2,18},{3,19},{4,20},{5,21},{6,22},{7,23},{8,24},{9,... | collective-permute-start | bytes 983048 | tf_op jit(solution)/shard_map/ppermute | solution.py:47
  175.3 11.0 %collective-permute-start.37 = (f32[320,256]{1,0:T(8,128)}, f32[320,256]{1,0:T(8,128)S(1)}, u32[]{:S(2)}, u32[]{:S(2)}) collective-permute-start(f32[320,256]{1,0:T(8,128)} %shard_map.103.refs_0_), channel_id=1, source_target_pairs={{0,1},{1,0},{2,3},{3,2},{4,5},{5,4},{6,7},{7,6},{8,9},{9,8},{10,11... | collective-permute-start | bytes 983048 | tf_op jit(solution)/shard_map/ppermute | solution.py:47
  186.3 3.6 %collective-permute-start.38 = (f32[320,256]{1,0:T(8,128)S(1)}, f32[320,256]{1,0:T(8,128)S(1)}, u32[]{:S(2)}, u32[]{:S(2)}) collective-permute-start(f32[320,256]{1,0:T(8,128)S(1)} %collective-permute-done.34.refs_1_), channel_id=1, source_target_pairs={{0,1},{1,0},{2,3},{3,2},{4,5},{5,4},{6,7},{7,6},{8,9},{9,8},{10,11... | collective-permute-start | bytes 983048 | tf_op jit(solution)/shard_map/ppermute | solution.py:47
  189.9 5.0 %collective-permute-start.39 = (f32[320,256]{1,0:T(8,128)S(1)}, f32[320,256]{1,0:T(8,128)S(1)}, u32[]{:S(2)}, u32[]{:S(2)}) collective-permute-start(f32[320,256]{1,0:T(8,128)S(1)} %collective-permute-done.35.refs_2_), channel_id=1, source_target_pairs={{0,1},{1,0},{2,3},{3,2},{4,5},{5,4},{6,7},{7,6},{8,9},{9,8},{10,11... | collective-permute-start | bytes 983048 | tf_op jit(solution)/shard_map/ppermute | solution.py:47
  197.9 4.1 %collective-permute-start.41 = (f32[48,1024]{1,0:T(8,128)}, f32[48,1024]{1,0:T(8,128)S(1)}, u32[]{:S(2)}, u32[]{:S(2)}) collective-permute-start(f32[48,1024]{1,0:T(8,128)} %get-tuple-element.84), channel_id=1, source_target_pairs={{0,128},{1,129},{2,130},{3,131},{4,132},{5,133},{6,134},{7,135},{8... | collective-permute-start | bytes 589832 | tf_op jit(solution)/shard_map/ppermute | solution.py:47
  203.7 3.9 %shard_map.104 = (f32[6,256,256]{2,1,0:T(8,128)}, f32[4,256,256]{2,1,0:T(8,128)}) custom-call(f32[320,256]{1,0:T(8,128)} %shard_map.103.refs_0_, f32[320,256]{1,0:T(8,128)} %copy-done.12, f32[320,256]{1,0:T(8,128)} %copy-done.13, f32[320,256]{1,0:T(8,128)} %copy-done.14, f32[320,256]{1,0:T(8,128)} %copy-done.15, f32[320,256]{1,0:T(8,128)} %copy-done.16, ...), custom_call_target="tpu_custom_call" | custom-call | bytes 2621440 | tf_op jit(solution)/shard_map/pallas_call | solution.py:303
  207.6 3.5 %collective-permute-done.41.got = f32[48,1024]{1,0:T(8,128)S(1)} collective-permute-done((f32[48,1024]{1,0:T(8,128)}, f32[48,1024]{1,0:T(8,128)S(1)}, u32[]{:S(2)}, u32[]{:S(2)}) %collective-permute-start.41) | collective-permute-done | bytes 196640 | tf_op jit(solution)/shard_map/ppermute | solution.py:47
  (159 shorter events, 59.8 us)
Async XLA Ops:
  3.5 19.4 %collective-permute-start.1 = (f32[48,1024]{1,0:T(8,128)}, f32[48,1024]{1,0:T(8,128)S(1)}, u32[]{:S(2)}, u32[]{:S(2)}) collective-permute-start(f32[48,1024]{1,0:T(8,128)} %shard_map.94), channel_id=1, source_target_pairs={{0,4},{1,5},{2,6},{3,7},{4,0},{5,1},{6,2},{7,3},{8,12},{9,13},{10,... | collective-permute-start | bytes 589832 | tf_op jit(solution)/shard_map/ppermute | solution.py:47
  6.5 16.7 %collective-permute-start = (f32[48,1024]{1,0:T(8,128)}, f32[48,1024]{1,0:T(8,128)S(1)}, u32[]{:S(2)}, u32[]{:S(2)}) collective-permute-start(f32[48,1024]{1,0:T(8,128)} %shard_map.94), channel_id=1, source_target_pairs={{0,2},{1,3},{2,4},{3,5},{4,6},{5,7},{6,0},{7,1},{8,10},{9,11},{10,... | collective-permute-start | bytes 589832 | tf_op jit(solution)/shard_map/ppermute | solution.py:47
  8.8 14.5 %collective-permute-start.3 = (f32[48,1024]{1,0:T(8,128)}, f32[48,1024]{1,0:T(8,128)S(1)}, u32[]{:S(2)}, u32[]{:S(2)}) collective-permute-start(f32[48,1024]{1,0:T(8,128)} %shard_map.94), channel_id=1, source_target_pairs={{0,32},{1,33},{2,34},{3,35},{4,36},{5,37},{6,38},{7,39},{8,40},{9,... | collective-permute-start | bytes 589832 | tf_op jit(solution)/shard_map/ppermute | solution.py:47
  10.1 13.3 %collective-permute-start.4 = (f32[48,1024]{1,0:T(8,128)}, f32[48,1024]{1,0:T(8,128)S(1)}, u32[]{:S(2)}, u32[]{:S(2)}) collective-permute-start(f32[48,1024]{1,0:T(8,128)} %shard_map.94), channel_id=1, source_target_pairs={{0,64},{1,65},{2,66},{3,67},{4,68},{5,69},{6,70},{7,71},{8,72},{9,... | collective-permute-start | bytes 589832 | tf_op jit(solution)/shard_map/ppermute | solution.py:47
  25.4 20.3 %collective-permute-start.6 = (f32[192,1024]{1,0:T(8,128)S(1)}, f32[192,1024]{1,0:T(8,128)S(1)}, u32[]{:S(2)}, u32[]{:S(2)}) collective-permute-start(f32[192,1024]{1,0:T(8,128)S(1)} %pad_maximum_fusion.near), channel_id=1, source_target_pairs={{0,8},{1,9},{2,10},{3,11},{4,12},{5,13},{6,14},{7,15},{8,16},{9,17... | collective-permute-start | bytes 2359304 | tf_op jit(solution)/shard_map/ppermute | solution.py:47
  26.7 19.0 %collective-permute-start.7 = (f32[192,1024]{1,0:T(8,128)S(1)}, f32[192,1024]{1,0:T(8,128)S(1)}, u32[]{:S(2)}, u32[]{:S(2)}) collective-permute-start(f32[192,1024]{1,0:T(8,128)S(1)} %pad_maximum_fusion.near), channel_id=1, source_target_pairs={{0,24},{1,25},{2,26},{3,27},{4,28},{5,29},{6,30},{7,31},{8,0},{9,1... | collective-permute-start | bytes 2359304 | tf_op jit(solution)/shard_map/ppermute | solution.py:47
  45.8 17.2 %collective-permute-start.11 = (f32[192,1024]{1,0:T(8,128)S(1)}, f32[192,1024]{1,0:T(8,128)S(1)}, u32[]{:S(2)}, u32[]{:S(2)}) collective-permute-start(f32[192,1024]{1,0:T(8,128)S(1)} %collective-permute-done.6.left), channel_id=1, source_target_pairs={{0,1},{1,0},{2,3},{3,2},{4,5},{5,4},{6,7},{7,6},{8,9},{9,8},{10,11... | collective-permute-start | bytes 2359304 | tf_op jit(solution)/shard_map/ppermute | solution.py:47
  46.7 16.3 %collective-permute-start.12 = (f32[192,1024]{1,0:T(8,128)S(1)}, f32[192,1024]{1,0:T(8,128)S(1)}, u32[]{:S(2)}, u32[]{:S(2)}) collective-permute-start(f32[192,1024]{1,0:T(8,128)S(1)} %collective-permute-done.7.right), channel_id=1, source_target_pairs={{0,1},{1,0},{2,3},{3,2},{4,5},{5,4},{6,7},{7,6},{8,9},{9,8},{10,11... | collective-permute-start | bytes 2359304 | tf_op jit(solution)/shard_map/ppermute | solution.py:47
  46.9 24.0 %collective-permute-start.9 = (f32[96,1024]{1,0:T(8,128)S(1)}, f32[96,1024]{1,0:T(8,128)S(1)}, u32[]{:S(2)}, u32[]{:S(2)}) collective-permute-start(f32[96,1024]{1,0:T(8,128)S(1)} %slice.6), channel_id=1, source_target_pairs={{0,8},{1,9},{2,10},{3,11},{4,12},{5,13},{6,14},{7,15},{8,16},{9,17... | collective-permute-start | bytes 1179656 | tf_op jit(solution)/shard_map/ppermute | solution.py:47
  48.1 22.7 %collective-permute-start.10 = (f32[96,1024]{1,0:T(8,128)S(1)}, f32[96,1024]{1,0:T(8,128)S(1)}, u32[]{:S(2)}, u32[]{:S(2)}) collective-permute-start(f32[96,1024]{1,0:T(8,128)S(1)} %slice.7), channel_id=1, source_target_pairs={{0,24},{1,25},{2,26},{3,27},{4,28},{5,29},{6,30},{7,31},{8,0},{9,1... | collective-permute-start | bytes 1179656 | tf_op jit(solution)/shard_map/ppermute | solution.py:47
  49.7 43.7 %collective-permute-start.19 = (f32[192,1024]{1,0:T(8,128)S(1)}, f32[192,1024]{1,0:T(8,128)S(1)}, u32[]{:S(2)}, u32[]{:S(2)}) collective-permute-start(f32[192,1024]{1,0:T(8,128)S(1)} %copy-done.28), channel_id=1, source_target_pairs={{0,128},{1,129},{2,130},{3,131},{4,132},{5,133},{6,134},{7,135},{8... | collective-permute-start | bytes 2359304 | tf_op jit(solution)/shard_map/ppermute | solution.py:47
  70.9 23.0 %collective-permute-start.13 = (f32[96,1024]{1,0:T(8,128)S(1)}, f32[96,1024]{1,0:T(8,128)S(1)}, u32[]{:S(2)}, u32[]{:S(2)}) collective-permute-start(f32[96,1024]{1,0:T(8,128)S(1)} %collective-permute-done.9.refs_3_), channel_id=1, source_target_pairs={{0,1},{1,0},{2,3},{3,2},{4,5},{5,4},{6,7},{7,6},{8,9},{9,8},{10,11... | collective-permute-start | bytes 1179656 | tf_op jit(solution)/shard_map/ppermute | solution.py:47
  72.2 21.7 %collective-permute-start.14 = (f32[96,1024]{1,0:T(8,128)S(1)}, f32[96,1024]{1,0:T(8,128)S(1)}, u32[]{:S(2)}, u32[]{:S(2)}) collective-permute-start(f32[96,1024]{1,0:T(8,128)S(1)} %collective-permute-done.10.refs_4_), channel_id=1, source_target_pairs={{0,1},{1,0},{2,3},{3,2},{4,5},{5,4},{6,7},{7,6},{8,9},{9,8},{10,11... | collective-permute-start | bytes 1179656 | tf_op jit(solution)/shard_map/ppermute | solution.py:47
  72.3 29.3 %collective-permute-start.20 = (f32[192,1024]{1,0:T(8,128)S(1)}, f32[192,1024]{1,0:T(8,128)S(1)}, u32[]{:S(2)}, u32[]{:S(2)}) collective-permute-start(f32[192,1024]{1,0:T(8,128)S(1)} %copy-done.28), channel_id=1, source_target_pairs={{0,1},{1,0},{2,3},{3,2},{4,5},{5,4},{6,7},{7,6},{8,9},{9,8},{10,11... | collective-permute-start | bytes 2359304 | tf_op jit(solution)/shard_map/ppermute | solution.py:47
  114.1 17.1 %collective-permute-start.23 = (f32[320,256]{1,0:T(8,128)}, f32[320,256]{1,0:T(8,128)S(1)}, u32[]{:S(2)}, u32[]{:S(2)}) collective-permute-start(f32[320,256]{1,0:T(8,128)} %get-tuple-element.75), channel_id=1, source_target_pairs={{0,16},{1,17},{2,18},{3,19},{4,20},{5,21},{6,22},{7,23},{8,24},{9,... | collective-permute-start | bytes 983048 | tf_op jit(solution)/shard_map/ppermute | solution.py:47
  116.6 15.3 %collective-permute-start.24 = (f32[320,256]{1,0:T(8,128)}, f32[320,256]{1,0:T(8,128)S(1)}, u32[]{:S(2)}, u32[]{:S(2)}) collective-permute-start(f32[320,256]{1,0:T(8,128)} %get-tuple-element.76), channel_id=1, source_target_pairs={{0,24},{1,25},{2,26},{3,27},{4,28},{5,29},{6,30},{7,31},{8,0},{9,1... | collective-permute-start | bytes 983048 | tf_op jit(solution)/shard_map/ppermute | solution.py:47
  142.3 30.7 %collective-permute-start.15 = (f32[2,48,1024]{2,1,0:T(8,128)S(1)}, f32[2,48,1024]{2,1,0:T(8,128)S(1)}, u32[]{:S(2)}, u32[]{:S(2)}) collective-permute-start(f32[2,48,1024]{2,1,0:T(8,128)S(1)} %copy-done.33), channel_id=1, source_target_pairs={{0,32},{1,33},{2,34},{3,35},{4,36},{5,37},{6,38},{7,39},{8,40},{9,... | collective-permute-start | bytes 1179656 | tf_op jit(solution)/shard_map/ppermute | solution.py:47
  161.7 13.5 %collective-permute-start.16 = (f32[2,48,1024]{2,1,0:T(8,128)S(1)}, f32[2,48,1024]{2,1,0:T(8,128)S(1)}, u32[]{:S(2)}, u32[]{:S(2)}) collective-permute-start(f32[2,48,1024]{2,1,0:T(8,128)S(1)} %copy-done.32), channel_id=1, source_target_pairs={{0,64},{1,65},{2,66},{3,67},{4,68},{5,69},{6,70},{7,71},{8,72},{9,... | collective-permute-start | bytes 1179656 | tf_op jit(solution)/shard_map/ppermute | solution.py:47
  167.5 18.8 %collective-permute-start.34 = (f32[320,256]{1,0:T(8,128)}, f32[320,256]{1,0:T(8,128)S(1)}, u32[]{:S(2)}, u32[]{:S(2)}) collective-permute-start(f32[320,256]{1,0:T(8,128)} %shard_map.103.refs_0_), channel_id=1, source_target_pairs={{0,8},{1,9},{2,10},{3,11},{4,12},{5,13},{6,14},{7,15},{8,16},{9,17... | collective-permute-start | bytes 983048 | tf_op jit(solution)/shard_map/ppermute | solution.py:47
  170.1 19.8 %collective-permute-start.35 = (f32[320,256]{1,0:T(8,128)}, f32[320,256]{1,0:T(8,128)S(1)}, u32[]{:S(2)}, u32[]{:S(2)}) collective-permute-start(f32[320,256]{1,0:T(8,128)} %shard_map.103.refs_0_), channel_id=1, source_target_pairs={{0,16},{1,17},{2,18},{3,19},{4,20},{5,21},{6,22},{7,23},{8,24},{9,... | collective-permute-start | bytes 983048 | tf_op jit(solution)/shard_map/ppermute | solution.py:47
  173.0 21.9 %collective-permute-start.36 = (f32[320,256]{1,0:T(8,128)}, f32[320,256]{1,0:T(8,128)S(1)}, u32[]{:S(2)}, u32[]{:S(2)}) collective-permute-start(f32[320,256]{1,0:T(8,128)} %shard_map.103.refs_0_), channel_id=1, source_target_pairs={{0,24},{1,25},{2,26},{3,27},{4,28},{5,29},{6,30},{7,31},{8,0},{9,1... | collective-permute-start | bytes 983048 | tf_op jit(solution)/shard_map/ppermute | solution.py:47
  173.0 21.9 %collective-permute-start.17 = (f32[2,48,1024]{2,1,0:T(8,128)S(1)}, f32[2,48,1024]{2,1,0:T(8,128)S(1)}, u32[]{:S(2)}, u32[]{:S(2)}) collective-permute-start(f32[2,48,1024]{2,1,0:T(8,128)S(1)} %copy-done.31), channel_id=1, source_target_pairs={{0,96},{1,97},{2,98},{3,99},{4,100},{5,101},{6,102},{7,103},{8,104... | collective-permute-start | bytes 1179656 | tf_op jit(solution)/shard_map/ppermute | solution.py:47
  175.3 26.7 %collective-permute-start.37 = (f32[320,256]{1,0:T(8,128)}, f32[320,256]{1,0:T(8,128)S(1)}, u32[]{:S(2)}, u32[]{:S(2)}) collective-permute-start(f32[320,256]{1,0:T(8,128)} %shard_map.103.refs_0_), channel_id=1, source_target_pairs={{0,1},{1,0},{2,3},{3,2},{4,5},{5,4},{6,7},{7,6},{8,9},{9,8},{10,11... | collective-permute-start | bytes 983048 | tf_op jit(solution)/shard_map/ppermute | solution.py:47
  186.3 15.7 %collective-permute-start.38 = (f32[320,256]{1,0:T(8,128)S(1)}, f32[320,256]{1,0:T(8,128)S(1)}, u32[]{:S(2)}, u32[]{:S(2)}) collective-permute-start(f32[320,256]{1,0:T(8,128)S(1)} %collective-permute-done.34.refs_1_), channel_id=1, source_target_pairs={{0,1},{1,0},{2,3},{3,2},{4,5},{5,4},{6,7},{7,6},{8,9},{9,8},{10,11... | collective-permute-start | bytes 983048 | tf_op jit(solution)/shard_map/ppermute | solution.py:47
  (56 other events, 496.7 us)

commit v4 on v1

--- a/solution.py
+++ b/solution.py
@@ -126,11 +126,12 @@
             out[rows, :] = out[rows, :] + mul(kept(ihigh, ilow, at(q, m)), kept(shigh, slow, at(q, j)), (0, 0))
 
 
-def put(piece, top, bot, row_of):
+def put(piece, top, bot, row_of, weight=None):
     def step(r, carry):
         src = pl.multiple_of(r * RW, 16)
         dst = pl.multiple_of(row_of(r), 16)
-        hi, lo = halves(piece[pl.ds(src, RW), :])
+        value = piece[pl.ds(src, RW), :]
+        hi, lo = halves(value if weight is None else value * weight(r))
         top[pl.ds(dst, RW), :] = hi
         bot[pl.ds(dst, RW), :] = lo
         return carry
@@ -152,7 +153,7 @@
             return carry
 
         lax.fori_loop(0, local.shape[0] // RW, step, 0)
-    put(cross, rtop, rbot, lambda r: ((at["x"] - r) & 3) * RW)
+    put(cross, rtop, rbot, lambda r: r * RW, lambda r: jnp.where(r == 1, 1.0, 0.5).astype(F32))
     for par, piece in enumerate((near, twin)):
         core = at["c"] ^ par
         put(piece, top, bot, lambda r: (((at["zl"] - r) & 3) * 2 + core) * RW)
@@ -181,16 +182,18 @@
         core = at["c"] ^ (i // 2)
         start = 2 * (i % 2)
         put(piece, top, bot, lambda r: (((at["zl"] - r - start) & 3) * 2 + core) * RW)
-    here = pl.ds(pl.multiple_of(at["zh"] * quad, 16), quad)
-    rtop[here, :] = ra[...]
-    rbot[here, :] = rb[...]
-    put(distant, rtop, rbot, lambda r: (1 - at["zh"]) * quad + ((at["x"] - r) & 3) * RW)
+    rtop[:quad, :] = ra[...]
+    rbot[:quad, :] = rb[...]
+    put(distant, rtop, rbot, lambda r: quad + r * RW)
     cols = slice(3 * span, 4 * span)
     value = early[...] + mul((ltop[:, cols], lbot[:, cols]), (top[...], bot[...]))
     result[...] = value
-    hi, lo = halves(value)
-    ptop[...] = hi
-    pbot[...] = lo
+    taken = [at["zh"] * 4 + ((at["x"] + k) & 3) for k in range(3)]
+    taken += [(1 - at["zh"]) * 4 + ((at["x"] + k + at["zh"]) & 3) for k in range(2)]
+    for i, block in enumerate(taken):
+        hi, lo = halves(result[pl.ds(pl.multiple_of(block * RW, 16), RW), :])
+        ptop[i * RW : (i + 1) * RW, :] = hi
+        pbot[i * RW : (i + 1) * RW, :] = lo
     for k, out in enumerate(outs):
         xa = (at["x"] + k) & 3
         for r in range(2):
@@ -200,6 +203,7 @@
     for i, (m, j) in enumerate(order):
         one, two = slice(m * W, (m + 1) * W), slice(j * W, (j + 1) * W)
         block = mul((rtop[:, one], rbot[:, one]), (ptop[:, two], pbot[:, two]), (0, 0))
+        block = block + mul((ptop[:, one], pbot[:, one]), (rtop[:, two], rbot[:, two]), (0, 0))
         rows = slice(i * W, (i + 1) * W)
         block = block + jnp.where(lead, base[rows, :], 0.0)
         first, second = block[:, :HALF], block[:, HALF:]
@@ -308,6 +312,7 @@
 
 
 def shards(inv_anc, factor_cols, couple, diag_inv, pattern, parent):
+    at = place()
     local = inv_anc.reshape(-1, inv_anc.shape[3])
     height = local.shape[0]
 
@@ -319,7 +324,7 @@
     span = local.shape[1] // 4
 
     near = gathered(own, "zl")
-    cross = gathered(own, "x")
+    cross = [own, moved(own, "x", 3), moved(own, "x", 2)]
     _, couple_later = tie(own, couple)
     base = kernel(
         functools.partial(base_kernel, ALL_BLOCKS),
@@ -330,11 +335,11 @@
         flops=1 << 31,
     )
     near = jnp.concatenate(near, axis=0)
-    near, base, *cross = tie(near, base, *cross)
+    near, base = tie(near, base)
     cross = jnp.concatenate(cross, axis=0)
 
     left, right = moved(near, "y", 1), moved(near, "y", 3)
-    distant = moved(cross, "zh", 1)
+    distant = moved(lax.dynamic_slice_in_dim(cross, (1 - at["zh"]) * RW, 2 * RW, 0), "zh", 1)
     start, ltop, lbot, ra, rb = kernel(
         near_kernel,
         [local, near, moved(near, "c", 1), cross],
@@ -359,9 +364,9 @@
         + [far_a, far_b, moved(far_a, "c", 1), moved(far_b, "c", 1)],
         [(2, RW, width)] * 4 + [(tall, HALF)] * 2,
         [((span, width), BF16)] * 2
-        + [((height, width), BF16)] * 2
+        + [((5 * RW, width), BF16)] * 2
         + [((height, width), F32)]
-        + [((height, width), BF16)] * 2,
+        + [((5 * RW, width), BF16)] * 2,
         flops=1 << 32,
     )
 
@@ -373,19 +378,20 @@
     summed = moved(give, "zh", 1)
     cut = split_sum(across, "x")
     total = total_of(scattered(cut, "x"))
-    total, summed = tie(total, summed)
     total = total + sent(total, "zl", lambda a: a ^ 1)
     total = total + sent(total, "zl", lambda a: a ^ 2)
     total = total + moved(total, "zh", 1)
     lines = gathered(total, "x")
     total = kernel(functools.partial(join_kernel, "x"), lines, (4 * total.shape[0], HALF))
     lanes = gathered(total, "y")
+    twins = [moved(v, "c", 1) for v in lanes]
     pair_blocks, diagonal = kernel(
         functools.partial(final_kernel, [ALL_BLOCKS]),
-        lanes + [moved(v, "c", 1) for v in lanes],
+        lanes + twins,
         [(len(PAIRS), W, W), (NSUP, W, W)],
         [((tall, W), F32)],
     )
+    keep, pair_blocks, diagonal = tie(keep, pair_blocks, diagonal)
     columns = kernel(columns_kernel, [keep, summed], (NSUP, RW, W))
     return (columns, pair_blocks, diagonal)
 

time: 209 us -> 196 us (0.938)
  the two profiles are of different devices: /device:TPU:97 before, /device:TPU:39 now
where the time goes in v4:
time: 196 us; the launch traced here: 195 us
  starting transfers between devices  74.8 us (38%)
  waiting for transfers between devices  64 us (33%)
  Pallas kernels  44.3 us (23%)
  local copies, waits for them, and re-layouts  9.3 us (5%)
    ppermute x39, starting transfers between devices, sent(): return lax.ppermute(value, BOTH, perm)  74.8 us
    ppermute x39, waiting for transfers between devices, sent(): return lax.ppermute(value, BOTH, perm)  64 us
    pallas_call x11, Pallas kernels, kernel(): pl.pallas_call(body, out_shape=jax.ShapeDtypeStruct(out_shapes, F32) if s...  44.3 us
    unnamed x64, local copies, waits for them, and re-layouts  8.46 us
  transfers between devices with their start and end apart: 39, of which 17 were waited for; matrix products, arithmetic and copies ran while one was open for 1% of the time, Pallas kernels for 13%

profile of v4, /device:TPU:39, one launch (start us, length us, event | category | flops | bytes accessed | tf_op | source)
XLA Modules:
  0.0 195.2 jit_solution(15362771010163427216)
XLA Ops:
  3.5 3.0 %collective-permute-start.1 = (f32[48,1024]{1,0:T(8,128)}, f32[48,1024]{1,0:T(8,128)S(1)}, u32[]{:S(2)}, u32[]{:S(2)}) collective-permute-start(f32[48,1024]{1,0:T(8,128)} %shard_map.85), channel_id=1, source_target_pairs={{0,4},{1,5},{2,6},{3,7},{4,0},{5,1},{6,2},{7,3},{8,12},{9,13},{10,... | collective-permute-start | bytes 589832 | tf_op jit(solution)/shard_map/ppermute | solution.py:46
  8.8 5.7 %shard_map.86.refs_1_ = f32[2560,256]{1,0:T(8,128)} custom-call(s32[4]{0:T(128)} %parent.3, f32[6,256,256]{2,1,0:T(8,128)} %couple.2, f32[4,256,256]{2,1,0:T(8,128)} %diag_inv.1), custom_call_target="tpu_custom_call" | custom-call | flops 2147483648 | bytes 2621456 | tf_op jit(solution)/shard_map/pallas_call | solution.py:274
  14.6 4.4 %collective-permute-done.1 = f32[48,1024]{1,0:T(8,128)S(1)} collective-permute-done((f32[48,1024]{1,0:T(8,128)}, f32[48,1024]{1,0:T(8,128)S(1)}, u32[]{:S(2)}, u32[]{:S(2)}) %collective-permute-start.1) | collective-permute-done | bytes 196640 | tf_op jit(solution)/shard_map/ppermute | solution.py:46
  19.0 4.2 %collective-permute-done = f32[48,1024]{1,0:T(8,128)S(1)} collective-permute-done((f32[48,1024]{1,0:T(8,128)}, f32[48,1024]{1,0:T(8,128)S(1)}, u32[]{:S(2)}, u32[]{:S(2)}) %collective-permute-start) | collective-permute-done | bytes 196640 | tf_op jit(solution)/shard_map/ppermute | solution.py:46
  28.6 6.5 %collective-permute-done.7 = f32[48,1024]{1,0:T(8,128)S(1)} collective-permute-done((f32[48,1024]{1,0:T(8,128)S(1)}, f32[48,1024]{1,0:T(8,128)S(1)}, u32[]{:S(2)}, u32[]{:S(2)}) %collective-permute-start.7) | collective-permute-done | bytes 196640 | tf_op jit(solution)/shard_map/ppermute | solution.py:46
  35.1 4.9 %collective-permute-done.6 = f32[48,1024]{1,0:T(8,128)S(1)} collective-permute-done((f32[48,1024]{1,0:T(8,128)S(1)}, f32[48,1024]{1,0:T(8,128)S(1)}, u32[]{:S(2)}, u32[]{:S(2)}) %collective-permute-start.6) | collective-permute-done | bytes 196640 | tf_op jit(solution)/shard_map/ppermute | solution.py:46
  41.8 5.7 %shard_map.87 = (f32[384,1024]{1,0:T(8,128)}, bf16[384,1536]{1,0:T(8,128)(2,1)}, bf16[384,1536]{1,0:T(8,128)(2,1)}, bf16[144,1024]{1,0:T(8,128)(2,1)}, bf16[144,1024]{1,0:T(8,128)(2,1)}) custom-call(f32[384,1536]{1,0:T(8,128)} %bitcast.1, f32[192,1024]{1,0:T(8,128)} %copy-done.6, f32[192,1024]{1,0:T(8,128)} %copy-done.25, f32[144,1024]{1,0:T(8,128)} %pad_maximum_fusion.1.cross), custom_call_target="tpu_custom_call" | custom-call | flops 2147483648 | bytes 4521984 | tf_op jit(solution)/shard_map/pallas_call | solution.py:274
  51.8 5.2 %collective-permute-start.12 = (f32[96,1024]{1,0:T(8,128)S(1)}, f32[96,1024]{1,0:T(8,128)S(1)}, u32[]{:S(2)}, u32[]{:S(2)}) collective-permute-start(f32[96,1024]{1,0:T(8,128)S(1)} %constant_dynamic-slice_fusion), channel_id=1, source_target_pairs={{0,128},{1,129},{2,130},{3,131},{4,132},{5,133},{6,134},{7,135},{8... | collective-permute-start | bytes 1179656 | tf_op jit(solution)/shard_map/ppermute | solution.py:46
  57.9 6.7 %shard_map.88.refs_0_ = f32[384,1024]{1,0:T(8,128)} custom-call(f32[384,1024]{1,0:T(8,128)} %get-tuple-element.43.start, bf16[384,1536]{1,0:T(8,128)(2,1)} %get-tuple-element.44.ltop.refs_2_, bf16[384,1536]{1,0:T(8,128)(2,1)} %get-tuple-element.45.lbot.refs_3_, f32[192,1024]{1,0:T(8,128)} %copy-done.1, f32[192,1024]{1,0:T(8,128)} %copy-done, ...), custom_call_target="tpu_custom_call" | custom-call | flops 2147483648 | bytes 9437184 | tf_op jit(solution)/shard_map/pallas_call | solution.py:274
  65.7 9.2 %collective-permute-done.12.refs_6_ = f32[96,1024]{1,0:T(8,128)S(1)} collective-permute-done((f32[96,1024]{1,0:T(8,128)S(1)}, f32[96,1024]{1,0:T(8,128)S(1)}, u32[]{:S(2)}, u32[]{:S(2)}) %collective-permute-start.12) | collective-permute-done | bytes 393248 | tf_op jit(solution)/shard_map/ppermute | solution.py:46
  75.9 9.3 %shard_map.89 = (f32[2,48,1024]{2,1,0:T(8,128)}, f32[2,48,1024]{2,1,0:T(8,128)}, f32[2,48,1024]{2,1,0:T(8,128)}, f32[2,48,1024]{2,1,0:T(8,128)}, f32[2560,128]{1,0:T(8,128)}, /*index=5*/f32[2560,128]{1,0:T(8,128)}) custom-call(f32[384,1024]{1,0:T(8,128)} %shard_map.88.refs_0_, f32[2560,256]{1,0:T(8,128)} %shard_map.86.refs_1_, ...), custom_call_target="tpu_custom_call" | custom-call | flops 4294967296 | bytes 12058624 | tf_op jit(solution)/shard_map/pallas_call | solution.py:274
  89.7 2.9 %shard_map.91 = (f32[640,128]{1,0:T(8,128)}, f32[640,128]{1,0:T(8,128)}, f32[640,128]{1,0:T(8,128)}, f32[640,128]{1,0:T(8,128)}) custom-call(f32[2560,128]{1,0:T(8,128)} %get-tuple-element.57.refs_0_, f32[2560,128]{1,0:T(8,128)} %copy-done.4), custom_call_target="tpu_custom_call" | custom-call | bytes 2621440 | tf_op jit(solution)/shard_map/pallas_call | solution.py:274
  92.6 3.8 %collective-permute-start.20 = (f32[640,128]{1,0:T(8,128)}, f32[640,128]{1,0:T(8,128)S(1)}, u32[]{:S(2)}, u32[]{:S(2)}) collective-permute-start(f32[640,128]{1,0:T(8,128)} %get-tuple-element.61), channel_id=1, source_target_pairs={{0,16},{1,17},{2,18},{3,19},{4,20},{5,21},{6,22},{7,23},{8,24},{9,... | collective-permute-start | bytes 983048 | tf_op jit(solution)/shard_map/ppermute | solution.py:46
  96.5 6.5 %collective-permute-done.19.refs_1_ = f32[640,128]{1,0:T(8,128)S(1)} collective-permute-done((f32[640,128]{1,0:T(8,128)}, f32[640,128]{1,0:T(8,128)S(1)}, u32[]{:S(2)}, u32[]{:S(2)}) %collective-permute-start.19) | collective-permute-done | bytes 327712 | tf_op jit(solution)/shard_map/ppermute | solution.py:46
  102.9 8.2 %collective-permute-done.20.refs_2_ = f32[640,128]{1,0:T(8,128)S(1)} collective-permute-done((f32[640,128]{1,0:T(8,128)}, f32[640,128]{1,0:T(8,128)S(1)}, u32[]{:S(2)}, u32[]{:S(2)}) %collective-permute-start.20) | collective-permute-done | bytes 327712 | tf_op jit(solution)/shard_map/ppermute | solution.py:46
  129.0 5.6 %collective-permute-start.27 = (f32[160,128]{1,0:T(8,128)S(1)}, f32[160,128]{1,0:T(8,128)S(1)}, u32[]{:S(2)}, u32[]{:S(2)}) collective-permute-start(f32[160,128]{1,0:T(8,128)S(1)} %add.26), channel_id=1, source_target_pairs={{0,128},{1,129},{2,130},{3,131},{4,132},{5,133},{6,134},{7,135},{8... | collective-permute-start | bytes 245768 | tf_op jit(solution)/shard_map/ppermute | solution.py:46
  136.9 4.1 %collective-permute-start.29 = (f32[160,128]{1,0:T(8,128)S(1)}, f32[160,128]{1,0:T(8,128)S(1)}, u32[]{:S(2)}, u32[]{:S(2)}) collective-permute-start(f32[160,128]{1,0:T(8,128)S(1)} %add.27.refs_0_), channel_id=1, source_target_pairs={{0,64},{1,65},{2,66},{3,67},{4,68},{5,69},{6,70},{7,71},{8,72},{9,... | collective-permute-start | bytes 245768 | tf_op jit(solution)/shard_map/ppermute | solution.py:46
  146.7 3.9 %collective-permute-start.33 = (f32[640,128]{1,0:T(8,128)}, f32[640,128]{1,0:T(8,128)S(1)}, u32[]{:S(2)}, u32[]{:S(2)}) collective-permute-start(f32[640,128]{1,0:T(8,128)} %shard_map.93.refs_0_), channel_id=1, source_target_pairs={{0,24},{1,25},{2,26},{3,27},{4,28},{5,29},{6,30},{7,31},{8,0},{9,1... | collective-permute-start | bytes 983048 | tf_op jit(solution)/shard_map/ppermute | solution.py:46
  152.0 12.5 %collective-permute-start.34 = (f32[640,128]{1,0:T(8,128)}, f32[640,128]{1,0:T(8,128)S(1)}, u32[]{:S(2)}, u32[]{:S(2)}) collective-permute-start(f32[640,128]{1,0:T(8,128)} %shard_map.93.refs_0_), channel_id=1, source_target_pairs={{0,1},{1,0},{2,3},{3,2},{4,5},{5,4},{6,7},{7,6},{8,9},{9,8},{10,11... | collective-permute-start | bytes 983048 | tf_op jit(solution)/shard_map/ppermute | solution.py:46
  164.4 7.4 %collective-permute-start.37 = (f32[640,128]{1,0:T(8,128)S(1)}, f32[640,128]{1,0:T(8,128)S(1)}, u32[]{:S(2)}, u32[]{:S(2)}) collective-permute-start(f32[640,128]{1,0:T(8,128)S(1)} %collective-permute-done.33.refs_3_), channel_id=1, source_target_pairs={{0,1},{1,0},{2,3},{3,2},{4,5},{5,4},{6,7},{7,6},{8,9},{9,8},{10,11... | collective-permute-start | bytes 983048 | tf_op jit(solution)/shard_map/ppermute | solution.py:46
  172.3 3.1 %collective-permute-start.35 = (f32[640,128]{1,0:T(8,128)S(1)}, f32[640,128]{1,0:T(8,128)S(1)}, u32[]{:S(2)}, u32[]{:S(2)}) collective-permute-start(f32[640,128]{1,0:T(8,128)S(1)} %collective-permute-done.31.refs_1_), channel_id=1, source_target_pairs={{0,1},{1,0},{2,3},{3,2},{4,5},{5,4},{6,7},{7,6},{8,9},{9,8},{10,11... | collective-permute-start | bytes 983048 | tf_op jit(solution)/shard_map/ppermute | solution.py:46
  178.3 3.0 %collective-permute-start.38 = (f32[48,1024]{1,0:T(8,128)}, f32[48,1024]{1,0:T(8,128)S(1)}, u32[]{:S(2)}, u32[]{:S(2)}) collective-permute-start(f32[48,1024]{1,0:T(8,128)} %get-tuple-element.70), channel_id=1, source_target_pairs={{0,128},{1,129},{2,130},{3,131},{4,132},{5,133},{6,134},{7,135},{8... | collective-permute-start | bytes 589832 | tf_op jit(solution)/shard_map/ppermute | solution.py:46
  183.0 3.5 %shard_map.94 = (f32[6,256,256]{2,1,0:T(8,128)}, f32[4,256,256]{2,1,0:T(8,128)}) custom-call(f32[640,128]{1,0:T(8,128)} %shard_map.93.refs_0_, f32[640,128]{1,0:T(8,128)} %copy-done.12, f32[640,128]{1,0:T(8,128)} %copy-done.11, f32[640,128]{1,0:T(8,128)} %copy-done.10, f32[640,128]{1,0:T(8,128)} %copy-done.13, f32[640,128]{1,0:T(8,128)} %copy-done.16, ...), custom_call_target="tpu_custom_call" | custom-call | bytes 2621440 | tf_op jit(solution)/shard_map/pallas_call | solution.py:274
  186.5 6.3 %collective-permute-done.38.got = f32[48,1024]{1,0:T(8,128)S(1)} collective-permute-done((f32[48,1024]{1,0:T(8,128)}, f32[48,1024]{1,0:T(8,128)S(1)}, u32[]{:S(2)}, u32[]{:S(2)}) %collective-permute-start.38) | collective-permute-done | bytes 196640 | tf_op jit(solution)/shard_map/ppermute | solution.py:46
  (138 shorter events, 58.8 us)
Async XLA Ops:
  3.5 11.1 %collective-permute-start.2 = (f32[48,1024]{1,0:T(8,128)}, f32[48,1024]{1,0:T(8,128)S(1)}, u32[]{:S(2)}, u32[]{:S(2)}) collective-permute-start(f32[48,1024]{1,0:T(8,128)} %shard_map.85), channel_id=1, source_target_pairs={{0,6},{1,7},{2,0},{3,1},{4,2},{5,3},{6,4},{7,5},{8,14},{9,15},{10,... | collective-permute-start | bytes 589832 | tf_op jit(solution)/shard_map/ppermute | solution.py:46
  3.5 15.5 %collective-permute-start.1 = (f32[48,1024]{1,0:T(8,128)}, f32[48,1024]{1,0:T(8,128)S(1)}, u32[]{:S(2)}, u32[]{:S(2)}) collective-permute-start(f32[48,1024]{1,0:T(8,128)} %shard_map.85), channel_id=1, source_target_pairs={{0,4},{1,5},{2,6},{3,7},{4,0},{5,1},{6,2},{7,3},{8,12},{9,13},{10,... | collective-permute-start | bytes 589832 | tf_op jit(solution)/shard_map/ppermute | solution.py:46
  6.5 16.7 %collective-permute-start = (f32[48,1024]{1,0:T(8,128)}, f32[48,1024]{1,0:T(8,128)S(1)}, u32[]{:S(2)}, u32[]{:S(2)}) collective-permute-start(f32[48,1024]{1,0:T(8,128)} %shard_map.85), channel_id=1, source_target_pairs={{0,2},{1,3},{2,4},{3,5},{4,6},{5,7},{6,0},{7,1},{8,10},{9,11},{10,... | collective-permute-start | bytes 589832 | tf_op jit(solution)/shard_map/ppermute | solution.py:46
  23.3 17.6 %collective-permute-start.5 = (f32[192,1024]{1,0:T(8,128)S(1)}, f32[192,1024]{1,0:T(8,128)S(1)}, u32[]{:S(2)}, u32[]{:S(2)}) collective-permute-start(f32[192,1024]{1,0:T(8,128)S(1)} %pad_maximum_fusion.near), channel_id=1, source_target_pairs={{0,1},{1,0},{2,3},{3,2},{4,5},{5,4},{6,7},{7,6},{8,9},{9,8},{10,11... | collective-permute-start | bytes 2359304 | tf_op jit(solution)/shard_map/ppermute | solution.py:46
  24.8 22.8 %collective-permute-start.4 = (f32[192,1024]{1,0:T(8,128)S(1)}, f32[192,1024]{1,0:T(8,128)S(1)}, u32[]{:S(2)}, u32[]{:S(2)}) collective-permute-start(f32[192,1024]{1,0:T(8,128)S(1)} %pad_maximum_fusion.near), channel_id=1, source_target_pairs={{0,24},{1,25},{2,26},{3,27},{4,28},{5,29},{6,30},{7,31},{8,0},{9,1... | collective-permute-start | bytes 2359304 | tf_op jit(solution)/shard_map/ppermute | solution.py:46
  27.5 20.0 %collective-permute-start.3 = (f32[192,1024]{1,0:T(8,128)S(1)}, f32[192,1024]{1,0:T(8,128)S(1)}, u32[]{:S(2)}, u32[]{:S(2)}) collective-permute-start(f32[192,1024]{1,0:T(8,128)S(1)} %pad_maximum_fusion.near), channel_id=1, source_target_pairs={{0,8},{1,9},{2,10},{3,11},{4,12},{5,13},{6,14},{7,15},{8,16},{9,17... | collective-permute-start | bytes 2359304 | tf_op jit(solution)/shard_map/ppermute | solution.py:46
  28.6 11.4 %collective-permute-start.6 = (f32[48,1024]{1,0:T(8,128)S(1)}, f32[48,1024]{1,0:T(8,128)S(1)}, u32[]{:S(2)}, u32[]{:S(2)}) collective-permute-start(f32[48,1024]{1,0:T(8,128)S(1)} %copy-done.2), channel_id=1, source_target_pairs={{0,96},{1,97},{2,98},{3,99},{4,100},{5,101},{6,102},{7,103},{8,104... | collective-permute-start | bytes 589832 | tf_op jit(solution)/shard_map/ppermute | solution.py:46
  49.5 15.0 %collective-permute-start.9 = (f32[96,1024]{1,0:T(8,128)}, f32[96,1024]{1,0:T(8,128)}, u32[]{:S(2)}, u32[]{:S(2)}) collective-permute-start(f32[96,1024]{1,0:T(8,128)} %slice.7), channel_id=1, source_target_pairs={{0,24},{1,25},{2,26},{3,27},{4,28},{5,29},{6,30},{7,31},{8,0},{9,1... | collective-permute-start | bytes 1179656 | tf_op jit(solution)/shard_map/ppermute | solution.py:46
  51.7 12.8 %collective-permute-start.8 = (f32[96,1024]{1,0:T(8,128)S(1)}, f32[96,1024]{1,0:T(8,128)}, u32[]{:S(2)}, u32[]{:S(2)}) collective-permute-start(f32[96,1024]{1,0:T(8,128)S(1)} %slice.6), channel_id=1, source_target_pairs={{0,8},{1,9},{2,10},{3,11},{4,12},{5,13},{6,14},{7,15},{8,16},{9,17... | collective-permute-start | bytes 1179656 | tf_op jit(solution)/shard_map/ppermute | solution.py:46
  51.8 23.1 %collective-permute-start.12 = (f32[96,1024]{1,0:T(8,128)S(1)}, f32[96,1024]{1,0:T(8,128)S(1)}, u32[]{:S(2)}, u32[]{:S(2)}) collective-permute-start(f32[96,1024]{1,0:T(8,128)S(1)} %constant_dynamic-slice_fusion), channel_id=1, source_target_pairs={{0,128},{1,129},{2,130},{3,131},{4,132},{5,133},{6,134},{7,135},{8... | collective-permute-start | bytes 1179656 | tf_op jit(solution)/shard_map/ppermute | solution.py:46
  64.5 10.4 %collective-permute-start.13 = (f32[96,1024]{1,0:T(8,128)}, f32[96,1024]{1,0:T(8,128)S(1)}, u32[]{:S(2)}, u32[]{:S(2)}) collective-permute-start(f32[96,1024]{1,0:T(8,128)} %collective-permute-done.8.refs_7_), channel_id=1, source_target_pairs={{0,1},{1,0},{2,3},{3,2},{4,5},{5,4},{6,7},{7,6},{8,9},{9,8},{10,11... | collective-permute-start | bytes 1179656 | tf_op jit(solution)/shard_map/ppermute | solution.py:46
  92.6 10.3 %collective-permute-start.19 = (f32[640,128]{1,0:T(8,128)}, f32[640,128]{1,0:T(8,128)S(1)}, u32[]{:S(2)}, u32[]{:S(2)}) collective-permute-start(f32[640,128]{1,0:T(8,128)} %get-tuple-element.60), channel_id=1, source_target_pairs={{0,8},{1,9},{2,10},{3,11},{4,12},{5,13},{6,14},{7,15},{8,16},{9,17... | collective-permute-start | bytes 983048 | tf_op jit(solution)/shard_map/ppermute | solution.py:46
  92.6 18.5 %collective-permute-start.20 = (f32[640,128]{1,0:T(8,128)}, f32[640,128]{1,0:T(8,128)S(1)}, u32[]{:S(2)}, u32[]{:S(2)}) collective-permute-start(f32[640,128]{1,0:T(8,128)} %get-tuple-element.61), channel_id=1, source_target_pairs={{0,16},{1,17},{2,18},{3,19},{4,20},{5,21},{6,22},{7,23},{8,24},{9,... | collective-permute-start | bytes 983048 | tf_op jit(solution)/shard_map/ppermute | solution.py:46
  96.5 14.7 %collective-permute-start.21 = (f32[640,128]{1,0:T(8,128)}, f32[640,128]{1,0:T(8,128)S(1)}, u32[]{:S(2)}, u32[]{:S(2)}) collective-permute-start(f32[640,128]{1,0:T(8,128)} %get-tuple-element.62), channel_id=1, source_target_pairs={{0,24},{1,25},{2,26},{3,27},{4,28},{5,29},{6,30},{7,31},{8,0},{9,1... | collective-permute-start | bytes 983048 | tf_op jit(solution)/shard_map/ppermute | solution.py:46
  121.3 29.9 %collective-permute-start.15 = (f32[2,48,1024]{2,1,0:T(8,128)S(1)}, f32[2,48,1024]{2,1,0:T(8,128)S(1)}, u32[]{:S(2)}, u32[]{:S(2)}) collective-permute-start(f32[2,48,1024]{2,1,0:T(8,128)S(1)} %copy-done.28), channel_id=1, source_target_pairs={{0,32},{1,33},{2,34},{3,35},{4,36},{5,37},{6,38},{7,39},{8,40},{9,... | collective-permute-start | bytes 1179656 | tf_op jit(solution)/shard_map/ppermute | solution.py:46
  141.0 11.0 %collective-permute-start.16 = (f32[2,48,1024]{2,1,0:T(8,128)S(1)}, f32[2,48,1024]{2,1,0:T(8,128)S(1)}, u32[]{:S(2)}, u32[]{:S(2)}) collective-permute-start(f32[2,48,1024]{2,1,0:T(8,128)S(1)} %copy-done.27), channel_id=1, source_target_pairs={{0,64},{1,65},{2,66},{3,67},{4,68},{5,69},{6,70},{7,71},{8,72},{9,... | collective-permute-start | bytes 1179656 | tf_op jit(solution)/shard_map/ppermute | solution.py:46
  146.7 17.7 %collective-permute-start.33 = (f32[640,128]{1,0:T(8,128)}, f32[640,128]{1,0:T(8,128)S(1)}, u32[]{:S(2)}, u32[]{:S(2)}) collective-permute-start(f32[640,128]{1,0:T(8,128)} %shard_map.93.refs_0_), channel_id=1, source_target_pairs={{0,24},{1,25},{2,26},{3,27},{4,28},{5,29},{6,30},{7,31},{8,0},{9,1... | collective-permute-start | bytes 983048 | tf_op jit(solution)/shard_map/ppermute | solution.py:46
  150.6 21.2 %collective-permute-start.32 = (f32[640,128]{1,0:T(8,128)}, f32[640,128]{1,0:T(8,128)S(1)}, u32[]{:S(2)}, u32[]{:S(2)}) collective-permute-start(f32[640,128]{1,0:T(8,128)} %shard_map.93.refs_0_), channel_id=1, source_target_pairs={{0,16},{1,17},{2,18},{3,19},{4,20},{5,21},{6,22},{7,23},{8,24},{9,... | collective-permute-start | bytes 983048 | tf_op jit(solution)/shard_map/ppermute | solution.py:46
  150.6 21.7 %collective-permute-start.31 = (f32[640,128]{1,0:T(8,128)}, f32[640,128]{1,0:T(8,128)S(1)}, u32[]{:S(2)}, u32[]{:S(2)}) collective-permute-start(f32[640,128]{1,0:T(8,128)} %shard_map.93.refs_0_), channel_id=1, source_target_pairs={{0,8},{1,9},{2,10},{3,11},{4,12},{5,13},{6,14},{7,15},{8,16},{9,17... | collective-permute-start | bytes 983048 | tf_op jit(solution)/shard_map/ppermute | solution.py:46
  151.2 24.2 %collective-permute-start.17 = (f32[2,48,1024]{2,1,0:T(8,128)S(1)}, f32[2,48,1024]{2,1,0:T(8,128)S(1)}, u32[]{:S(2)}, u32[]{:S(2)}) collective-permute-start(f32[2,48,1024]{2,1,0:T(8,128)S(1)} %copy-done.26), channel_id=1, source_target_pairs={{0,96},{1,97},{2,98},{3,99},{4,100},{5,101},{6,102},{7,103},{8,104... | collective-permute-start | bytes 1179656 | tf_op jit(solution)/shard_map/ppermute | solution.py:46
  152.0 29.3 %collective-permute-start.34 = (f32[640,128]{1,0:T(8,128)}, f32[640,128]{1,0:T(8,128)S(1)}, u32[]{:S(2)}, u32[]{:S(2)}) collective-permute-start(f32[640,128]{1,0:T(8,128)} %shard_map.93.refs_0_), channel_id=1, source_target_pairs={{0,1},{1,0},{2,3},{3,2},{4,5},{5,4},{6,7},{7,6},{8,9},{9,8},{10,11... | collective-permute-start | bytes 983048 | tf_op jit(solution)/shard_map/ppermute | solution.py:46
  164.4 16.9 %collective-permute-start.37 = (f32[640,128]{1,0:T(8,128)S(1)}, f32[640,128]{1,0:T(8,128)S(1)}, u32[]{:S(2)}, u32[]{:S(2)}) collective-permute-start(f32[640,128]{1,0:T(8,128)S(1)} %collective-permute-done.33.refs_3_), channel_id=1, source_target_pairs={{0,1},{1,0},{2,3},{3,2},{4,5},{5,4},{6,7},{7,6},{8,9},{9,8},{10,11... | collective-permute-start | bytes 983048 | tf_op jit(solution)/shard_map/ppermute | solution.py:46
  171.8 9.5 %collective-permute-start.36 = (f32[640,128]{1,0:T(8,128)S(1)}, f32[640,128]{1,0:T(8,128)S(1)}, u32[]{:S(2)}, u32[]{:S(2)}) collective-permute-start(f32[640,128]{1,0:T(8,128)S(1)} %collective-permute-done.32.refs_2_), channel_id=1, source_target_pairs={{0,1},{1,0},{2,3},{3,2},{4,5},{5,4},{6,7},{7,6},{8,9},{9,8},{10,11... | collective-permute-start | bytes 983048 | tf_op jit(solution)/shard_map/ppermute | solution.py:46
  178.3 14.5 %collective-permute-start.38 = (f32[48,1024]{1,0:T(8,128)}, f32[48,1024]{1,0:T(8,128)S(1)}, u32[]{:S(2)}, u32[]{:S(2)}) collective-permute-start(f32[48,1024]{1,0:T(8,128)} %get-tuple-element.70), channel_id=1, source_target_pairs={{0,128},{1,129},{2,130},{3,131},{4,132},{5,133},{6,134},{7,135},{8... | collective-permute-start | bytes 589832 | tf_op jit(solution)/shard_map/ppermute | solution.py:46
  (47 other events, 405.0 us)

commit v5 on v4

--- a/solution.py
+++ b/solution.py
@@ -92,7 +92,12 @@
             values[j] = values[j] - mul(left, halves(blocks[j, m]))
 
 
-def base_kernel(order, parent, couple, diag_inv, out, *held):
+def base_table(order):
+    at = lambda q, j: order.index((q, j))
+    return [(at(m, j), at(q, m), at(q, j)) for j in range(NSUP) for m in range(j + 1) for q in range(m)]
+
+
+def base_kernel(order, parent, table, couple, diag_inv, out, *held):
     chigh, clow, ihigh, ilow, shigh, slow = held
     at = lambda q, j: order.index((q, j))
 
@@ -120,10 +125,14 @@
             value = mul(kept(shigh, slow, at(q, q)), kept(ihigh, ilow, i))
             out[i * W : (i + 1) * W, :] = value
             keep(shigh, slow, i, value)
-    for i, (m, j) in enumerate(order):
-        rows = slice(i * W, (i + 1) * W)
-        for q in range(m):
-            out[rows, :] = out[rows, :] + mul(kept(ihigh, ilow, at(q, m)), kept(shigh, slow, at(q, j)), (0, 0))
+
+    def gain(t, carry):
+        where = pl.ds(pl.multiple_of(table[t, 0] * W, W), W)
+        left, right = kept(ihigh, ilow, table[t, 1]), kept(shigh, slow, table[t, 2])
+        out[where, :] = out[where, :] + mul(left, right, (0, 0))
+        return carry
+
+    lax.fori_loop(0, len(base_table(order)), gain, 0)
 
 
 def put(piece, top, bot, row_of, weight=None):
@@ -139,7 +148,7 @@
     lax.fori_loop(0, piece.shape[0] // RW, step, 0)
 
 
-def near_kernel(local, near, twin, cross, out, ltop, lbot, rtop, rbot, top, bot):
+def near_kernel(local, own, rest, twin, cross, out, ltop, lbot, rtop, rbot, top, bot):
     at = place()
     span = local.shape[1] // 4
     for i, k in enumerate((0, 1, 3, 2)):
@@ -154,18 +163,23 @@
 
         lax.fori_loop(0, local.shape[0] // RW, step, 0)
     put(cross, rtop, rbot, lambda r: r * RW, lambda r: jnp.where(r == 1, 1.0, 0.5).astype(F32))
-    for par, piece in enumerate((near, twin)):
+    for piece, par, skip in ((own, 0, 0), (rest, 0, 1), (twin, 1, 0)):
         core = at["c"] ^ par
-        put(piece, top, bot, lambda r: (((at["zl"] - r) & 3) * 2 + core) * RW)
+        put(piece, top, bot, lambda r: (((at["zl"] - r - skip) & 3) * 2 + core) * RW)
     out[...] = mul((ltop[:, :span], lbot[:, :span]), (top[...], bot[...]))
 
 
-def early_kernel(start, ltop, lbot, left, right, ltwin, rtwin, out, top, bot):
+def early_kernel(start, ltop, lbot, *refs):
+    pieces, (out, top, bot) = refs[:6], refs[6:]
     at = place()
     span = ltop.shape[1] // 4
-    for i, piece in enumerate((left, right, ltwin, rtwin)):
-        core = at["c"] ^ (i // 2)
-        put(piece, top, bot, lambda r: ((i % 2) * 8 + ((at["zl"] - r) & 3) * 2 + core) * RW)
+    for i, piece in enumerate(pieces):
+        core = at["c"] ^ (i // 3)
+        if i % 3 == 0:
+            put(piece, top, bot, lambda r: (r * 8 + at["zl"] * 2 + core) * RW)
+        else:
+            side = i % 3 - 1
+            put(piece, top, bot, lambda r: (side * 8 + ((at["zl"] - r - 1) & 3) * 2 + core) * RW)
     cols = slice(span, 3 * span)
     out[...] = start[...] + mul((ltop[:, cols], lbot[:, cols]), (top[...], bot[...]))
 
@@ -203,7 +217,10 @@
     for i, (m, j) in enumerate(order):
         one, two = slice(m * W, (m + 1) * W), slice(j * W, (j + 1) * W)
         block = mul((rtop[:, one], rbot[:, one]), (ptop[:, two], pbot[:, two]), (0, 0))
-        block = block + mul((ptop[:, one], pbot[:, one]), (rtop[:, two], rbot[:, two]), (0, 0))
+        if m == j:
+            block = block + block.T
+        else:
+            block = block + mul((ptop[:, one], pbot[:, one]), (rtop[:, two], rbot[:, two]), (0, 0))
         rows = slice(i * W, (i + 1) * W)
         block = block + jnp.where(lead, base[rows, :], 0.0)
         first, second = block[:, :HALF], block[:, HALF:]
@@ -221,52 +238,27 @@
         out[...] = total
 
 
-def columns_kernel(keep, got, out):
+def final_kernel(order, *refs):
+    pieces, (keep, got) = refs[:8], refs[8:10]
+    columns, pair_out, diag_out, whole = refs[10:]
+    at = place()
+    rows = pieces[0].shape[0]
+    small = rows // 4
+    for i, piece in enumerate(pieces):
+        par, k = divmod(i, 4)
+        lane = pl.multiple_of((at["c"] ^ par) * HALF, HALF)
+        for r in range(4):
+            dst = pl.multiple_of(((at["y"] - k) & 3) * rows + ((at["x"] - r) & 3) * small, 8)
+            whole[pl.ds(dst, small), pl.ds(lane, HALF)] = piece[r * small : (r + 1) * small, :]
+    for b, (m, j) in enumerate(order):
+        block = whole[b * W : (b + 1) * W, :]
+        if m == j:
+            diag_out[j] = block
+        else:
+            pair_out[PAIRS.index((m, j))] = block
     for j in range(NSUP):
         cols = slice(j * W, (j + 1) * W)
-        out[j] = -(keep[:, cols] + got[:, cols])
-
-
-def join_kernel(axis, *refs):
-    pieces, out = refs[:-1], refs[-1]
-    at = place()[axis]
-    rows = pieces[0].shape[0]
-    for k, piece in enumerate(pieces):
-        dst = pl.multiple_of(((at - k) & (SIZES[axis] - 1)) * rows, 8)
-        out[pl.ds(dst, rows), :] = piece[...]
-
-
-def add_split_kernel(axis, count, *refs):
-    values, outs = refs[:count], refs[count:]
-    at = place()[axis]
-    rows = outs[0].shape[0]
-    for k, out in enumerate(outs):
-        src = pl.ds(pl.multiple_of(((at + k) & (SIZES[axis] - 1)) * rows, 8), rows)
-        total = values[0][src, :]
-        for value in values[1:]:
-            total = total + value[src, :]
-        out[...] = total
-
-
-def final_kernel(orders, *refs):
-    count = 8 * len(orders)
-    pieces, pair_out, diag_out, wholes = refs[:count], refs[count], refs[count + 1], refs[count + 2 :]
-    at = place()
-    for i, order in enumerate(orders):
-        whole = wholes[i]
-        for par in range(2):
-            for k in range(4):
-                piece = pieces[i * 8 + par * 4 + k]
-                rows = piece.shape[0]
-                dst = pl.multiple_of(((at["y"] - k) & 3) * rows, 8)
-                lane = pl.multiple_of((at["c"] ^ par) * HALF, HALF)
-                whole[pl.ds(dst, rows), pl.ds(lane, HALF)] = piece[...]
-        for b, (m, j) in enumerate(order):
-            rows = slice(b * W, (b + 1) * W)
-            if m == j:
-                diag_out[j] = whole[rows, :]
-            else:
-                pair_out[PAIRS.index((m, j))] = whole[rows, :]
+        columns[j] = -(keep[:, cols] + got[:, cols])
 
 
 def kernel(body, args, out_shapes, scratch=(), smem=0, flops=0):
@@ -286,14 +278,11 @@
     )(*args)
 
 
-def split_sum(values, axis):
-    rows, width = values[0].shape
+def split_sum(values, at, axis):
     n = SIZES[axis]
-    return kernel(
-        functools.partial(add_split_kernel, axis, len(values)),
-        list(values),
-        [(rows // n, width)] * n,
-    )
+    rows = values[0].shape[0] // n
+    part = lambda v, k: lax.dynamic_slice_in_dim(v, ((at[axis] + k) & (n - 1)) * rows, rows, 0)
+    return [total_of([part(v, k) for v in values]) for k in range(n)]
 
 
 def scattered(pieces, axis):
@@ -324,35 +313,38 @@
     span = local.shape[1] // 4
 
     near = gathered(own, "zl")
+    firsts = [moved(own, "y", 1), moved(own, "y", 3)]
     cross = [own, moved(own, "x", 3), moved(own, "x", 2)]
     _, couple_later = tie(own, couple)
     base = kernel(
         functools.partial(base_kernel, ALL_BLOCKS),
-        [parent, couple_later, diag_inv],
+        [parent, jnp.array(base_table(ALL_BLOCKS), jnp.int32), couple_later, diag_inv],
         (tall, W),
         [((len(ALL_BLOCKS), W, W), BF16)] * 6,
-        smem=1,
+        smem=2,
         flops=1 << 31,
     )
-    near = jnp.concatenate(near, axis=0)
-    near, base = tie(near, base)
-    cross = jnp.concatenate(cross, axis=0)
-
-    left, right = moved(near, "y", 1), moved(near, "y", 3)
+    rest = jnp.concatenate(near[1:], axis=0)
+    rest, base = tie(rest, base)
+    both = jnp.concatenate(firsts, axis=0)
+    cross, both = tie(jnp.concatenate(cross, axis=0), both)
+
+    left, right = moved(rest, "y", 1), moved(rest, "y", 3)
     distant = moved(lax.dynamic_slice_in_dim(cross, (1 - at["zh"]) * RW, 2 * RW, 0), "zh", 1)
+    twin = moved(jnp.concatenate([own, rest], axis=0), "c", 1)
     start, ltop, lbot, ra, rb = kernel(
         near_kernel,
-        [local, near, moved(near, "c", 1), cross],
+        [local, own, rest, twin, cross],
         [(height, width)] + [((height, 4 * span), BF16)] * 2 + [(cross.shape, BF16)] * 2,
         [((span, width), BF16)] * 2,
         flops=1 << 31,
     )
     left, right, start = tie(left, right, start)
-    half = near.shape[0] // 2
-    far_a, far_b = moved(left[:half], "y", 1), moved(right[half:], "y", 3)
+    far_a = moved(jnp.concatenate([firsts[0], left[:RW]], axis=0), "y", 1)
+    far_b = moved(right[RW:], "y", 3)
     early = kernel(
         early_kernel,
-        [start, ltop, lbot, left, right, moved(left, "c", 1), moved(right, "c", 1)],
+        [start, ltop, lbot, both, left, right] + [moved(v, "c", 1) for v in (both, left, right)],
         (height, width),
         [((2 * span, width), BF16)] * 2,
         flops=1 << 31,
@@ -371,29 +363,26 @@
     )
 
     got = moved(given, "c", 1)
-    cut = split_sum([kept, got], "y")
+    cut = split_sum([kept, got], at, "y")
     cols = scattered(parts, "x")
     across = scattered(cut, "y")
     keep, give = kernel(pick_kernel, cols, [(RW, width)] * 2)
     summed = moved(give, "zh", 1)
-    cut = split_sum(across, "x")
+    cut = split_sum(across, at, "x")
     total = total_of(scattered(cut, "x"))
     total = total + sent(total, "zl", lambda a: a ^ 1)
     total = total + sent(total, "zl", lambda a: a ^ 2)
     total = total + moved(total, "zh", 1)
     lines = gathered(total, "x")
-    total = kernel(functools.partial(join_kernel, "x"), lines, (4 * total.shape[0], HALF))
+    total = jnp.concatenate(lines, axis=0)
     lanes = gathered(total, "y")
     twins = [moved(v, "c", 1) for v in lanes]
-    pair_blocks, diagonal = kernel(
-        functools.partial(final_kernel, [ALL_BLOCKS]),
-        lanes + twins,
-        [(len(PAIRS), W, W), (NSUP, W, W)],
+    return kernel(
+        functools.partial(final_kernel, ALL_BLOCKS),
+        lanes + twins + [keep, summed],
+        [(NSUP, RW, W), (len(PAIRS), W, W), (NSUP, W, W)],
         [((tall, W), F32)],
     )
-    keep, pair_blocks, diagonal = tie(keep, pair_blocks, diagonal)
-    columns = kernel(columns_kernel, [keep, summed], (NSUP, RW, W))
-    return (columns, pair_blocks, diagonal)
 
 
 def solution(mesh):

time: 196 us -> 190 us (0.969)
  the two profiles are of different devices: /device:TPU:39 before, /device:TPU:97 now
where the time goes in v5:
time: 190 us
  starting transfers between devices  80.2 us (42%)
  waiting for transfers between devices  62.1 us (33%)
  Pallas kernels  37.8 us (20%)
  local copies, waits for them, and re-layouts  5.28 us (3%)
  other arithmetic  3.3 us (2%)
    ppermute x42, starting transfers between devices, sent(): return lax.ppermute(value, BOTH, perm)  80.2 us
    ppermute x42, waiting for transfers between devices, sent(): return lax.ppermute(value, BOTH, perm)  62.1 us
    pallas_call x7, Pallas kernels, kernel(): pl.pallas_call(body, out_shape=jax.ShapeDtypeStruct(out_shapes, F32) if s...  37.8 us
    unnamed x54, local copies, waits for them, and re-layouts  4.47 us
  transfers between devices with their start and end apart: 42, of which 19 were waited for; matrix products, arithmetic and copies ran while one was open for 1% of the time, Pallas kernels for 12%

profile of v5, /device:TPU:97, one launch (start us, length us, event | category | flops | bytes accessed | tf_op | source)
XLA Modules:
  0.0 189.6 jit_solution(149804227055566385)
XLA Ops:
  0.6 2.9 %shard_map.94.own = f32[48,1024]{1,0:T(8,128)} custom-call(s32[4]{0:T(128)} %parent.3, s32[4,48]{1,0:T(4,128)} %pattern.1, f32[4,48,256]{2,1,0:T(8,128)} %factor.1, f32[6,256,256]{2,1,0:T(8,128)} %couple.2), custom_call_target="tpu_custom_call" | custom-call | flops 1048576 | bytes 1770256 | tf_op jit(solution)/shard_map/pallas_call | solution.py:266
  5.0 7.8 %shard_map.95.refs_1_ = f32[2560,256]{1,0:T(8,128)} custom-call(s32[4]{0:T(128)} %parent.3, s32[10,3]{1,0:T(8,128)} %constant.29.clone.table, f32[6,256,256]{2,1,0:T(8,128)} %couple.2, f32[4,256,256]{2,1,0:T(8,128)} %diag_inv.1), custom_call_target="tpu_custom_call" | custom-call | flops 2147483648 | bytes 2621576 | tf_op jit(solution)/shard_map/pallas_call | solution.py:266
  12.7 8.9 %collective-permute-done.2 = f32[48,1024]{1,0:T(8,128)S(1)} collective-permute-done((f32[48,1024]{1,0:T(8,128)}, f32[48,1024]{1,0:T(8,128)S(1)}, u32[]{:S(2)}, u32[]{:S(2)}) %collective-permute-start.2) | collective-permute-done | bytes 196640 | tf_op jit(solution)/shard_map/ppermute | solution.py:46
  26.2 2.7 %collective-permute-start.5 = (f32[144,1024]{1,0:T(8,128)S(1)}, f32[144,1024]{1,0:T(8,128)S(1)}, u32[]{:S(2)}, u32[]{:S(2)}) collective-permute-start(f32[144,1024]{1,0:T(8,128)S(1)} %pad_maximum_fusion.1.rest), channel_id=1, source_target_pairs={{0,24},{1,25},{2,26},{3,27},{4,28},{5,29},{6,30},{7,31},{8,0},{9,1... | collective-permute-start | bytes 1769480 | tf_op jit(solution)/shard_map/ppermute | solution.py:46
  31.1 2.5 %collective-permute-start.7 = (f32[48,1024]{1,0:T(8,128)S(1)}, f32[48,1024]{1,0:T(8,128)S(1)}, u32[]{:S(2)}, u32[]{:S(2)}) collective-permute-start(f32[48,1024]{1,0:T(8,128)S(1)} %copy-done.1), channel_id=1, source_target_pairs={{0,96},{1,97},{2,98},{3,99},{4,100},{5,101},{6,102},{7,103},{8,104... | collective-permute-start | bytes 589832 | tf_op jit(solution)/shard_map/ppermute | solution.py:46
  34.2 3.9 %collective-permute-done.7 = f32[48,1024]{1,0:T(8,128)S(1)} collective-permute-done((f32[48,1024]{1,0:T(8,128)S(1)}, f32[48,1024]{1,0:T(8,128)S(1)}, u32[]{:S(2)}, u32[]{:S(2)}) %collective-permute-start.7) | collective-permute-done | bytes 196640 | tf_op jit(solution)/shard_map/ppermute | solution.py:46
  41.4 5.7 %shard_map.96 = (f32[384,1024]{1,0:T(8,128)}, bf16[384,1536]{1,0:T(8,128)(2,1)}, bf16[384,1536]{1,0:T(8,128)(2,1)}, bf16[144,1024]{1,0:T(8,128)(2,1)}, bf16[144,1024]{1,0:T(8,128)(2,1)}) custom-call(f32[384,1536]{1,0:T(8,128)} %bitcast.1, f32[48,1024]{1,0:T(8,128)} %shard_map.94.own, f32[144,1024]{1,0:T(8,128)} %copy-done, f32[192,1024]{1,0:T(8,128)} %copy-done.20, ...), custom_call_target="tpu_custom_call" | custom-call | flops 2147483648 | bytes 4521984 | tf_op jit(solution)/shard_map/pallas_call | solution.py:266
  47.2 3.4 %collective-permute-start.13 = (f32[144,1024]{1,0:T(8,128)S(1)}, f32[144,1024]{1,0:T(8,128)S(1)}, u32[]{:S(2)}, u32[]{:S(2)}) collective-permute-start(f32[144,1024]{1,0:T(8,128)S(1)} %collective-permute-done.4.refs_1_), channel_id=1, source_target_pairs={{0,1},{1,0},{2,3},{3,2},{4,5},{5,4},{6,7},{7,6},{8,9},{9,8},{10,11... | collective-permute-start | bytes 1769480 | tf_op jit(solution)/shard_map/ppermute | solution.py:46
  52.7 2.7 %collective-permute-start.11 = (f32[96,1024]{1,0:T(8,128)}, f32[96,1024]{1,0:T(8,128)}, u32[]{:S(2)}, u32[]{:S(2)}) collective-permute-start(f32[96,1024]{1,0:T(8,128)} %slice.7), channel_id=1, source_target_pairs={{0,24},{1,25},{2,26},{3,27},{4,28},{5,29},{6,30},{7,31},{8,0},{9,1... | collective-permute-start | bytes 1179656 | tf_op jit(solution)/shard_map/ppermute | solution.py:46
  55.4 5.2 %collective-permute-start.15 = (f32[96,1024]{1,0:T(8,128)S(1)}, f32[96,1024]{1,0:T(8,128)S(1)}, u32[]{:S(2)}, u32[]{:S(2)}) collective-permute-start(f32[96,1024]{1,0:T(8,128)S(1)} %constant_dynamic-slice_fusion), channel_id=1, source_target_pairs={{0,128},{1,129},{2,130},{3,131},{4,132},{5,133},{6,134},{7,135},{8... | collective-permute-start | bytes 1179656 | tf_op jit(solution)/shard_map/ppermute | solution.py:46
  61.6 6.7 %shard_map.97.refs_0_ = f32[384,1024]{1,0:T(8,128)} custom-call(f32[384,1024]{1,0:T(8,128)} %get-tuple-element.33.start, bf16[384,1536]{1,0:T(8,128)(2,1)} %get-tuple-element.34.ltop.refs_2_, bf16[384,1536]{1,0:T(8,128)(2,1)} %get-tuple-element.35.lbot.refs_3_, f32[96,1024]{1,0:T(8,128)} %copy-done.4, f32[144,1024]{1,0:T(8,128)} %copy-done.6, ...), custom_call_target="tpu_custom_call" | custom-call | flops 2147483648 | bytes 9437184 | tf_op jit(solution)/shard_map/pallas_call | solution.py:266
  72.3 8.9 %shard_map.98 = (f32[2,48,1024]{2,1,0:T(8,128)}, f32[2,48,1024]{2,1,0:T(8,128)}, f32[2,48,1024]{2,1,0:T(8,128)}, f32[2,48,1024]{2,1,0:T(8,128)}, f32[2560,128]{1,0:T(8,128)}, /*index=5*/f32[2560,128]{1,0:T(8,128)}) custom-call(f32[384,1024]{1,0:T(8,128)} %shard_map.97.refs_0_, f32[2560,256]{1,0:T(8,128)} %shard_map.95.refs_1_, ...), custom_call_target="tpu_custom_call" | custom-call | flops 4294967296 | bytes 12058624 | tf_op jit(solution)/shard_map/pallas_call | solution.py:266
  81.6 2.9 %collective-permute-done.18 = f32[2560,128]{1,0:T(8,128)S(1)} collective-permute-done((f32[2560,128]{1,0:T(8,128)}, f32[2560,128]{1,0:T(8,128)S(1)}, u32[]{:S(2)}, u32[]{:S(2)}) %collective-permute-start.18) | collective-permute-done | bytes 1310752 | tf_op jit(solution)/shard_map/ppermute | solution.py:46
  88.6 14.5 %collective-permute-done.19 = f32[640,128]{1,0:T(8,128)S(1)} collective-permute-done((f32[640,128]{1,0:T(8,128)S(1)}, f32[640,128]{1,0:T(8,128)S(1)}, u32[]{:S(2)}, u32[]{:S(2)}) %collective-permute-start.19) | collective-permute-done | bytes 327712 | tf_op jit(solution)/shard_map/ppermute | solution.py:46
  105.4 2.7 %collective-permute-start.23 = (f32[160,128]{1,0:T(8,128)S(1)}, f32[160,128]{1,0:T(8,128)S(1)}, u32[]{:S(2)}, u32[]{:S(2)}) collective-permute-start(f32[160,128]{1,0:T(8,128)S(1)} %get-tuple-element.57), channel_id=1, source_target_pairs={{0,64},{1,65},{2,66},{3,67},{4,68},{5,69},{6,70},{7,71},{8,72},{9,... | collective-permute-start | bytes 245768 | tf_op jit(solution)/shard_map/ppermute | solution.py:46
  112.6 6.6 %collective-permute-start.25 = (f32[160,128]{1,0:T(8,128)S(1)}, f32[160,128]{1,0:T(8,128)S(1)}, u32[]{:S(2)}, u32[]{:S(2)}) collective-permute-start(f32[160,128]{1,0:T(8,128)S(1)} %add_add_fusion), channel_id=1, source_target_pairs={{0,2},{1,3},{2,0},{3,1},{4,6},{5,7},{6,4},{7,5},{8,10},{9,11},{10,... | collective-permute-start | bytes 245768 | tf_op jit(solution)/shard_map/ppermute | solution.py:46
  121.0 4.5 %collective-permute-start.26 = (f32[160,128]{1,0:T(8,128)S(1)}, f32[160,128]{1,0:T(8,128)S(1)}, u32[]{:S(2)}, u32[]{:S(2)}) collective-permute-start(f32[160,128]{1,0:T(8,128)S(1)} %add.173), channel_id=1, source_target_pairs={{0,4},{1,5},{2,6},{3,7},{4,0},{5,1},{6,2},{7,3},{8,12},{9,13},{10,... | collective-permute-start | bytes 245768 | tf_op jit(solution)/shard_map/ppermute | solution.py:46
  128.0 5.4 %collective-permute-start.27 = (f32[160,128]{1,0:T(8,128)S(1)}, f32[160,128]{1,0:T(8,128)S(1)}, u32[]{:S(2)}, u32[]{:S(2)}) collective-permute-start(f32[160,128]{1,0:T(8,128)S(1)} %add.174), channel_id=1, source_target_pairs={{0,128},{1,129},{2,130},{3,131},{4,132},{5,133},{6,134},{7,135},{8... | collective-permute-start | bytes 245768 | tf_op jit(solution)/shard_map/ppermute | solution.py:46
  141.6 2.9 %collective-permute-start.31 = (f32[640,128]{1,0:T(8,128)S(1)}, f32[640,128]{1,0:T(8,128)S(1)}, u32[]{:S(2)}, u32[]{:S(2)}) collective-permute-start(f32[640,128]{1,0:T(8,128)S(1)} %pad_maximum_fusion.5.refs_0_), channel_id=1, source_target_pairs={{0,8},{1,9},{2,10},{3,11},{4,12},{5,13},{6,14},{7,15},{8,16},{9,17... | collective-permute-start | bytes 983048 | tf_op jit(solution)/shard_map/ppermute | solution.py:46
  148.4 11.1 %collective-permute-start.34 = (f32[640,128]{1,0:T(8,128)S(1)}, f32[640,128]{1,0:T(8,128)S(1)}, u32[]{:S(2)}, u32[]{:S(2)}) collective-permute-start(f32[640,128]{1,0:T(8,128)S(1)} %pad_maximum_fusion.5.refs_0_), channel_id=1, source_target_pairs={{0,1},{1,0},{2,3},{3,2},{4,5},{5,4},{6,7},{7,6},{8,9},{9,8},{10,11... | collective-permute-start | bytes 983048 | tf_op jit(solution)/shard_map/ppermute | solution.py:46
  159.5 3.0 %collective-permute-start.35 = (f32[640,128]{1,0:T(8,128)S(1)}, f32[640,128]{1,0:T(8,128)S(1)}, u32[]{:S(2)}, u32[]{:S(2)}) collective-permute-start(f32[640,128]{1,0:T(8,128)S(1)} %collective-permute-done.31.refs_1_), channel_id=1, source_target_pairs={{0,1},{1,0},{2,3},{3,2},{4,5},{5,4},{6,7},{7,6},{8,9},{9,8},{10,11... | collective-permute-start | bytes 983048 | tf_op jit(solution)/shard_map/ppermute | solution.py:46
  162.5 5.0 %collective-permute-start.36 = (f32[640,128]{1,0:T(8,128)S(1)}, f32[640,128]{1,0:T(8,128)S(1)}, u32[]{:S(2)}, u32[]{:S(2)}) collective-permute-start(f32[640,128]{1,0:T(8,128)S(1)} %collective-permute-done.32.refs_2_), channel_id=1, source_target_pairs={{0,1},{1,0},{2,3},{3,2},{4,5},{5,4},{6,7},{7,6},{8,9},{9,8},{10,11... | collective-permute-start | bytes 983048 | tf_op jit(solution)/shard_map/ppermute | solution.py:46
  170.9 13.9 %collective-permute-done.41.refs_9_ = f32[48,1024]{1,0:T(8,128)S(1)} collective-permute-done((f32[48,1024]{1,0:T(8,128)}, f32[48,1024]{1,0:T(8,128)S(1)}, u32[]{:S(2)}, u32[]{:S(2)}) %collective-permute-start.41) | collective-permute-done | bytes 196640 | tf_op jit(solution)/shard_map/ppermute | solution.py:46
  186.0 3.6 %shard_map.100 = (f32[4,48,256]{2,1,0:T(8,128)}, f32[6,256,256]{2,1,0:T(8,128)}, f32[4,256,256]{2,1,0:T(8,128)}) custom-call(f32[640,128]{1,0:T(8,128)} %copy-done.5, f32[640,128]{1,0:T(8,128)} %copy-done.12, f32[640,128]{1,0:T(8,128)} %copy-done.13, f32[640,128]{1,0:T(8,128)} %copy-done.14, f32[640,128]{1,0:T(8,128)} %copy-done.15, f32[640,128]{1,0:T(8,128)} %copy-done.16, ...), custom_call_target="tpu_custom_call" | custom-call | bytes 3014656 | tf_op jit(solution)/shard_map/pallas_call | solution.py:266
  (136 shorter events, 51.3 us)
Async XLA Ops:
  3.5 18.2 %collective-permute-start.2 = (f32[48,1024]{1,0:T(8,128)}, f32[48,1024]{1,0:T(8,128)S(1)}, u32[]{:S(2)}, u32[]{:S(2)}) collective-permute-start(f32[48,1024]{1,0:T(8,128)} %shard_map.94.own), channel_id=1, source_target_pairs={{0,4},{1,5},{2,6},{3,7},{4,0},{5,1},{6,2},{7,3},{8,12},{9,13},{10,... | collective-permute-start | bytes 589832 | tf_op jit(solution)/shard_map/ppermute | solution.py:46
  4.5 17.2 %collective-permute-start.3 = (f32[48,1024]{1,0:T(8,128)}, f32[48,1024]{1,0:T(8,128)S(1)}, u32[]{:S(2)}, u32[]{:S(2)}) collective-permute-start(f32[48,1024]{1,0:T(8,128)} %shard_map.94.own), channel_id=1, source_target_pairs={{0,6},{1,7},{2,0},{3,1},{4,2},{5,3},{6,4},{7,5},{8,14},{9,15},{10,... | collective-permute-start | bytes 589832 | tf_op jit(solution)/shard_map/ppermute | solution.py:46
  21.8 18.7 %collective-permute-start.6 = (f32[192,1024]{1,0:T(8,128)S(1)}, f32[192,1024]{1,0:T(8,128)S(1)}, u32[]{:S(2)}, u32[]{:S(2)}) collective-permute-start(f32[192,1024]{1,0:T(8,128)S(1)} %pad_maximum_fusion), channel_id=1, source_target_pairs={{0,1},{1,0},{2,3},{3,2},{4,5},{5,4},{6,7},{7,6},{8,9},{9,8},{10,11... | collective-permute-start | bytes 2359304 | tf_op jit(solution)/shard_map/ppermute | solution.py:46
  26.2 20.9 %collective-permute-start.4 = (f32[144,1024]{1,0:T(8,128)S(1)}, f32[144,1024]{1,0:T(8,128)S(1)}, u32[]{:S(2)}, u32[]{:S(2)}) collective-permute-start(f32[144,1024]{1,0:T(8,128)S(1)} %pad_maximum_fusion.1.rest), channel_id=1, source_target_pairs={{0,8},{1,9},{2,10},{3,11},{4,12},{5,13},{6,14},{7,15},{8,16},{9,17... | collective-permute-start | bytes 1769480 | tf_op jit(solution)/shard_map/ppermute | solution.py:46
  26.2 20.9 %collective-permute-start.5 = (f32[144,1024]{1,0:T(8,128)S(1)}, f32[144,1024]{1,0:T(8,128)S(1)}, u32[]{:S(2)}, u32[]{:S(2)}) collective-permute-start(f32[144,1024]{1,0:T(8,128)S(1)} %pad_maximum_fusion.1.rest), channel_id=1, source_target_pairs={{0,24},{1,25},{2,26},{3,27},{4,28},{5,29},{6,30},{7,31},{8,0},{9,1... | collective-permute-start | bytes 1769480 | tf_op jit(solution)/shard_map/ppermute | solution.py:46
  47.2 13.4 %collective-permute-start.13 = (f32[144,1024]{1,0:T(8,128)S(1)}, f32[144,1024]{1,0:T(8,128)S(1)}, u32[]{:S(2)}, u32[]{:S(2)}) collective-permute-start(f32[144,1024]{1,0:T(8,128)S(1)} %collective-permute-done.4.refs_1_), channel_id=1, source_target_pairs={{0,1},{1,0},{2,3},{3,2},{4,5},{5,4},{6,7},{7,6},{8,9},{9,8},{10,11... | collective-permute-start | bytes 1769480 | tf_op jit(solution)/shard_map/ppermute | solution.py:46
  50.6 10.0 %collective-permute-start.14 = (f32[144,1024]{1,0:T(8,128)S(1)}, f32[144,1024]{1,0:T(8,128)S(1)}, u32[]{:S(2)}, u32[]{:S(2)}) collective-permute-start(f32[144,1024]{1,0:T(8,128)S(1)} %collective-permute-done.5.refs_2_), channel_id=1, source_target_pairs={{0,1},{1,0},{2,3},{3,2},{4,5},{5,4},{6,7},{7,6},{8,9},{9,8},{10,11... | collective-permute-start | bytes 1769480 | tf_op jit(solution)/shard_map/ppermute | solution.py:46
  52.7 15.7 %collective-permute-start.10 = (f32[96,1024]{1,0:T(8,128)}, f32[96,1024]{1,0:T(8,128)}, u32[]{:S(2)}, u32[]{:S(2)}) collective-permute-start(f32[96,1024]{1,0:T(8,128)} %pad_maximum_fusion.4), channel_id=1, source_target_pairs={{0,8},{1,9},{2,10},{3,11},{4,12},{5,13},{6,14},{7,15},{8,16},{9,17... | collective-permute-start | bytes 1179656 | tf_op jit(solution)/shard_map/ppermute | solution.py:46
  52.7 15.7 %collective-permute-start.11 = (f32[96,1024]{1,0:T(8,128)}, f32[96,1024]{1,0:T(8,128)}, u32[]{:S(2)}, u32[]{:S(2)}) collective-permute-start(f32[96,1024]{1,0:T(8,128)} %slice.7), channel_id=1, source_target_pairs={{0,24},{1,25},{2,26},{3,27},{4,28},{5,29},{6,30},{7,31},{8,0},{9,1... | collective-permute-start | bytes 1179656 | tf_op jit(solution)/shard_map/ppermute | solution.py:46
  55.4 14.3 %collective-permute-start.15 = (f32[96,1024]{1,0:T(8,128)S(1)}, f32[96,1024]{1,0:T(8,128)S(1)}, u32[]{:S(2)}, u32[]{:S(2)}) collective-permute-start(f32[96,1024]{1,0:T(8,128)S(1)} %constant_dynamic-slice_fusion), channel_id=1, source_target_pairs={{0,128},{1,129},{2,130},{3,131},{4,132},{5,133},{6,134},{7,135},{8... | collective-permute-start | bytes 1179656 | tf_op jit(solution)/shard_map/ppermute | solution.py:46
  85.9 17.2 %collective-permute-start.19 = (f32[640,128]{1,0:T(8,128)S(1)}, f32[640,128]{1,0:T(8,128)S(1)}, u32[]{:S(2)}, u32[]{:S(2)}) collective-permute-start(f32[640,128]{1,0:T(8,128)S(1)} %get-tuple-element.54), channel_id=1, source_target_pairs={{0,8},{1,9},{2,10},{3,11},{4,12},{5,13},{6,14},{7,15},{8,16},{9,17... | collective-permute-start | bytes 983048 | tf_op jit(solution)/shard_map/ppermute | solution.py:46
  85.9 17.1 %collective-permute-start.20 = (f32[640,128]{1,0:T(8,128)S(1)}, f32[640,128]{1,0:T(8,128)S(1)}, u32[]{:S(2)}, u32[]{:S(2)}) collective-permute-start(f32[640,128]{1,0:T(8,128)S(1)} %get-tuple-element.53), channel_id=1, source_target_pairs={{0,16},{1,17},{2,18},{3,19},{4,20},{5,21},{6,22},{7,23},{8,24},{9,... | collective-permute-start | bytes 983048 | tf_op jit(solution)/shard_map/ppermute | solution.py:46
  87.3 16.1 %collective-permute-start.21 = (f32[640,128]{1,0:T(8,128)S(1)}, f32[640,128]{1,0:T(8,128)S(1)}, u32[]{:S(2)}, u32[]{:S(2)}) collective-permute-start(f32[640,128]{1,0:T(8,128)S(1)} %get-tuple-element.52), channel_id=1, source_target_pairs={{0,24},{1,25},{2,26},{3,27},{4,28},{5,29},{6,30},{7,31},{8,0},{9,1... | collective-permute-start | bytes 983048 | tf_op jit(solution)/shard_map/ppermute | solution.py:46
  125.6 21.4 %collective-permute-start.38 = (f32[2,48,1024]{2,1,0:T(8,128)S(1)}, f32[2,48,1024]{2,1,0:T(8,128)S(1)}, u32[]{:S(2)}, u32[]{:S(2)}) collective-permute-start(f32[2,48,1024]{2,1,0:T(8,128)S(1)} %copy-done.23), channel_id=1, source_target_pairs={{0,32},{1,33},{2,34},{3,35},{4,36},{5,37},{6,38},{7,39},{8,40},{9,... | collective-permute-start | bytes 1179656 | tf_op jit(solution)/shard_map/ppermute | solution.py:46
  138.3 10.1 %collective-permute-start.39 = (f32[2,48,1024]{2,1,0:T(8,128)S(1)}, f32[2,48,1024]{2,1,0:T(8,128)S(1)}, u32[]{:S(2)}, u32[]{:S(2)}) collective-permute-start(f32[2,48,1024]{2,1,0:T(8,128)S(1)} %copy-done.22), channel_id=1, source_target_pairs={{0,64},{1,65},{2,66},{3,67},{4,68},{5,69},{6,70},{7,71},{8,72},{9,... | collective-permute-start | bytes 1179656 | tf_op jit(solution)/shard_map/ppermute | solution.py:46
  141.6 17.9 %collective-permute-start.31 = (f32[640,128]{1,0:T(8,128)S(1)}, f32[640,128]{1,0:T(8,128)S(1)}, u32[]{:S(2)}, u32[]{:S(2)}) collective-permute-start(f32[640,128]{1,0:T(8,128)S(1)} %pad_maximum_fusion.5.refs_0_), channel_id=1, source_target_pairs={{0,8},{1,9},{2,10},{3,11},{4,12},{5,13},{6,14},{7,15},{8,16},{9,17... | collective-permute-start | bytes 983048 | tf_op jit(solution)/shard_map/ppermute | solution.py:46
  144.5 18.0 %collective-permute-start.32 = (f32[640,128]{1,0:T(8,128)S(1)}, f32[640,128]{1,0:T(8,128)S(1)}, u32[]{:S(2)}, u32[]{:S(2)}) collective-permute-start(f32[640,128]{1,0:T(8,128)S(1)} %pad_maximum_fusion.5.refs_0_), channel_id=1, source_target_pairs={{0,16},{1,17},{2,18},{3,19},{4,20},{5,21},{6,22},{7,23},{8,24},{9,... | collective-permute-start | bytes 983048 | tf_op jit(solution)/shard_map/ppermute | solution.py:46
  146.4 21.1 %collective-permute-start.33 = (f32[640,128]{1,0:T(8,128)S(1)}, f32[640,128]{1,0:T(8,128)S(1)}, u32[]{:S(2)}, u32[]{:S(2)}) collective-permute-start(f32[640,128]{1,0:T(8,128)S(1)} %pad_maximum_fusion.5.refs_0_), channel_id=1, source_target_pairs={{0,24},{1,25},{2,26},{3,27},{4,28},{5,29},{6,30},{7,31},{8,0},{9,1... | collective-permute-start | bytes 983048 | tf_op jit(solution)/shard_map/ppermute | solution.py:46
  147.0 20.6 %collective-permute-start.40 = (f32[2,48,1024]{2,1,0:T(8,128)S(1)}, f32[2,48,1024]{2,1,0:T(8,128)S(1)}, u32[]{:S(2)}, u32[]{:S(2)}) collective-permute-start(f32[2,48,1024]{2,1,0:T(8,128)S(1)} %copy-done.21), channel_id=1, source_target_pairs={{0,96},{1,97},{2,98},{3,99},{4,100},{5,101},{6,102},{7,103},{8,104... | collective-permute-start | bytes 1179656 | tf_op jit(solution)/shard_map/ppermute | solution.py:46
  148.4 36.5 %collective-permute-start.34 = (f32[640,128]{1,0:T(8,128)S(1)}, f32[640,128]{1,0:T(8,128)S(1)}, u32[]{:S(2)}, u32[]{:S(2)}) collective-permute-start(f32[640,128]{1,0:T(8,128)S(1)} %pad_maximum_fusion.5.refs_0_), channel_id=1, source_target_pairs={{0,1},{1,0},{2,3},{3,2},{4,5},{5,4},{6,7},{7,6},{8,9},{9,8},{10,11... | collective-permute-start | bytes 983048 | tf_op jit(solution)/shard_map/ppermute | solution.py:46
  159.5 25.4 %collective-permute-start.35 = (f32[640,128]{1,0:T(8,128)S(1)}, f32[640,128]{1,0:T(8,128)S(1)}, u32[]{:S(2)}, u32[]{:S(2)}) collective-permute-start(f32[640,128]{1,0:T(8,128)S(1)} %collective-permute-done.31.refs_1_), channel_id=1, source_target_pairs={{0,1},{1,0},{2,3},{3,2},{4,5},{5,4},{6,7},{7,6},{8,9},{9,8},{10,11... | collective-permute-start | bytes 983048 | tf_op jit(solution)/shard_map/ppermute | solution.py:46
  162.5 22.4 %collective-permute-start.36 = (f32[640,128]{1,0:T(8,128)S(1)}, f32[640,128]{1,0:T(8,128)S(1)}, u32[]{:S(2)}, u32[]{:S(2)}) collective-permute-start(f32[640,128]{1,0:T(8,128)S(1)} %collective-permute-done.32.refs_2_), channel_id=1, source_target_pairs={{0,1},{1,0},{2,3},{3,2},{4,5},{5,4},{6,7},{7,6},{8,9},{9,8},{10,11... | collective-permute-start | bytes 983048 | tf_op jit(solution)/shard_map/ppermute | solution.py:46
  167.4 17.5 %collective-permute-start.37 = (f32[640,128]{1,0:T(8,128)S(1)}, f32[640,128]{1,0:T(8,128)S(1)}, u32[]{:S(2)}, u32[]{:S(2)}) collective-permute-start(f32[640,128]{1,0:T(8,128)S(1)} %collective-permute-done.33.refs_3_), channel_id=1, source_target_pairs={{0,1},{1,0},{2,3},{3,2},{4,5},{5,4},{6,7},{7,6},{8,9},{9,8},{10,11... | collective-permute-start | bytes 983048 | tf_op jit(solution)/shard_map/ppermute | solution.py:46
  170.5 14.4 %collective-permute-start.41 = (f32[48,1024]{1,0:T(8,128)}, f32[48,1024]{1,0:T(8,128)S(1)}, u32[]{:S(2)}, u32[]{:S(2)}) collective-permute-start(f32[48,1024]{1,0:T(8,128)} %get-tuple-element.50), channel_id=1, source_target_pairs={{0,128},{1,129},{2,130},{3,131},{4,132},{5,133},{6,134},{7,135},{8... | collective-permute-start | bytes 589832 | tf_op jit(solution)/shard_map/ppermute | solution.py:46
  (45 other events, 451.7 us)
